TPU v7x, 256 devices: a whole 4x4x8 slice. The times are simulated.
256 devices in a mesh: grp: 8 (over y, core), dev: 32 (over z, x).
Axes of the slice: x: 4, y: 4, z: 8, core: 2. Of those that a mesh axis runs over, the one named last changes fastest.
Arguments:
- u_blocks: float32 [6144, 32, 1024], P(('grp', 'dev')), may hold values from -20 to 20
- v_blocks: float32 [6144, 32, 1024], P(('grp', 'dev')), may hold values from -0.1875 to 0.1875
- sketch: float32 [512, 32, 1024], P(('grp', 'dev')), may hold values from -6 to 6
- near_diag: float32 [512, 1024], P(('grp', 'dev')), may hold values from 0.3 to 72
- block_row: int32 [6144], P(('grp', 'dev')), may hold values from 0 to 63, as said below
- col_count: int32 [512], P(('grp', 'dev')), may hold values from 8 to 12, as said below
Outputs:
- leaf_basis: float32 [512, 32, 1024], P(('grp', 'dev'))
- transfer_leaf: float32 [512, 32, 32], P(('grp', 'dev'))
- transfer_group: float32 [8, 32, 32], P('grp')
Inputs may be any that keep to these rules, and one draw needn't show every extreme that they name: A device's slots hold its blocks in the order of its column clusters, col_count[c] of them for cluster c; the remaining slots are empty. The row cluster block_row[s] belongs to device block_row[s] // 2 of the same subtree. Among the live slots of one device at most 3 have row clusters of any one device, and in every subtree some device is named by exactly 3 live slots of every device of that subtree.
All inputs are finite; a program needn't handle non-finite values.
Results may differ from a plain program's by a relative error of at most 0.0003.
Values sent between devices are 32-bit elements; how exact they have to be, the bound alone decides.
No kernel may reach another device: no remote copies, remote signals or barrier semaphores. Data moves between devices by JAX's collectives and lax.ppermute only.
A program may use at most 128 MiB of HBM per device.

v0:
```python
import math

import jax
import jax.numpy as jnp
from jax import lax
from jax.sharding import PartitionSpec as P

CMAX = 12


def lower_solve(lower_factor, right_side):
    return lax.linalg.triangular_solve(lower_factor, right_side, left_side=True, lower=True)


def body(u_blocks, v_blocks, sketch, near_diag, block_row, col_count):
    highest = lax.Precision.HIGHEST
    blocks, factor_rank, leaf_rows = u_blocks.shape
    local_count = sketch.shape[0]
    members = lax.axis_size("dev")
    groups = lax.axis_size("grp")
    group_count = members * local_count
    capacity = max(3, (local_count * CMAX + members - 1) // members)
    slot_index = jnp.arange(blocks, dtype=jnp.int32)
    slot_ends = jnp.cumsum(col_count)
    live_slot = slot_index < slot_ends[-1]
    col_local = jnp.minimum(
        jnp.sum((slot_ends[None, :] <= slot_index[:, None]).astype(jnp.int32), axis=1),
        local_count - 1,
    )
    picked = jnp.take(sketch, col_local, axis=0)
    coupling = jnp.einsum(
        "bkl,bml->bkm", v_blocks, picked, precision=highest, preferred_element_type=jnp.float32
    )
    coupling = jnp.where(live_slot[:, None, None], coupling, 0.0)
    target_dev = block_row // local_count
    target_local = block_row % local_count
    earlier = (
        (target_dev[None, :] == target_dev[:, None])
        & live_slot[None, :]
        & (slot_index[None, :] < slot_index[:, None])
    )
    order_rank = jnp.sum(earlier.astype(jnp.int32), axis=1)
    position = jnp.where(live_slot, target_dev * capacity + order_rank, -1)
    buffer_ids = jnp.arange(members * capacity, dtype=jnp.int32)
    matches = position[None, :] == buffer_ids[:, None]
    filled = jnp.any(matches, axis=1)
    source = jnp.sum(jnp.where(matches, slot_index[None, :], 0), axis=1)
    local_hit = target_local[:, None] == jnp.arange(local_count, dtype=jnp.int32)[None, :]
    placed = jnp.where(local_hit[:, :, None, None], coupling[:, None, :, :], 0.0).reshape(
        blocks, -1
    )
    send_factor = jnp.where(filled[:, None, None], jnp.take(u_blocks, source, axis=0), 0.0)
    send_coupling = jnp.where(filled[:, None], jnp.take(placed, source, axis=0), 0.0)
    got_factor, got_coupling = (
        lax.all_to_all(send_factor, "dev", split_axis=0, concat_axis=0, tiled=True),
        lax.all_to_all(send_coupling, "dev", split_axis=0, concat_axis=0, tiled=True),
    )
    got_coupling = got_coupling.reshape(-1, local_count, factor_rank, factor_rank)
    far_sample = jnp.einsum(
        "pkam,pal->kml",
        got_coupling,
        got_factor,
        precision=highest,
        preferred_element_type=jnp.float32,
    )
    sample = far_sample + near_diag[:, None, :] * sketch
    leaf_gram = jnp.einsum(
        "kml,knl->kmn", sample, sample, precision=highest, preferred_element_type=jnp.float32
    )
    leaf_lower = jnp.linalg.cholesky(leaf_gram)
    leaf_basis = lower_solve(leaf_lower, sample) * math.sqrt(leaf_rows)
    leaf_factor = jnp.swapaxes(leaf_lower, 1, 2)
    every_factor = lax.all_gather(leaf_factor, "dev", axis=0, tiled=True)
    group_gram = jnp.einsum(
        "cab,cad->bd",
        every_factor,
        every_factor,
        precision=highest,
        preferred_element_type=jnp.float32,
    )
    group_lower = jnp.linalg.cholesky(group_gram)
    group_factor = jnp.transpose(group_lower)
    leaf_transposed = lower_solve(jnp.broadcast_to(group_lower, leaf_lower.shape), leaf_lower)
    transfer_leaf = jnp.swapaxes(leaf_transposed, 1, 2) * math.sqrt(group_count)
    every_group = lax.all_gather(group_factor[None], "grp", axis=0, tiled=True)
    root_gram = jnp.einsum(
        "cab,cad->bd",
        every_group,
        every_group,
        precision=highest,
        preferred_element_type=jnp.float32,
    )
    root_lower = jnp.linalg.cholesky(root_gram)
    group_transposed = lower_solve(root_lower, group_lower)
    transfer_group = jnp.transpose(group_transposed) * math.sqrt(groups)
    return (leaf_basis, transfer_leaf, transfer_group[None])


def solution(mesh):
    in_specs = (
        P(("grp", "dev"), None, None),
        P(("grp", "dev"), None, None),
        P(("grp", "dev"), None, None),
        P(("grp", "dev"), None),
        P(("grp", "dev")),
        P(("grp", "dev")),
    )
    out_specs = (P(("grp", "dev"), None, None), P(("grp", "dev"), None, None), P("grp", None, None))
    return jax.shard_map(body, mesh=mesh, in_specs=in_specs, out_specs=out_specs, check_vma=False)
```

profile of v0, /device:TPU:1, one launch (start us, length us, event | category | flops | bytes accessed | tf_op | source)
XLA Modules:
  0.0 479.8 jit_solution(11583333941677051870)
XLA Ops:
  6.9 3.4 gather_fusion
  10.2 5.9 %fusion.9 = f32[24,32,32]{1,2,0:T(8,128)S(1)} fusion(f32[24,32,1024]{2,1,0:T(8,128)} %param.8, f32[24,32,1024]{2,1,0:T(8,128)} %gather_fusion, pred[24]{0:T(512)(128)(4,1)} %get-tuple-element.8, pred[24]{0:T(512)(128)(4,1)} %copy-done.5), kind=kOutput, calls=%fused_computation.11 | convolution fusion | flops 302800896 | bytes 6389808 | tf_op jit(solution)/shard_map/bkl,bml->bkm/dot_general | solution.py:31
  17.8 2.0 broadcast_select_fusion
  19.8 1.5 select_n.111
  21.3 1.8 gather_fusion.1
  23.1 2.4 gather.16
  25.7 2.7 select_select_fusion.1
  28.4 12.0 %all-to-all-start = ((f32[32,3,2048]{2,1,0:T(4,128)}), f32[32,3,2048]{2,1,0:T(4,128)}, u32[]{:S(2)}, u32[]{:S(2)}) async-start(f32[32,3,2048]{2,1,0:T(4,128)} %select_select_fusion.1), calls=%async_computation | async-start | bytes 2097152 | tf_op jit(solution)/shard_map/all_to_all | solution.py:56
  40.4 6.0 %gather_fusion.2 = f32[96,32,1024]{2,1,0:T(8,128)} fusion(f32[24,32,1024]{2,1,0:T(8,128)S(1)} %copy-done, s32[1024]{0:T(1024)} %pad_clamp_fusion), kind=kCustom, calls=%fused_computation.2 | custom fusion | bytes 25166208 | tf_op jit(solution)/shard_map/jit(_take)/gather | solution.py:52
  46.3 12.3 %select_select_fusion = f32[96,32,1024]{2,1,0:T(8,128)} fusion(f32[96,32,1024]{2,1,0:T(8,128)} %gather_fusion.2, pred[96]{0:T(512)(128)(4,1)S(1)} %compare_and_fusion.1, pred[96]{0:T(512)(128)(4,1)S(1)} %copy-done.6), kind=kLoop, calls=%fused_computation.5 | loop fusion | flops 6291456 | bytes 25166016 | tf_op jit(solution)/shard_map/jit(_where)/select_n | solution.py:52
  58.7 7.9 %all-to-all-done = f32[32,3,2048]{2,1,0:T(4,128)} async-done(((f32[32,3,2048]{2,1,0:T(4,128)}), f32[32,3,2048]{2,1,0:T(4,128)}, u32[]{:S(2)}, u32[]{:S(2)}) %all-to-all-start) | async-done | bytes 786464 | tf_op jit(solution)/shard_map/all_to_all | solution.py:56
  66.5 6.7 %all-to-all-start.1 = ((f32[96,32,1024]{2,1,0:T(8,128)}), f32[96,32,1024]{2,1,0:T(8,128)}, u32[]{:S(2)}, u32[]{:S(2)}) async-start(f32[96,32,1024]{2,1,0:T(8,128)} %select_select_fusion), calls=%async_computation.1 | async-start | bytes 25165824 | tf_op jit(solution)/shard_map/all_to_all | solution.py:55
  73.3 3.8 reshape.139
  77.0 279.9 %all-to-all-done.1 = f32[96,32,1024]{2,1,0:T(8,128)} async-done(((f32[96,32,1024]{2,1,0:T(8,128)}), f32[96,32,1024]{2,1,0:T(8,128)}, u32[]{:S(2)}, u32[]{:S(2)}) %all-to-all-start.1) | async-done | bytes 12582944 | tf_op jit(solution)/shard_map/all_to_all | solution.py:55
  357.0 15.2 %fusion.15 = f32[2,32,1024]{2,1,0:T(8,128)S(1)} fusion(f32[96,2,32,32]{3,2,1,0:T(8,128)} %reshape.139, f32[96,32,1024]{2,1,0:T(8,128)} %all-to-all-done.1, f32[2,32,1024]{2,1,0:T(8,128)S(1)} %copy-done.1, f32[2,1024]{1,0:T(2,128)S(1)} %copy-done.4), kind=kOutput, calls=%fused_computation.14 | convolution fusion | flops 2416050176 | bytes 13901824 | tf_op jit(solution)/shard_map/pkam,pal->kml/dot_general | solution.py:59
  373.3 5.9 %custom-call.15 = f32[2,32,32]{2,1,0:T(8,128)S(1)} custom-call(f32[2,32,32]{2,1,0:T(8,128)S(1)} %fusion.21), custom_call_target="Cholesky" | custom-call | tf_op jit(solution)/shard_map/jit(cholesky)/cholesky | solution.py:70
  379.5 47.4 %all_gather.6 = f32[64,32,32]{2,1,0:T(8,128)S(1)} all-gather(f32[2,32,32]{2,1,0:T(8,128)S(1)} %copy.51), channel_id=1, replica_groups=mesh['grp'=8,'dev'=32] {'dev'}, dimensions={0}, use_global_device_ids=true | all-gather | bytes 270336 | tf_op jit(solution)/shard_map/all_gather | solution.py:73
  426.9 1.8 convolution_bitcast_fusion.1
  428.8 2.9 cholesky.83
  433.8 26.1 %all-gather = f32[256,32]{1,0:T(8,128)S(1)} all-gather(f32[32,32]{1,0:T(8,128)S(1)} %copy.56), channel_id=2, replica_groups=mesh['grp'=8,'dev'=32] {'grp'}, dimensions={0}, use_global_device_ids=true | all-gather | bytes 36864 | tf_op jit(solution)/shard_map/all_gather | solution.py:85
  460.4 2.9 cholesky.94
  464.6 2.4 custom-call.18
  467.9 4.9 %custom-call.17 = f32[2,1,32,32]{2,3,1,0:T(8,128)S(1)} custom-call(f32[2,1,32,32]{3,2,1,0:T(8,128)S(1)} %broadcast_select_fusion.1), custom_call_target="InvertDiagBlocksLowerTriangular" | custom-call | tf_op jit(solution)/shard_map/triangular_solve | solution.py:12
  473.8 4.9 %custom-call.16 = f32[2,1,32,32]{2,3,1,0:T(8,128)S(1)} custom-call(f32[2,1,32,32]{3,2,1,0:T(8,128)S(1)} %get-tuple-element.5), custom_call_target="InvertDiagBlocksLowerTriangular" | custom-call | tf_op jit(solution)/shard_map/triangular_solve | solution.py:12
  (63 shorter events, 16.2 us)
Async XLA Ops:
  0.6 39.7 %copy-start = (f32[24,32,1024]{2,1,0:T(8,128)S(1)}, f32[24,32,1024]{2,1,0:T(8,128)}, u32[]{:S(2)}) copy-start(f32[24,32,1024]{2,1,0:T(8,128)} %param.7) | copy-start | bytes 9437188
  3.5 2.1 copy-start.5
  5.6 0.7 copy-start.7
  21.3 4.3 copy-start.6
  28.4 38.2 %all-to-all-start = ((f32[32,3,2048]{2,1,0:T(4,128)}), f32[32,3,2048]{2,1,0:T(4,128)}, u32[]{:S(2)}, u32[]{:S(2)}) async-start(f32[32,3,2048]{2,1,0:T(4,128)} %select_select_fusion.1), calls=%async_computation | async-start | bytes 2097152 | tf_op jit(solution)/shard_map/all_to_all | solution.py:56
  40.4 6.0 %copy-start.8 = (s32[96]{0:T(128)S(1)}, s32[96]{0:T(128)}, u32[]{:S(2)}) copy-start(s32[96]{0:T(128)} %copy-done.7) | copy-start | bytes 1156
  66.5 290.4 %all-to-all-start.1 = ((f32[96,32,1024]{2,1,0:T(8,128)}), f32[96,32,1024]{2,1,0:T(8,128)}, u32[]{:S(2)}, u32[]{:S(2)}) async-start(f32[96,32,1024]{2,1,0:T(8,128)} %select_select_fusion), calls=%async_computation.1 | async-start | bytes 25165824 | tf_op jit(solution)/shard_map/all_to_all | solution.py:55
  73.2 283.8 %copy-start.1 = (f32[2,32,1024]{2,1,0:T(8,128)S(1)}, f32[2,32,1024]{2,1,0:T(8,128)}, u32[]{:S(2)}) copy-start(f32[2,32,1024]{2,1,0:T(8,128)} %param.9) | copy-start | bytes 786436
  73.2 283.8 %copy-start.4 = (f32[2,1024]{1,0:T(2,128)S(1)}, f32[2,1024]{1,0:T(2,128)}, u32[]{:S(2)}) copy-start(f32[2,1024]{1,0:T(2,128)} %param.10) | copy-start | bytes 24580
  372.2 0.7 copy-start.2
  373.2 105.5 %copy-start.3 = (f32[2,32,1024]{2,1,0:T(8,128)S(1)}, f32[2,32,1024]{2,1,0:T(8,128)}, u32[]{:S(2)}) copy-start(f32[2,32,1024]{2,1,0:T(8,128)} %copy-done.2) | copy-start | bytes 786436
where the time goes:
time: 481 us; the launch traced here: 480 us
  waiting for transfers between devices  288 us (60%)
  blocking collectives  73.5 us (15%)
  other arithmetic  50.8 us (11%)
  matrix products  26.6 us (6%)
  local copies, waits for them, and re-layouts  21.7 us (5%)
  starting transfers between devices  18.6 us (4%)
    all_to_all x1, waiting for transfers between devices, body(): lax.all_to_all(send_factor, 'dev', split_axis=0, concat_axis=0, tiled=True)  280 us
    all_gather x1, blocking collectives, body(): every_factor = lax.all_gather(leaf_factor, 'dev', axis=0, tiled=True)  47.4 us
    all_gather x1, blocking collectives, body(): every_group = lax.all_gather(group_factor[None], 'grp', axis=0, tiled=True)  26.1 us
    dot_general x1, matrix products, body(): jnp.einsum('pkam,pal->kml', got_coupling, got_factor, precision=highest,...  15.2 us
    another operation x6, other arithmetic, lower_solve(): lax.linalg.triangular_solve(lower_factor, right_side, left_side=True, low...  12.9 us
    select_n x1, other arithmetic, body(): jnp.where(filled[:, None, None], jnp.take(u_blocks, source, axis=0), 0.0)  12.3 us
    all_to_all x1, starting transfers between devices, body(): lax.all_to_all(send_coupling, 'dev', split_axis=0, concat_axis=0, tiled=T...  12 us
  transfers between devices with their start and end apart: 2, of which 2 were waited for; matrix products, arithmetic and copies ran while one was open for 5% of the time, Pallas kernels for 0%

commit v1 on v0

v1 whole, which is shorter than its diff:
```python
import functools
import math

import jax
import jax.numpy as jnp
from jax import lax
from jax.experimental import pallas as pl
from jax.experimental.pallas import tpu as pltpu
from jax.sharding import PartitionSpec as P

NZ, NX = 8, 4
R = 32
LEAF = 1024
SPLIT = 512
SLOTS_STEP = 4
HIGHEST = lax.Precision.HIGHEST


def halves(value):
    high = value.astype(jnp.bfloat16)
    low = (value - high.astype(jnp.float32)).astype(jnp.bfloat16)
    return high, low


def contribution_kernel(rows_ref, count_ref, place_ref, u_ref, v_ref, sketch_ref, xfirst_ref, zfirst_ref):
    step = pl.program_id(0)

    @pl.when(step == 0)
    def _():
        xfirst_ref[...] = jnp.zeros_like(xfirst_ref)
        zfirst_ref[...] = jnp.zeros_like(zfirst_ref)

    first_count = count_ref[0]
    live_count = first_count + count_ref[1]
    sketch_high, sketch_low = halves(sketch_ref[...].reshape(2 * R, LEAF))
    v_high, v_low = halves(v_ref[...].reshape(SLOTS_STEP * R, LEAF))
    contract = (((1,), (1,)), ((), ()))
    both = jnp.concatenate([sketch_high, sketch_low], axis=0)
    wide = lax.dot_general(v_high, both, contract, preferred_element_type=jnp.float32)
    couplings = (
        wide[:, : 2 * R]
        + wide[:, 2 * R :]
        + lax.dot_general(v_low, sketch_high, contract, preferred_element_type=jnp.float32)
    )
    for t in range(SLOTS_STEP):
        slot = step * SLOTS_STEP + t

        @pl.when(slot < live_count)
        def _():
            row = rows_ref[slot]
            device = row // 2
            cluster = row % 2
            dz = (device // NX - place_ref[0] + NZ) % NZ
            dx = (device % NX - place_ref[1] + NX) % NX
            part = couplings[t * R : (t + 1) * R]
            coupling = jnp.where(slot < first_count, part[:, :R], part[:, R:])
            c_high, c_low = halves(coupling)
            u_high, u_low = halves(u_ref[t])
            left = jnp.concatenate([c_high, c_low, c_high], axis=0)
            right = jnp.concatenate([u_high, u_high, u_low], axis=0)
            value = lax.dot_general(
                left, right, (((0,), (0,)), ((), ())), preferred_element_type=jnp.float32
            )
            xfirst_ref[dx, cluster, dz] += value[:, :SPLIT]
            zfirst_ref[dz, cluster, dx] += value[:, SPLIT:]


def contributions(block_row, col_count, place, u_blocks, v_blocks, sketch):
    slots = u_blocks.shape[0]
    xshape = (NX, 2, NZ, R, SPLIT)
    zshape = (NZ, 2, NX, R, LEAF - SPLIT)
    block = lambda i, *_: (i, 0, 0)
    whole = lambda i, *_: (0, 0, 0, 0, 0)
    return pl.pallas_call(
        contribution_kernel,
        out_shape=(
            jax.ShapeDtypeStruct(xshape, jnp.float32),
            jax.ShapeDtypeStruct(zshape, jnp.float32),
        ),
        grid_spec=pltpu.PrefetchScalarGridSpec(
            num_scalar_prefetch=3,
            grid=(slots // SLOTS_STEP,),
            in_specs=[
                pl.BlockSpec((SLOTS_STEP, R, LEAF), block),
                pl.BlockSpec((SLOTS_STEP, R, LEAF), block),
                pl.BlockSpec((2, R, LEAF), lambda i, *_: (0, 0, 0)),
            ],
            out_specs=(pl.BlockSpec(xshape, whole), pl.BlockSpec(zshape, whole)),
        ),
        compiler_params=pltpu.CompilerParams(vmem_limit_bytes=40 << 20),
        cost_estimate=pl.CostEstimate(flops=10**9, bytes_accessed=16 << 20, transcendentals=0),
        name="contributions",
    )(block_row, col_count, place, u_blocks, v_blocks, sketch)


def shift(value, dz, dx):
    pairs = [
        (z * NX + x, (z + dz) % NZ * NX + (x + dx) % NX) for z in range(NZ) for x in range(NX)
    ]
    return lax.ppermute(value, "dev", pairs)


def ring_sum(chunks, plus, minus):
    count = len(chunks)
    middle = count // 2
    forward = plus(chunks[middle][:1])
    backward = minus(chunks[middle][1:])
    for r in range(middle - 1, 0, -1):
        ahead, behind = chunks[r], chunks[count - r]
        if r == middle - 1:
            forward = jnp.concatenate([ahead[:1] + forward, ahead[1:]], axis=0)
            backward = jnp.concatenate([behind[:1], behind[1:] + backward], axis=0)
        else:
            forward = ahead + forward
            backward = behind + backward
        forward = plus(forward)
        backward = minus(backward)
    return chunks[0], forward, backward


def pack(gram):
    return jnp.concatenate([gram[8 * i : 8 * i + 8] for i in range(4)], axis=1)


def unpack(packed):
    return jnp.concatenate([packed[:, R * i : R * i + R] for i in range(4)], axis=0)


def eliminate(grams):
    count = len(grams)
    eye = (
        lax.broadcasted_iota(jnp.int32, (R, R), 0) == lax.broadcasted_iota(jnp.int32, (R, R), 1)
    ).astype(jnp.float32)
    work = [jnp.concatenate([gram, eye], axis=1) for gram in grams]
    sublane = lax.broadcasted_iota(jnp.int32, (R, 2 * R), 0)
    done = [jnp.zeros((R, 2 * R), jnp.float32) for _ in grams]
    for j in range(R):
        for i in range(count):
            column = jnp.broadcast_to(work[i][:, j : j + 1], (R, 2 * R))
            pivot = column[j : j + 1]
            scale = lax.rsqrt(pivot)
            scale = scale * (1.5 - 0.5 * pivot * scale * scale)
            row = jnp.broadcast_to(work[i][j : j + 1] * scale, (R, 2 * R))
            done[i] = jnp.where(sublane == j, row, done[i])
            work[i] = work[i] - (column * jnp.broadcast_to(scale, (R, 2 * R))) * row
    return [(d[:, :R], d[:, R:]) for d in done]


def sample_kernel(xo_ref, xf_ref, xb_ref, zo_ref, zf_ref, zb_ref, diag_ref, sketch_ref, sample_ref, gram_ref, packed_ref):
    total = jnp.zeros((R, R), jnp.float32)
    for i in range(2):
        far = jnp.concatenate(
            [xo_ref[i] + xf_ref[i] + xb_ref[i], zo_ref[i] + zf_ref[i] + zb_ref[i]], axis=1
        )
        sample = far + diag_ref[i : i + 1] * sketch_ref[i]
        sample_ref[i] = sample
        gram = lax.dot_general(
            sample,
            sample,
            (((1,), (1,)), ((), ())),
            precision=HIGHEST,
            preferred_element_type=jnp.float32,
        )
        gram_ref[i] = gram
        total = total + gram
    packed_ref[...] = jnp.broadcast_to(pack(total)[None], packed_ref.shape)


def leaf_kernel(gram_ref, sample_ref, basis_ref, upper_ref):
    factors = eliminate([gram_ref[0], gram_ref[1]])
    for i, (upper, inverse) in enumerate(factors):
        rows = lax.broadcasted_iota(jnp.int32, (R, R), 0)
        cols = lax.broadcasted_iota(jnp.int32, (R, R), 1)
        upper_ref[i] = jnp.where(rows <= cols, upper, 0.0)
        basis_ref[i] = jnp.dot(
            inverse * math.sqrt(LEAF),
            sample_ref[i],
            precision=HIGHEST,
            preferred_element_type=jnp.float32,
        )


def group_kernel(every_ref, packed_ref):
    packed_ref[...] = jnp.broadcast_to(jnp.sum(every_ref[...], axis=0)[None], packed_ref.shape)


def transfer_kernel(leaves, own_ref, every_ref, upper_ref, leaf_ref, group_ref):
    groups = every_ref.shape[0]
    group_gram = unpack(own_ref[0])
    root_gram = unpack(jnp.sum(every_ref[...], axis=0))
    (group_upper, group_inverse), (_, root_inverse) = eliminate([group_gram, root_gram])
    rows = lax.broadcasted_iota(jnp.int32, (R, R), 0)
    cols = lax.broadcasted_iota(jnp.int32, (R, R), 1)
    group_upper = jnp.where(rows <= cols, group_upper, 0.0)
    contract = (((1,), (1,)), ((), ()))
    for i in range(2):
        leaf_ref[i] = lax.dot_general(
            upper_ref[i],
            group_inverse * math.sqrt(leaves),
            contract,
            precision=HIGHEST,
            preferred_element_type=jnp.float32,
        )
    group_ref[0] = lax.dot_general(
        group_upper,
        root_inverse * math.sqrt(groups),
        contract,
        precision=HIGHEST,
        preferred_element_type=jnp.float32,
    )


def body(u_blocks, v_blocks, sketch, near_diag, block_row, col_count):
    members = lax.axis_size("dev")
    groups = lax.axis_size("grp")
    me = lax.axis_index("dev")
    place = jnp.stack([me // NX, me % NX]).astype(jnp.int32)
    xfirst, zfirst = contributions(block_row, col_count, place, u_blocks, v_blocks, sketch)
    along = {
        "x": (lambda a: shift(a, 0, 1), lambda a: shift(a, 0, -1)),
        "z": (lambda a: shift(a, 1, 0), lambda a: shift(a, -1, 0)),
    }
    own, ahead, behind = ring_sum([xfirst[i] for i in range(NX)], *along["x"])
    part = own + ahead + behind
    xterms = ring_sum([part[:, i] for i in range(NZ)], *along["z"])
    own, ahead, behind = ring_sum([zfirst[i] for i in range(NZ)], *along["z"])
    part = own + ahead + behind
    zterms = ring_sum([part[:, i] for i in range(NX)], *along["x"])
    sample, gram, packed = pl.pallas_call(
        sample_kernel,
        out_shape=(
            jax.ShapeDtypeStruct((2, R, LEAF), jnp.float32),
            jax.ShapeDtypeStruct((2, R, R), jnp.float32),
            jax.ShapeDtypeStruct((members, 8, 128), jnp.float32),
        ),
        name="sample",
    )(*xterms, *zterms, near_diag, sketch)
    every = lax.all_to_all(packed, "dev", split_axis=0, concat_axis=0, tiled=True)
    leaf_basis, upper = pl.pallas_call(
        leaf_kernel,
        out_shape=(
            jax.ShapeDtypeStruct((2, R, LEAF), jnp.float32),
            jax.ShapeDtypeStruct((2, R, R), jnp.float32),
        ),
        name="leaf",
    )(gram, sample)
    own_gram = pl.pallas_call(
        group_kernel,
        out_shape=jax.ShapeDtypeStruct((groups, 8, 128), jnp.float32),
        name="group",
    )(every)
    every_group = lax.all_to_all(own_gram, "grp", split_axis=0, concat_axis=0, tiled=True)
    transfer_leaf, transfer_group = pl.pallas_call(
        functools.partial(transfer_kernel, 2 * members),
        out_shape=(
            jax.ShapeDtypeStruct((2, R, R), jnp.float32),
            jax.ShapeDtypeStruct((1, R, R), jnp.float32),
        ),
        name="transfer",
    )(own_gram, every_group, upper)
    return (leaf_basis, transfer_leaf, transfer_group)


def solution(mesh):
    in_specs = (
        P(("grp", "dev"), None, None),
        P(("grp", "dev"), None, None),
        P(("grp", "dev"), None, None),
        P(("grp", "dev"), None),
        P(("grp", "dev")),
        P(("grp", "dev")),
    )
    out_specs = (P(("grp", "dev"), None, None), P(("grp", "dev"), None, None), P("grp", None, None))
    return jax.shard_map(body, mesh=mesh, in_specs=in_specs, out_specs=out_specs, check_vma=False)
```

time: 481 us -> 151 us (0.31)
  waiting for transfers between devices: 288 us -> 47.9 us
  blocking collectives: 73.5 us -> 18.1 us
  other arithmetic: 50.8 us -> 1.74 us
  starting transfers between devices: 18.6 us -> 48.1 us
  matrix products: 26.6 us -> 0 us
  Pallas kernels: 0 us -> 23.9 us
  local copies, waits for them, and re-layouts: 21.7 us -> 11 us
    all_to_all x2 -> x1, waiting for transfers between devices: 288 us -> 0.01 us  [body(): lax.all_to_all(own_gram, 'grp', split_axis=0, concat_axis=0, tiled=True)]
    all_gather x2 -> x0, blocking collectives: 73.5 us -> none  [the longest x1 47.4 us: body(): every_factor = lax.all_gather(leaf_factor, 'dev', axis=0, tiled=True)]
    ppermute x0 -> x24, waiting for transfers between devices: none -> 47.9 us  [shift(): return lax.ppermute(value, 'dev', pairs)]
    ppermute x0 -> x24, starting transfers between devices: none -> 32.3 us  [shift(): return lax.ppermute(value, 'dev', pairs)]
    another operation x17 -> x1, other arithmetic: 27.1 us -> 0.08 us  [body(): place = jnp.stack([me // NX, me % NX]).astype(jnp.int32)]
    pallas_call x0 -> x5, Pallas kernels: none -> 23.9 us  [the longest x1 10.3 us: contributions(): pl.pallas_call(contribution_kernel, out_shape=(jax.ShapeDtypeStruct(xshap...]
    dot_general x5 -> x0, matrix products: 23.6 us -> none  [the longest x1 15.2 us: body(): jnp.einsum('pkam,pal->kml', got_coupling, got_factor, precision=highest,...]
    select_n x8 -> x0, other arithmetic: 19.5 us -> none  [the longest x1 12.3 us: body(): jnp.where(filled[:, None, None], jnp.take(u_blocks, source, axis=0), 0.0)]
  transfers between devices with their start and end apart: 2 -> 25, of which waited for: 2 -> 13; matrix products, arithmetic and copies ran while one was open for 5% -> 2% of each run, Pallas kernels for 0% -> 3%
where the time goes in v1:
time: 151 us; the launch traced here: 152 us
  starting transfers between devices  48.1 us (32%)
  waiting for transfers between devices  47.9 us (32%)
  Pallas kernels  23.9 us (16%)
  blocking collectives  18.1 us (12%)
  local copies, waits for them, and re-layouts  11 us (7%)
  other arithmetic  1.74 us (1%)
    ppermute x24, waiting for transfers between devices, shift(): return lax.ppermute(value, 'dev', pairs)  47.9 us
    ppermute x24, starting transfers between devices, shift(): return lax.ppermute(value, 'dev', pairs)  32.3 us
    all_to_all x1, blocking collectives, body(): lax.all_to_all(packed, 'dev', split_axis=0, concat_axis=0, tiled=True)  18.1 us
    all_to_all x1, starting transfers between devices, body(): lax.all_to_all(own_gram, 'grp', split_axis=0, concat_axis=0, tiled=True)  15.8 us
    pallas_call x1, Pallas kernels, contributions(): pl.pallas_call(contribution_kernel, out_shape=(jax.ShapeDtypeStruct(xshap...  10.3 us
    unnamed x22, local copies, waits for them, and re-layouts  7.94 us
    pallas_call x1, Pallas kernels, body(): pl.pallas_call(leaf_kernel, out_shape=(jax.ShapeDtypeStruct((2, R, LEAF),...  5.09 us
    pallas_call x1, Pallas kernels, body(): pl.pallas_call(functools.partial(transfer_kernel, 2 * members), out_shape...  4.57 us
  transfers between devices with their start and end apart: 25, of which 13 were waited for; matrix products, arithmetic and copies ran while one was open for 2% of the time, Pallas kernels for 3%

profile of v1, /device:TPU:1, one launch (start us, length us, event | category | flops | bytes accessed | tf_op | source)
XLA Modules:
  0.0 151.6 jit_solution(2690509036842726599)
XLA Ops:
  0.7 1.9 %copy-done = f32[24,32,1024]{2,1,0:T(8,128)S(1)} copy-done((f32[24,32,1024]{2,1,0:T(8,128)S(1)}, f32[24,32,1024]{2,1,0:T(8,128)}, u32[]{:S(2)}) %copy-start) | copy-done | bytes 3145752
  2.6 1.9 %copy-done.1 = f32[24,32,1024]{2,1,0:T(8,128)S(1)} copy-done((f32[24,32,1024]{2,1,0:T(8,128)S(1)}, f32[24,32,1024]{2,1,0:T(8,128)}, u32[]{:S(2)}) %copy-start.1) | copy-done | bytes 3145752
  6.8 10.3 %contributions.1 = (f32[4,2,8,32,512]{4,3,2,1,0:T(8,128)S(1)}, f32[8,2,4,32,512]{4,3,2,1,0:T(8,128)}) custom-call(s32[24]{0:T(128)S(1)} %copy-done.3, s32[2]{0:T(128)S(1)} %copy-done.4, s32[2]{0:T(128)S(1)} %pad_add_fusion.place_ref, f32[24,32,1024]{2,1,0:T(8,128)S(1)} %copy-done, f32[24,32,1024]{2,1,0:T(8,128)S(1)} %copy-done.1, f32[2,32,1024]{2,1,0:T(8,128)S(1)} %copy-done.2), custom_call_target="tpu_custom_call" | custom-call | flops 1000000000 | bytes 16777216 | tf_op jit(solution)/shard_map/contributions/pallas_call | solution.py:74
  18.5 3.6 %collective-permute-start.12 = (f32[1,4,32,512]{3,2,1,0:T(8,128)S(1)}, f32[1,4,32,512]{3,2,1,0:T(8,128)S(1)}, u32[]{:S(2)}, u32[]{:S(2)}) collective-permute-start(f32[1,4,32,512]{3,2,1,0:T(8,128)S(1)} %get-tuple-element.25), channel_id=1, source_target_pairs={{0,4},{1,5},{2,6},{3,7},{4,8},{5,9},{6,10},{7,11},{8,12},{9,13},{1... | collective-permute-start | bytes 786440 | tf_op jit(solution)/shard_map/ppermute | solution.py:100
  22.0 2.5 %collective-permute-start.16 = (f32[1,4,32,512]{3,2,1,0:T(8,128)S(1)}, f32[1,4,32,512]{3,2,1,0:T(8,128)S(1)}, u32[]{:S(2)}, u32[]{:S(2)}) collective-permute-start(f32[1,4,32,512]{3,2,1,0:T(8,128)S(1)} %get-tuple-element.26), channel_id=1, source_target_pairs={{0,28},{1,29},{2,30},{3,31},{4,0},{5,1},{6,2},{7,3},{8,4},{9,5},{1... | collective-permute-start | bytes 786440 | tf_op jit(solution)/shard_map/ppermute | solution.py:100
  27.5 2.0 %collective-permute-done.12 = f32[1,4,32,512]{3,2,1,0:T(8,128)S(1)} collective-permute-done((f32[1,4,32,512]{3,2,1,0:T(8,128)S(1)}, f32[1,4,32,512]{3,2,1,0:T(8,128)S(1)}, u32[]{:S(2)}, u32[]{:S(2)}) %collective-permute-start.12) | collective-permute-done | bytes 262176 | tf_op jit(solution)/shard_map/ppermute | solution.py:100
  29.7 2.5 %collective-permute-start.17 = (f32[2,4,32,512]{3,2,1,0:T(8,128)S(1)}, f32[2,4,32,512]{3,2,1,0:T(8,128)S(1)}, u32[]{:S(2)}, u32[]{:S(2)}) collective-permute-start(f32[2,4,32,512]{3,2,1,0:T(8,128)S(1)} %pad_maximum_fusion.3), channel_id=1, source_target_pairs={{0,28},{1,29},{2,30},{3,31},{4,0},{5,1},{6,2},{7,3},{8,4},{9,5},{1... | collective-permute-start | bytes 1572872 | tf_op jit(solution)/shard_map/ppermute | solution.py:100
  32.4 5.3 %collective-permute-done = f32[1,8,32,512]{3,2,1,0:T(8,128)S(1)} collective-permute-done((f32[1,8,32,512]{3,2,1,0:T(8,128)S(1)}, f32[1,8,32,512]{3,2,1,0:T(8,128)S(1)}, u32[]{:S(2)}, u32[]{:S(2)}) %collective-permute-start) | collective-permute-done | bytes 524320 | tf_op jit(solution)/shard_map/ppermute | solution.py:100
  40.6 3.7 %collective-permute-done.13 = f32[2,4,32,512]{3,2,1,0:T(8,128)S(1)} collective-permute-done((f32[2,4,32,512]{3,2,1,0:T(8,128)S(1)}, f32[2,4,32,512]{3,2,1,0:T(8,128)S(1)}, u32[]{:S(2)}, u32[]{:S(2)}) %collective-permute-start.13) | collective-permute-done | bytes 524320 | tf_op jit(solution)/shard_map/ppermute | solution.py:100
  44.5 11.0 %collective-permute-done.14 = f32[2,4,32,512]{3,2,1,0:T(8,128)S(1)} collective-permute-done((f32[2,4,32,512]{3,2,1,0:T(8,128)S(1)}, f32[2,4,32,512]{3,2,1,0:T(8,128)S(1)}, u32[]{:S(2)}, u32[]{:S(2)}) %collective-permute-start.14) | collective-permute-done | bytes 524320 | tf_op jit(solution)/shard_map/ppermute | solution.py:100
  55.9 4.8 %collective-permute-done.3 = f32[2,8,32,512]{3,2,1,0:T(8,128)S(1)} collective-permute-done((f32[2,8,32,512]{3,2,1,0:T(8,128)S(1)}, f32[2,8,32,512]{3,2,1,0:T(8,128)S(1)}, u32[]{:S(2)}, u32[]{:S(2)}) %collective-permute-start.3) | collective-permute-done | bytes 1048608 | tf_op jit(solution)/shard_map/ppermute | solution.py:100
  60.7 2.4 %collective-permute-done.1 = f32[2,8,32,512]{3,2,1,0:T(8,128)S(1)} collective-permute-done((f32[2,8,32,512]{3,2,1,0:T(8,128)S(1)}, f32[2,8,32,512]{3,2,1,0:T(8,128)S(1)}, u32[]{:S(2)}, u32[]{:S(2)}) %collective-permute-start.1) | collective-permute-done | bytes 1048608 | tf_op jit(solution)/shard_map/ppermute | solution.py:100
  69.4 2.8 %collective-permute-start.5 = (f32[2,32,512]{2,1,0:T(8,128)S(1)}, f32[2,32,512]{2,1,0:T(8,128)S(1)}, u32[]{:S(2)}, u32[]{:S(2)}) collective-permute-start(f32[2,32,512]{2,1,0:T(8,128)S(1)} %pad_maximum_fusion.4), channel_id=1, source_target_pairs={{0,4},{1,5},{2,6},{3,7},{4,8},{5,9},{6,10},{7,11},{8,12},{9,13},{1... | collective-permute-start | bytes 393224 | tf_op jit(solution)/shard_map/ppermute | solution.py:100
  73.9 7.7 %collective-permute-done.5 = f32[2,32,512]{2,1,0:T(8,128)S(1)} collective-permute-done((f32[2,32,512]{2,1,0:T(8,128)S(1)}, f32[2,32,512]{2,1,0:T(8,128)S(1)}, u32[]{:S(2)}, u32[]{:S(2)}) %collective-permute-start.5) | collective-permute-done | bytes 131104 | tf_op jit(solution)/shard_map/ppermute | solution.py:100
  81.6 3.2 %collective-permute-done.9 = f32[2,32,512]{2,1,0:T(8,128)S(1)} collective-permute-done((f32[2,32,512]{2,1,0:T(8,128)S(1)}, f32[2,32,512]{2,1,0:T(8,128)S(1)}, u32[]{:S(2)}, u32[]{:S(2)}) %collective-permute-start.9) | collective-permute-done | bytes 131104 | tf_op jit(solution)/shard_map/ppermute | solution.py:100
  85.0 2.4 %collective-permute-start.6 = (f32[2,32,512]{2,1,0:T(8,128)S(1)}, f32[2,32,512]{2,1,0:T(8,128)S(1)}, u32[]{:S(2)}, u32[]{:S(2)}) collective-permute-start(f32[2,32,512]{2,1,0:T(8,128)S(1)} %get-tuple-element.38), channel_id=1, source_target_pairs={{0,4},{1,5},{2,6},{3,7},{4,8},{5,9},{6,10},{7,11},{8,12},{9,13},{1... | collective-permute-start | bytes 393224 | tf_op jit(solution)/shard_map/ppermute | solution.py:100
  87.6 4.8 %collective-permute-start.22 = (f32[1,32,512]{2,1,0:T(8,128)S(1)}, f32[1,32,512]{2,1,0:T(8,128)S(1)}, u32[]{:S(2)}, u32[]{:S(2)}) collective-permute-start(f32[1,32,512]{2,1,0:T(8,128)S(1)} %get-tuple-element.46), channel_id=1, source_target_pairs={{0,3},{1,0},{2,1},{3,2},{4,7},{5,4},{6,5},{7,6},{8,11},{9,8},{10,9... | collective-permute-start | bytes 196616 | tf_op jit(solution)/shard_map/ppermute | solution.py:100
  94.0 3.0 %collective-permute-done.20 = f32[1,32,512]{2,1,0:T(8,128)S(1)} collective-permute-done((f32[1,32,512]{2,1,0:T(8,128)S(1)}, f32[1,32,512]{2,1,0:T(8,128)S(1)}, u32[]{:S(2)}, u32[]{:S(2)}) %collective-permute-start.20) | collective-permute-done | bytes 65568 | tf_op jit(solution)/shard_map/ppermute | solution.py:100
  97.1 2.7 %collective-permute-start.23 = (f32[2,32,512]{2,1,0:T(8,128)S(1)}, f32[2,32,512]{2,1,0:T(8,128)S(1)}, u32[]{:S(2)}, u32[]{:S(2)}) collective-permute-start(f32[2,32,512]{2,1,0:T(8,128)S(1)} %pad_maximum_fusion.7), channel_id=1, source_target_pairs={{0,3},{1,0},{2,1},{3,2},{4,7},{5,4},{6,5},{7,6},{8,11},{9,8},{10,9... | collective-permute-start | bytes 393224 | tf_op jit(solution)/shard_map/ppermute | solution.py:100
  103.4 2.4 %sample.1 = (f32[2,32,1024]{2,1,0:T(8,128)}, f32[2,32,32]{2,1,0:T(8,128)}, f32[32,8,128]{2,1,0:T(8,128)}) custom-call(f32[2,32,512]{2,1,0:T(8,128)} %slice_bitcast_fusion.13.xo_ref, f32[2,32,512]{2,1,0:T(8,128)} %copy-done.8, f32[2,32,512]{2,1,0:T(8,128)} %copy-done.7, f32[2,32,512]{2,1,0:T(8,128)} %slice_bitcast_fusion.8.zo_ref, f32[2,32,512]{2,1,0:T(8,128)} %copy-done.9, ...), custom_call_target="tpu_custom_call" | custom-call | tf_op jit(solution)/shard_map/sample/pallas_call | solution.py:229
  105.9 18.1 %all_to_all.10.every_ref = f32[32,8,128]{2,1,0:T(8,128)} all-to-all(f32[32,8,128]{2,1,0:T(8,128)} %get-tuple-element.17), channel_id=1, replica_groups=mesh['grp'=8,'dev'=32] {'dev'}, dimensions={0} | all-to-all | bytes 262144 | tf_op jit(solution)/shard_map/all_to_all | solution.py:238
  125.5 15.8 %all-to-all-start.1 = ((f32[8,8,128]{2,1,0:T(8,128)}), f32[8,8,128]{2,1,0:T(8,128)S(1)}, u32[]{:S(2)}, u32[]{:S(2)}) async-start(f32[8,8,128]{2,1,0:T(8,128)} %group.1.own_ref), calls=%async_computation.1 | async-start | bytes 65536 | tf_op jit(solution)/shard_map/all_to_all | solution.py:252
  141.4 5.1 %leaf.1 = (f32[2,32,1024]{2,1,0:T(8,128)}, f32[2,32,32]{2,1,0:T(8,128)}) custom-call(f32[2,32,32]{2,1,0:T(8,128)} %get-tuple-element.14.gram_ref, f32[2,32,1024]{2,1,0:T(8,128)} %get-tuple-element.15.sample_ref), custom_call_target="tpu_custom_call" | custom-call | tf_op jit(solution)/shard_map/leaf/pallas_call | solution.py:239
  147.1 4.6 %transfer.1 = (f32[2,32,32]{2,1,0:T(8,128)}, f32[1,32,32]{2,1,0:T(8,128)}) custom-call(f32[8,8,128]{2,1,0:T(8,128)} %group.1.own_ref, f32[8,8,128]{2,1,0:T(8,128)} %copy-done.6, f32[2,32,32]{2,1,0:T(8,128)} %get-tuple-element.18.upper_ref), custom_call_target="tpu_custom_call" | custom-call | tf_op jit(solution)/shard_map/transfer/pallas_call | solution.py:253
  (80 shorter events, 26.1 us)
Async XLA Ops:
  18.5 11.1 %collective-permute-start.12 = (f32[1,4,32,512]{3,2,1,0:T(8,128)S(1)}, f32[1,4,32,512]{3,2,1,0:T(8,128)S(1)}, u32[]{:S(2)}, u32[]{:S(2)}) collective-permute-start(f32[1,4,32,512]{3,2,1,0:T(8,128)S(1)} %get-tuple-element.25), channel_id=1, source_target_pairs={{0,4},{1,5},{2,6},{3,7},{4,8},{5,9},{6,10},{7,11},{8,12},{9,13},{1... | collective-permute-start | bytes 786440 | tf_op jit(solution)/shard_map/ppermute | solution.py:100
  22.0 7.6 %collective-permute-start.16 = (f32[1,4,32,512]{3,2,1,0:T(8,128)S(1)}, f32[1,4,32,512]{3,2,1,0:T(8,128)S(1)}, u32[]{:S(2)}, u32[]{:S(2)}) collective-permute-start(f32[1,4,32,512]{3,2,1,0:T(8,128)S(1)} %get-tuple-element.26), channel_id=1, source_target_pairs={{0,28},{1,29},{2,30},{3,31},{4,0},{5,1},{6,2},{7,3},{8,4},{9,5},{1... | collective-permute-start | bytes 786440 | tf_op jit(solution)/shard_map/ppermute | solution.py:100
  24.8 12.9 %collective-permute-start = (f32[1,8,32,512]{3,2,1,0:T(8,128)S(1)}, f32[1,8,32,512]{3,2,1,0:T(8,128)S(1)}, u32[]{:S(2)}, u32[]{:S(2)}) collective-permute-start(f32[1,8,32,512]{3,2,1,0:T(8,128)S(1)} %get-tuple-element.31), channel_id=1, source_target_pairs={{0,1},{1,2},{2,3},{3,0},{4,5},{5,6},{6,7},{7,4},{8,9},{9,10},{10,1... | collective-permute-start | bytes 1572872 | tf_op jit(solution)/shard_map/ppermute | solution.py:100
  26.6 11.7 %collective-permute-start.2 = (f32[1,8,32,512]{3,2,1,0:T(8,128)S(1)}, f32[1,8,32,512]{3,2,1,0:T(8,128)S(1)}, u32[]{:S(2)}, u32[]{:S(2)}) collective-permute-start(f32[1,8,32,512]{3,2,1,0:T(8,128)S(1)} %get-tuple-element.32), channel_id=1, source_target_pairs={{0,3},{1,0},{2,1},{3,2},{4,7},{5,4},{6,5},{7,6},{8,11},{9,8},{10,9... | collective-permute-start | bytes 1572872 | tf_op jit(solution)/shard_map/ppermute | solution.py:100
  29.7 14.8 %collective-permute-start.17 = (f32[2,4,32,512]{3,2,1,0:T(8,128)S(1)}, f32[2,4,32,512]{3,2,1,0:T(8,128)S(1)}, u32[]{:S(2)}, u32[]{:S(2)}) collective-permute-start(f32[2,4,32,512]{3,2,1,0:T(8,128)S(1)} %pad_maximum_fusion.3), channel_id=1, source_target_pairs={{0,28},{1,29},{2,30},{3,31},{4,0},{5,1},{6,2},{7,3},{8,4},{9,5},{1... | collective-permute-start | bytes 1572872 | tf_op jit(solution)/shard_map/ppermute | solution.py:100
  32.3 12.0 %collective-permute-start.13 = (f32[2,4,32,512]{3,2,1,0:T(8,128)S(1)}, f32[2,4,32,512]{3,2,1,0:T(8,128)S(1)}, u32[]{:S(2)}, u32[]{:S(2)}) collective-permute-start(f32[2,4,32,512]{3,2,1,0:T(8,128)S(1)} %pad_maximum_fusion.2), channel_id=1, source_target_pairs={{0,4},{1,5},{2,6},{3,7},{4,8},{5,9},{6,10},{7,11},{8,12},{9,13},{1... | collective-permute-start | bytes 1572872 | tf_op jit(solution)/shard_map/ppermute | solution.py:100
  38.6 22.1 %collective-permute-start.3 = (f32[2,8,32,512]{3,2,1,0:T(8,128)S(1)}, f32[2,8,32,512]{3,2,1,0:T(8,128)S(1)}, u32[]{:S(2)}, u32[]{:S(2)}) collective-permute-start(f32[2,8,32,512]{3,2,1,0:T(8,128)S(1)} %pad_maximum_fusion.1), channel_id=1, source_target_pairs={{0,3},{1,0},{2,1},{3,2},{4,7},{5,4},{6,5},{7,6},{8,11},{9,8},{10,9... | collective-permute-start | bytes 3145736 | tf_op jit(solution)/shard_map/ppermute | solution.py:100
  40.5 22.6 %collective-permute-start.1 = (f32[2,8,32,512]{3,2,1,0:T(8,128)S(1)}, f32[2,8,32,512]{3,2,1,0:T(8,128)S(1)}, u32[]{:S(2)}, u32[]{:S(2)}) collective-permute-start(f32[2,8,32,512]{3,2,1,0:T(8,128)S(1)} %pad_maximum_fusion), channel_id=1, source_target_pairs={{0,1},{1,2},{2,3},{3,0},{4,5},{5,6},{6,7},{7,4},{8,9},{9,10},{10,1... | collective-permute-start | bytes 3145736 | tf_op jit(solution)/shard_map/ppermute | solution.py:100
  44.4 11.1 %collective-permute-start.14 = (f32[2,4,32,512]{3,2,1,0:T(8,128)S(1)}, f32[2,4,32,512]{3,2,1,0:T(8,128)S(1)}, u32[]{:S(2)}, u32[]{:S(2)}) collective-permute-start(f32[2,4,32,512]{3,2,1,0:T(8,128)S(1)} %bitcast_add_fusion.3), channel_id=1, source_target_pairs={{0,4},{1,5},{2,6},{3,7},{4,8},{5,9},{6,10},{7,11},{8,12},{9,13},{1... | collective-permute-start | bytes 1572872 | tf_op jit(solution)/shard_map/ppermute | solution.py:100
  55.8 16.5 %collective-permute-start.18 = (f32[2,4,32,512]{3,2,1,0:T(8,128)S(1)}, f32[2,4,32,512]{3,2,1,0:T(8,128)S(1)}, u32[]{:S(2)}, u32[]{:S(2)}) collective-permute-start(f32[2,4,32,512]{3,2,1,0:T(8,128)S(1)} %get-tuple-element.22), channel_id=1, source_target_pairs={{0,28},{1,29},{2,30},{3,31},{4,0},{5,1},{6,2},{7,3},{8,4},{9,5},{1... | collective-permute-start | bytes 1572872 | tf_op jit(solution)/shard_map/ppermute | solution.py:100
  63.6 5.0 %collective-permute-start.4 = (f32[1,32,512]{2,1,0:T(8,128)S(1)}, f32[1,32,512]{2,1,0:T(8,128)S(1)}, u32[]{:S(2)}, u32[]{:S(2)}) collective-permute-start(f32[1,32,512]{2,1,0:T(8,128)S(1)} %get-tuple-element.41), channel_id=1, source_target_pairs={{0,4},{1,5},{2,6},{3,7},{4,8},{5,9},{6,10},{7,11},{8,12},{9,13},{1... | collective-permute-start | bytes 196616 | tf_op jit(solution)/shard_map/ppermute | solution.py:100
  67.0 20.4 %collective-permute-start.15 = (f32[2,4,32,512]{3,2,1,0:T(8,128)S(1)}, f32[2,4,32,512]{3,2,1,0:T(8,128)S(1)}, u32[]{:S(2)}, u32[]{:S(2)}) collective-permute-start(f32[2,4,32,512]{3,2,1,0:T(8,128)S(1)} %get-tuple-element.21), channel_id=1, source_target_pairs={{0,4},{1,5},{2,6},{3,7},{4,8},{5,9},{6,10},{7,11},{8,12},{9,13},{1... | collective-permute-start | bytes 1572872 | tf_op jit(solution)/shard_map/ppermute | solution.py:100
  69.4 12.2 %collective-permute-start.5 = (f32[2,32,512]{2,1,0:T(8,128)S(1)}, f32[2,32,512]{2,1,0:T(8,128)S(1)}, u32[]{:S(2)}, u32[]{:S(2)}) collective-permute-start(f32[2,32,512]{2,1,0:T(8,128)S(1)} %pad_maximum_fusion.4), channel_id=1, source_target_pairs={{0,4},{1,5},{2,6},{3,7},{4,8},{5,9},{6,10},{7,11},{8,12},{9,13},{1... | collective-permute-start | bytes 393224 | tf_op jit(solution)/shard_map/ppermute | solution.py:100
  72.3 15.1 %collective-permute-start.19 = (f32[2,4,32,512]{3,2,1,0:T(8,128)S(1)}, f32[2,4,32,512]{3,2,1,0:T(8,128)S(1)}, u32[]{:S(2)}, u32[]{:S(2)}) collective-permute-start(f32[2,4,32,512]{3,2,1,0:T(8,128)S(1)} %bitcast_add_fusion.2), channel_id=1, source_target_pairs={{0,28},{1,29},{2,30},{3,31},{4,0},{5,1},{6,2},{7,3},{8,4},{9,5},{1... | collective-permute-start | bytes 1572872 | tf_op jit(solution)/shard_map/ppermute | solution.py:100
  72.4 12.4 %collective-permute-start.9 = (f32[2,32,512]{2,1,0:T(8,128)S(1)}, f32[2,32,512]{2,1,0:T(8,128)S(1)}, u32[]{:S(2)}, u32[]{:S(2)}) collective-permute-start(f32[2,32,512]{2,1,0:T(8,128)S(1)} %pad_maximum_fusion.5), channel_id=1, source_target_pairs={{0,28},{1,29},{2,30},{3,31},{4,0},{5,1},{6,2},{7,3},{8,4},{9,5},{1... | collective-permute-start | bytes 393224 | tf_op jit(solution)/shard_map/ppermute | solution.py:100
  84.8 7.5 %collective-permute-start.10 = (f32[2,32,512]{2,1,0:T(8,128)S(1)}, f32[2,32,512]{2,1,0:T(8,128)S(1)}, u32[]{:S(2)}, u32[]{:S(2)}) collective-permute-start(f32[2,32,512]{2,1,0:T(8,128)S(1)} %get-tuple-element.37), channel_id=1, source_target_pairs={{0,28},{1,29},{2,30},{3,31},{4,0},{5,1},{6,2},{7,3},{8,4},{9,5},{1... | collective-permute-start | bytes 393224 | tf_op jit(solution)/shard_map/ppermute | solution.py:100
  85.0 7.4 %collective-permute-start.6 = (f32[2,32,512]{2,1,0:T(8,128)S(1)}, f32[2,32,512]{2,1,0:T(8,128)S(1)}, u32[]{:S(2)}, u32[]{:S(2)}) collective-permute-start(f32[2,32,512]{2,1,0:T(8,128)S(1)} %get-tuple-element.38), channel_id=1, source_target_pairs={{0,4},{1,5},{2,6},{3,7},{4,8},{5,9},{6,10},{7,11},{8,12},{9,13},{1... | collective-permute-start | bytes 393224 | tf_op jit(solution)/shard_map/ppermute | solution.py:100
  87.6 6.4 %collective-permute-start.22 = (f32[1,32,512]{2,1,0:T(8,128)S(1)}, f32[1,32,512]{2,1,0:T(8,128)S(1)}, u32[]{:S(2)}, u32[]{:S(2)}) collective-permute-start(f32[1,32,512]{2,1,0:T(8,128)S(1)} %get-tuple-element.46), channel_id=1, source_target_pairs={{0,3},{1,0},{2,1},{3,2},{4,7},{5,4},{6,5},{7,6},{8,11},{9,8},{10,9... | collective-permute-start | bytes 196616 | tf_op jit(solution)/shard_map/ppermute | solution.py:100
  92.3 4.6 %collective-permute-start.20 = (f32[1,32,512]{2,1,0:T(8,128)S(1)}, f32[1,32,512]{2,1,0:T(8,128)S(1)}, u32[]{:S(2)}, u32[]{:S(2)}) collective-permute-start(f32[1,32,512]{2,1,0:T(8,128)S(1)} %get-tuple-element.48), channel_id=1, source_target_pairs={{0,1},{1,2},{2,3},{3,0},{4,5},{5,6},{6,7},{7,4},{8,9},{9,10},{10,1... | collective-permute-start | bytes 196616 | tf_op jit(solution)/shard_map/ppermute | solution.py:100
  92.4 8.1 %collective-permute-start.11 = (f32[2,32,512]{2,1,0:T(8,128)S(1)}, f32[2,32,512]{2,1,0:T(8,128)S(1)}, u32[]{:S(2)}, u32[]{:S(2)}) collective-permute-start(f32[2,32,512]{2,1,0:T(8,128)S(1)} %get-tuple-element.35), channel_id=1, source_target_pairs={{0,28},{1,29},{2,30},{3,31},{4,0},{5,1},{6,2},{7,3},{8,4},{9,5},{1... | collective-permute-start | bytes 393224 | tf_op jit(solution)/shard_map/ppermute | solution.py:100
  93.0 7.5 %collective-permute-start.7 = (f32[2,32,512]{2,1,0:T(8,128)S(1)}, f32[2,32,512]{2,1,0:T(8,128)S(1)}, u32[]{:S(2)}, u32[]{:S(2)}) collective-permute-start(f32[2,32,512]{2,1,0:T(8,128)S(1)} %get-tuple-element.36), channel_id=1, source_target_pairs={{0,4},{1,5},{2,6},{3,7},{4,8},{5,9},{6,10},{7,11},{8,12},{9,13},{1... | collective-permute-start | bytes 393224 | tf_op jit(solution)/shard_map/ppermute | solution.py:100
  97.0 5.1 %collective-permute-start.21 = (f32[2,32,512]{2,1,0:T(8,128)S(1)}, f32[2,32,512]{2,1,0:T(8,128)S(1)}, u32[]{:S(2)}, u32[]{:S(2)}) collective-permute-start(f32[2,32,512]{2,1,0:T(8,128)S(1)} %pad_maximum_fusion.6), channel_id=1, source_target_pairs={{0,1},{1,2},{2,3},{3,0},{4,5},{5,6},{6,7},{7,4},{8,9},{9,10},{10,1... | collective-permute-start | bytes 393224 | tf_op jit(solution)/shard_map/ppermute | solution.py:100
  97.1 5.0 %collective-permute-start.23 = (f32[2,32,512]{2,1,0:T(8,128)S(1)}, f32[2,32,512]{2,1,0:T(8,128)S(1)}, u32[]{:S(2)}, u32[]{:S(2)}) collective-permute-start(f32[2,32,512]{2,1,0:T(8,128)S(1)} %pad_maximum_fusion.7), channel_id=1, source_target_pairs={{0,3},{1,0},{2,1},{3,2},{4,7},{5,4},{6,5},{7,6},{8,11},{9,8},{10,9... | collective-permute-start | bytes 393224 | tf_op jit(solution)/shard_map/ppermute | solution.py:100
  125.5 20.9 %all-to-all-start.1 = ((f32[8,8,128]{2,1,0:T(8,128)}), f32[8,8,128]{2,1,0:T(8,128)S(1)}, u32[]{:S(2)}, u32[]{:S(2)}) async-start(f32[8,8,128]{2,1,0:T(8,128)} %group.1.own_ref), calls=%async_computation.1 | async-start | bytes 65536 | tf_op jit(solution)/shard_map/all_to_all | solution.py:252
  (12 other events, 27.9 us)

commit v2 on v1

--- a/solution.py
+++ b/solution.py
@@ -11,9 +11,10 @@
 NZ, NX = 8, 4
 R = 32
 LEAF = 1024
-SPLIT = 512
-SLOTS_STEP = 4
+PARTS = (("x", 0, 640, 0), ("z", 640, 384, 0), ("x", 0, 640, 1), ("z", 640, 384, 1))
+GROUP = 4
 HIGHEST = lax.Precision.HIGHEST
+X_ORDER, Z_ORDER = (0, 2, 3, 1), (0, 4, 6, 1, 3, 7, 5, 2)
 
 
 def halves(value):
@@ -22,100 +23,160 @@
     return high, low
 
 
-def contribution_kernel(rows_ref, count_ref, place_ref, u_ref, v_ref, sketch_ref, xfirst_ref, zfirst_ref):
-    step = pl.program_id(0)
-
-    @pl.when(step == 0)
-    def _():
-        xfirst_ref[...] = jnp.zeros_like(xfirst_ref)
-        zfirst_ref[...] = jnp.zeros_like(zfirst_ref)
-
+def lookup(table, index):
+    packed = sum(entry << (4 * i) for i, entry in enumerate(table))
+    return (jnp.int32(packed) >> (4 * index)) & 15
+
+
+def x_partner(step, core, x):
+    q = (x - core) % NX
+    return ((q ^ 1 if step == 0 else q ^ 3) + core) % NX
+
+
+def z_partner(step, core, z):
+    w = (z - core) % NZ
+    odd = w % 2
+    other = (w ^ 1, w - 1 + 2 * odd, w + 3 + 2 * odd)[step]
+    return (other + core) % NZ
+
+
+def contribution_kernel(rows_hbm, count_hbm, u_hbm, v_hbm, sketch_hbm, *refs):
+    outs, scratch = refs[: 2 * len(PARTS)], refs[2 * len(PARTS) :]
+    rows_ref, count_ref, u_ref, v_ref, sketch_ref, value_ref, sems = scratch
+    slots = u_ref.shape[0]
+    groups = slots // GROUP
+    small = [
+        pltpu.make_async_copy(rows_hbm, rows_ref, sems.at[0]),
+        pltpu.make_async_copy(count_hbm, count_ref, sems.at[1]),
+        pltpu.make_async_copy(sketch_hbm, sketch_ref, sems.at[2]),
+    ]
+    large = [
+        [
+            pltpu.make_async_copy(
+                hbm.at[pl.ds(g * GROUP, GROUP)],
+                ref.at[pl.ds(g * GROUP, GROUP)],
+                sems.at[3 + 2 * g + k],
+            )
+            for k, (hbm, ref) in enumerate(((v_hbm, v_ref), (u_hbm, u_ref)))
+        ]
+        for g in range(groups)
+    ]
+    for copy in small + sum(large, []):
+        copy.start()
+    for ref in outs:
+        ref[...] = jnp.zeros_like(ref)
+    core = lax.axis_index("grp") % 2
+    me = lax.axis_index("dev")
+    own_w = (me // NX - core) & (NZ - 1)
+    own_q = (me % NX - core) & (NX - 1)
+    for copy in small:
+        copy.wait()
     first_count = count_ref[0]
     live_count = first_count + count_ref[1]
     sketch_high, sketch_low = halves(sketch_ref[...].reshape(2 * R, LEAF))
-    v_high, v_low = halves(v_ref[...].reshape(SLOTS_STEP * R, LEAF))
+    both = jnp.concatenate([sketch_high, sketch_low], axis=0)
     contract = (((1,), (1,)), ((), ()))
-    both = jnp.concatenate([sketch_high, sketch_low], axis=0)
-    wide = lax.dot_general(v_high, both, contract, preferred_element_type=jnp.float32)
-    couplings = (
-        wide[:, : 2 * R]
-        + wide[:, 2 * R :]
-        + lax.dot_general(v_low, sketch_high, contract, preferred_element_type=jnp.float32)
-    )
-    for t in range(SLOTS_STEP):
-        slot = step * SLOTS_STEP + t
-
-        @pl.when(slot < live_count)
-        def _():
-            row = rows_ref[slot]
-            device = row // 2
-            cluster = row % 2
-            dz = (device // NX - place_ref[0] + NZ) % NZ
-            dx = (device % NX - place_ref[1] + NX) % NX
+    for g in range(groups):
+        large[g][0].wait()
+        v_high, v_low = halves(v_ref[g * GROUP : (g + 1) * GROUP].reshape(GROUP * R, LEAF))
+        wide = lax.dot_general(v_high, both, contract, preferred_element_type=jnp.float32)
+        couplings = (
+            wide[:, : 2 * R]
+            + wide[:, 2 * R :]
+            + lax.dot_general(v_low, sketch_high, contract, preferred_element_type=jnp.float32)
+        )
+        large[g][1].wait()
+        for t in range(GROUP):
             part = couplings[t * R : (t + 1) * R]
-            coupling = jnp.where(slot < first_count, part[:, :R], part[:, R:])
+            coupling = jnp.where(g * GROUP + t < first_count, part[:, :R], part[:, R:])
             c_high, c_low = halves(coupling)
-            u_high, u_low = halves(u_ref[t])
+            u_high, u_low = halves(u_ref[g * GROUP + t])
             left = jnp.concatenate([c_high, c_low, c_high], axis=0)
             right = jnp.concatenate([u_high, u_high, u_low], axis=0)
-            value = lax.dot_general(
+            value_ref[t] = lax.dot_general(
                 left, right, (((0,), (0,)), ((), ())), preferred_element_type=jnp.float32
             )
-            xfirst_ref[dx, cluster, dz] += value[:, :SPLIT]
-            zfirst_ref[dz, cluster, dx] += value[:, SPLIT:]
-
-
-def contributions(block_row, col_count, place, u_blocks, v_blocks, sketch):
+        for t in range(GROUP):
+            slot = g * GROUP + t
+            row = rows_ref[slot] & (2 * NZ * NX - 1)
+            cluster = row & 1
+            live = slot < live_count
+            to_q = (((row >> 1) & (NX - 1)) - core) & (NX - 1)
+            to_w = ((row >> 3) - core) & (NZ - 1)
+            step_z = jnp.where(own_w & 1 == 0, to_w - own_w, own_w - to_w) & (NZ - 1)
+            x_slot, z_slot = lookup(X_ORDER, own_q ^ to_q), lookup(Z_ORDER, step_z)
+            index = {"x": x_slot * NZ + z_slot, "z": z_slot * NX + x_slot}
+            for k, (axis, start, width, which) in enumerate(PARTS):
+                for far in range(2):
+                    here = live & (index[axis] >> 4 == far)
+                    if which >= 0:
+                        here = here & (cluster == which)
+
+                    @pl.when(here)
+                    def _():
+                        at = index[axis] & 15
+                        first = pl.multiple_of(cluster * R, R) if which < 0 else 0
+                        outs[2 * k + far][at, pl.ds(first, R)] += value_ref[
+                            t, :, start : start + width
+                        ]
+
+
+def contributions(block_row, col_count, u_blocks, v_blocks, sketch):
     slots = u_blocks.shape[0]
-    xshape = (NX, 2, NZ, R, SPLIT)
-    zshape = (NZ, 2, NX, R, LEAF - SPLIT)
-    block = lambda i, *_: (i, 0, 0)
-    whole = lambda i, *_: (0, 0, 0, 0, 0)
+    shapes = [
+        jax.ShapeDtypeStruct((NZ * NX // 2, R if which >= 0 else 2 * R, width), jnp.float32)
+        for _, _, width, which in PARTS
+        for _ in range(2)
+    ]
     return pl.pallas_call(
         contribution_kernel,
-        out_shape=(
-            jax.ShapeDtypeStruct(xshape, jnp.float32),
-            jax.ShapeDtypeStruct(zshape, jnp.float32),
-        ),
-        grid_spec=pltpu.PrefetchScalarGridSpec(
-            num_scalar_prefetch=3,
-            grid=(slots // SLOTS_STEP,),
-            in_specs=[
-                pl.BlockSpec((SLOTS_STEP, R, LEAF), block),
-                pl.BlockSpec((SLOTS_STEP, R, LEAF), block),
-                pl.BlockSpec((2, R, LEAF), lambda i, *_: (0, 0, 0)),
-            ],
-            out_specs=(pl.BlockSpec(xshape, whole), pl.BlockSpec(zshape, whole)),
-        ),
-        compiler_params=pltpu.CompilerParams(vmem_limit_bytes=40 << 20),
+        out_shape=shapes,
+        in_specs=[pl.BlockSpec(memory_space=pltpu.HBM)] * 5,
+        out_specs=[pl.BlockSpec(memory_space=pltpu.VMEM)] * len(shapes),
+        scratch_shapes=[
+            pltpu.SMEM((slots,), jnp.int32),
+            pltpu.SMEM((2,), jnp.int32),
+            pltpu.VMEM((slots, R, LEAF), jnp.float32),
+            pltpu.VMEM((slots, R, LEAF), jnp.float32),
+            pltpu.VMEM((2, R, LEAF), jnp.float32),
+            pltpu.VMEM((GROUP, R, LEAF), jnp.float32),
+            pltpu.SemaphoreType.DMA((3 + 2 * (slots // GROUP),)),
+        ],
+        compiler_params=pltpu.CompilerParams(vmem_limit_bytes=24 << 20),
         cost_estimate=pl.CostEstimate(flops=10**9, bytes_accessed=16 << 20, transcendentals=0),
         name="contributions",
-    )(block_row, col_count, place, u_blocks, v_blocks, sketch)
-
-
-def shift(value, dz, dx):
-    pairs = [
-        (z * NX + x, (z + dz) % NZ * NX + (x + dx) % NX) for z in range(NZ) for x in range(NX)
-    ]
-    return lax.ppermute(value, "dev", pairs)
-
-
-def ring_sum(chunks, plus, minus):
-    count = len(chunks)
-    middle = count // 2
-    forward = plus(chunks[middle][:1])
-    backward = minus(chunks[middle][1:])
-    for r in range(middle - 1, 0, -1):
-        ahead, behind = chunks[r], chunks[count - r]
-        if r == middle - 1:
-            forward = jnp.concatenate([ahead[:1] + forward, ahead[1:]], axis=0)
-            backward = jnp.concatenate([behind[:1], behind[1:] + backward], axis=0)
-        else:
-            forward = ahead + forward
-            backward = behind + backward
-        forward = plus(forward)
-        backward = minus(backward)
-    return chunks[0], forward, backward
+    )(block_row, col_count, u_blocks, v_blocks, sketch)
+
+
+def exchange(value, axis, step):
+    pairs = []
+    groups = lax.axis_size("grp")
+    for g in range(groups):
+        for z in range(NZ):
+            for x in range(NX):
+                if axis == "x":
+                    to = z * NX + x_partner(step, g % 2, x)
+                else:
+                    to = z_partner(step, g % 2, z) * NX + x
+                pairs.append((g * NZ * NX + z * NX + x, g * NZ * NX + to))
+    return lax.ppermute(value, ("grp", "dev"), pairs)
+
+
+def scatter_sums(parts):
+    order = {
+        "x": (("x", 0), ("x", 1), ("z", 0), ("z", 1), ("z", 2)),
+        "z": (("z", 0), ("z", 1), ("z", 2), ("x", 0), ("x", 1)),
+    }
+    terms = []
+    for (first, _, _, _), (keep, send) in zip(PARTS, parts):
+        for n, (axis, step) in enumerate(order[first]):
+            got = exchange(send, axis, step)
+            if n < 4:
+                half = keep.shape[0] // 2
+                send = keep[half:] + got[half:]
+                keep = keep[:half] + got[:half]
+        terms.append((keep[0], got[0]))
+    return terms
 
 
 def pack(gram):
@@ -146,14 +207,19 @@
     return [(d[:, :R], d[:, R:]) for d in done]
 
 
-def sample_kernel(xo_ref, xf_ref, xb_ref, zo_ref, zf_ref, zb_ref, diag_ref, sketch_ref, sample_ref, gram_ref, packed_ref):
+def sample_kernel(*refs):
+    terms, (diag_ref, sketch_ref, sample_ref, gram_ref, packed_ref) = refs[:-5], refs[-5:]
+    for k, (_, start, width, which) in enumerate(PARTS):
+        far = terms[2 * k][...] + terms[2 * k + 1][...]
+        for i in (0, 1) if which < 0 else (which,):
+            rows = far[i * R : (i + 1) * R] if which < 0 else far
+            columns = slice(start, start + width)
+            sample_ref[i, :, columns] = (
+                rows + diag_ref[i : i + 1, columns] * sketch_ref[i, :, columns]
+            )
     total = jnp.zeros((R, R), jnp.float32)
     for i in range(2):
-        far = jnp.concatenate(
-            [xo_ref[i] + xf_ref[i] + xb_ref[i], zo_ref[i] + zf_ref[i] + zb_ref[i]], axis=1
-        )
-        sample = far + diag_ref[i : i + 1] * sketch_ref[i]
-        sample_ref[i] = sample
+        sample = sample_ref[i]
         gram = lax.dot_general(
             sample,
             sample,
@@ -213,19 +279,8 @@
 def body(u_blocks, v_blocks, sketch, near_diag, block_row, col_count):
     members = lax.axis_size("dev")
     groups = lax.axis_size("grp")
-    me = lax.axis_index("dev")
-    place = jnp.stack([me // NX, me % NX]).astype(jnp.int32)
-    xfirst, zfirst = contributions(block_row, col_count, place, u_blocks, v_blocks, sketch)
-    along = {
-        "x": (lambda a: shift(a, 0, 1), lambda a: shift(a, 0, -1)),
-        "z": (lambda a: shift(a, 1, 0), lambda a: shift(a, -1, 0)),
-    }
-    own, ahead, behind = ring_sum([xfirst[i] for i in range(NX)], *along["x"])
-    part = own + ahead + behind
-    xterms = ring_sum([part[:, i] for i in range(NZ)], *along["z"])
-    own, ahead, behind = ring_sum([zfirst[i] for i in range(NZ)], *along["z"])
-    part = own + ahead + behind
-    zterms = ring_sum([part[:, i] for i in range(NX)], *along["x"])
+    halved = contributions(block_row, col_count, u_blocks, v_blocks, sketch)
+    terms = scatter_sums(list(zip(halved[::2], halved[1::2])))
     sample, gram, packed = pl.pallas_call(
         sample_kernel,
         out_shape=(
@@ -234,7 +289,7 @@
             jax.ShapeDtypeStruct((members, 8, 128), jnp.float32),
         ),
         name="sample",
-    )(*xterms, *zterms, near_diag, sketch)
+    )(*sum(terms, ()), near_diag, sketch)
     every = lax.all_to_all(packed, "dev", split_axis=0, concat_axis=0, tiled=True)
     leaf_basis, upper = pl.pallas_call(
         leaf_kernel,

time: 151 us -> 145 us (0.960)
  local copies, waits for them, and re-layouts: 11 us -> 7.27 us
  Pallas kernels: 23.9 us -> 20.6 us
  starting transfers between devices: 48.1 us -> 50.6 us
  blocking collectives: 18.1 us -> 15.9 us
  waiting for transfers between devices: 47.9 us -> 45.9 us
  other arithmetic: 1.74 us -> 3.49 us
    pallas_call x1, Pallas kernels: 10.3 us -> 7.04 us  [contributions(): pl.pallas_call(contribution_kernel, out_shape=shapes, in_specs=[pl.BlockS...]
    ppermute x24 -> x20, starting transfers between devices: 32.3 us -> 34.8 us  [exchange(): return lax.ppermute(value, ('grp', 'dev'), pairs)]
    all_to_all x1, blocking collectives: 18.1 us -> 15.9 us  [body(): lax.all_to_all(packed, 'dev', split_axis=0, concat_axis=0, tiled=True)]
    add x11 -> x16, other arithmetic: 1.34 us -> 3.49 us  [the longest x4 2.56 us: scatter_sums(): send = keep[half:] + got[half:]]
    ppermute x24 -> x20, waiting for transfers between devices: 47.9 us -> 45.9 us  [exchange(): return lax.ppermute(value, ('grp', 'dev'), pairs)]
    slice x4 -> x0, local copies, waits for them, and re-layouts: 1.73 us -> none  [the longest x2 1.69 us: ring_sum(): forward = plus(chunks[middle][:1])]
    unnamed x22 -> x20, local copies, waits for them, and re-layouts: 7.94 us -> 7.27 us
  transfers between devices with their start and end apart: 25 -> 21, of which waited for: 13 -> 10; matrix products, arithmetic and copies ran while one was open for 2% -> 2% of each run, Pallas kernels for 3% -> 4%
where the time goes in v2:
time: 145 us; the launch traced here: 144 us
  starting transfers between devices  50.6 us (35%)
  waiting for transfers between devices  45.9 us (32%)
  Pallas kernels  20.6 us (14%)
  blocking collectives  15.9 us (11%)
  local copies, waits for them, and re-layouts  7.27 us (5%)
  other arithmetic  3.49 us (2%)
    ppermute x20, waiting for transfers between devices, exchange(): return lax.ppermute(value, ('grp', 'dev'), pairs)  45.9 us
    ppermute x20, starting transfers between devices, exchange(): return lax.ppermute(value, ('grp', 'dev'), pairs)  34.8 us
    all_to_all x1, blocking collectives, body(): lax.all_to_all(packed, 'dev', split_axis=0, concat_axis=0, tiled=True)  15.9 us
    all_to_all x1, starting transfers between devices, body(): lax.all_to_all(own_gram, 'grp', split_axis=0, concat_axis=0, tiled=True)  15.8 us
    unnamed x20, local copies, waits for them, and re-layouts  7.27 us
    pallas_call x1, Pallas kernels, contributions(): pl.pallas_call(contribution_kernel, out_shape=shapes, in_specs=[pl.BlockS...  7.04 us
    pallas_call x1, Pallas kernels, body(): pl.pallas_call(leaf_kernel, out_shape=(jax.ShapeDtypeStruct((2, R, LEAF),...  5.09 us
    pallas_call x1, Pallas kernels, body(): pl.pallas_call(functools.partial(transfer_kernel, 2 * members), out_shape...  4.57 us
  transfers between devices with their start and end apart: 21, of which 10 were waited for; matrix products, arithmetic and copies ran while one was open for 2% of the time, Pallas kernels for 4%

profile of v2, /device:TPU:1, one launch (start us, length us, event | category | flops | bytes accessed | tf_op | source)
XLA Modules:
  0.0 144.5 jit_solution(16155613614167025142)
XLA Ops:
  0.6 1.9 %copy-done = f32[24,32,1024]{2,1,0:T(8,128)S(1)} copy-done((f32[24,32,1024]{2,1,0:T(8,128)S(1)}, f32[24,32,1024]{2,1,0:T(8,128)}, u32[]{:S(2)}) %copy-start) | copy-done | bytes 3145752
  2.5 1.9 %copy-done.1 = f32[24,32,1024]{2,1,0:T(8,128)S(1)} copy-done((f32[24,32,1024]{2,1,0:T(8,128)S(1)}, f32[24,32,1024]{2,1,0:T(8,128)}, u32[]{:S(2)}) %copy-start.1) | copy-done | bytes 3145752
  6.7 7.0 %contributions.1 = (f32[16,32,640]{2,1,0:T(8,128)S(1)}, f32[16,32,640]{2,1,0:T(8,128)S(1)}, f32[16,32,384]{2,1,0:T(8,128)S(1)}, f32[16,32,384]{2,1,0:T(8,128)S(1...) custom-call(s32[24]{0:T(128)S(1)} %copy-done.3, ...), custom_call_target="tpu_custom_call" | custom-call | flops 1000000000 | bytes 16777216 | tf_op jit(solution)/shard_map/contributions/pallas_call | solution.py:131
  13.7 6.5 %collective-permute-start.5 = (f32[16,32,384]{2,1,0:T(8,128)S(1)}, f32[16,32,384]{2,1,0:T(8,128)S(1)}, u32[]{:S(2)}, u32[]{:S(2)}) collective-permute-start(f32[16,32,384]{2,1,0:T(8,128)S(1)} %get-tuple-element.21), channel_id=1, source_target_pairs={{0,4},{1,5},{2,6},{3,7},{4,0},{5,1},{6,2},{7,3},{8,12},{9,13},{10,... | collective-permute-start | bytes 2359304 | tf_op jit(solution)/shard_map/ppermute | solution.py:162
  20.3 2.5 %collective-permute-start = (f32[16,32,640]{2,1,0:T(8,128)S(1)}, f32[16,32,640]{2,1,0:T(8,128)S(1)}, u32[]{:S(2)}, u32[]{:S(2)}) collective-permute-start(f32[16,32,640]{2,1,0:T(8,128)S(1)} %get-tuple-element.19), channel_id=1, source_target_pairs={{0,1},{1,0},{2,3},{3,2},{4,5},{5,4},{6,7},{7,6},{8,9},{9,8},{10,11... | collective-permute-start | bytes 3932168 | tf_op jit(solution)/shard_map/ppermute | solution.py:162
  23.0 6.6 %collective-permute-done.5 = f32[16,32,384]{2,1,0:T(8,128)S(1)} collective-permute-done((f32[16,32,384]{2,1,0:T(8,128)S(1)}, f32[16,32,384]{2,1,0:T(8,128)S(1)}, u32[]{:S(2)}, u32[]{:S(2)}) %collective-permute-start.5) | collective-permute-done | bytes 786464 | tf_op jit(solution)/shard_map/ppermute | solution.py:162
  29.8 12.2 %collective-permute-done.15 = f32[16,32,384]{2,1,0:T(8,128)S(1)} collective-permute-done((f32[16,32,384]{2,1,0:T(8,128)S(1)}, f32[16,32,384]{2,1,0:T(8,128)S(1)}, u32[]{:S(2)}, u32[]{:S(2)}) %collective-permute-start.15) | collective-permute-done | bytes 786464 | tf_op jit(solution)/shard_map/ppermute | solution.py:162
  42.3 4.2 %collective-permute-start.7 = (f32[4,32,384]{2,1,0:T(8,128)S(1)}, f32[4,32,384]{2,1,0:T(8,128)S(1)}, u32[]{:S(2)}, u32[]{:S(2)}) collective-permute-start(f32[4,32,384]{2,1,0:T(8,128)S(1)} %get-tuple-element.48), channel_id=1, source_target_pairs={{0,12},{1,13},{2,14},{3,15},{4,24},{5,25},{6,26},{7,27},{8,20},{9,... | collective-permute-start | bytes 589832 | tf_op jit(solution)/shard_map/ppermute | solution.py:162
  46.5 4.7 %collective-permute-done.16 = f32[8,32,384]{2,1,0:T(8,128)S(1)} collective-permute-done((f32[8,32,384]{2,1,0:T(8,128)S(1)}, f32[8,32,384]{2,1,0:T(8,128)S(1)}, u32[]{:S(2)}, u32[]{:S(2)}) %collective-permute-start.16) | collective-permute-done | bytes 393248 | tf_op jit(solution)/shard_map/ppermute | solution.py:162
  51.3 6.3 %collective-permute-start.17 = (f32[4,32,384]{2,1,0:T(8,128)S(1)}, f32[4,32,384]{2,1,0:T(8,128)S(1)}, u32[]{:S(2)}, u32[]{:S(2)}) collective-permute-start(f32[4,32,384]{2,1,0:T(8,128)S(1)} %get-tuple-element.46), channel_id=1, source_target_pairs={{0,12},{1,13},{2,14},{3,15},{4,24},{5,25},{6,26},{7,27},{8,20},{9,... | collective-permute-start | bytes 589832 | tf_op jit(solution)/shard_map/ppermute | solution.py:162
  59.6 2.6 %collective-permute-start.8 = (f32[2,32,384]{2,1,0:T(8,128)S(1)}, f32[2,32,384]{2,1,0:T(8,128)S(1)}, u32[]{:S(2)}, u32[]{:S(2)}) collective-permute-start(f32[2,32,384]{2,1,0:T(8,128)S(1)} %get-tuple-element.56), channel_id=1, source_target_pairs={{0,1},{1,0},{2,3},{3,2},{4,5},{5,4},{6,7},{7,6},{8,9},{9,8},{10,11... | collective-permute-start | bytes 294920 | tf_op jit(solution)/shard_map/ppermute | solution.py:162
  63.6 4.0 %collective-permute-done.1 = f32[8,32,640]{2,1,0:T(8,128)S(1)} collective-permute-done((f32[8,32,640]{2,1,0:T(8,128)S(1)}, f32[8,32,640]{2,1,0:T(8,128)S(1)}, u32[]{:S(2)}, u32[]{:S(2)}) %collective-permute-start.1) | collective-permute-done | bytes 655392 | tf_op jit(solution)/shard_map/ppermute | solution.py:162
  68.4 8.3 %collective-permute-done.11 = f32[8,32,640]{2,1,0:T(8,128)S(1)} collective-permute-done((f32[8,32,640]{2,1,0:T(8,128)S(1)}, f32[8,32,640]{2,1,0:T(8,128)S(1)}, u32[]{:S(2)}, u32[]{:S(2)}) %collective-permute-start.11) | collective-permute-done | bytes 655392 | tf_op jit(solution)/shard_map/ppermute | solution.py:162
  79.2 2.4 %collective-permute-start.3 = (f32[2,32,640]{2,1,0:T(8,128)S(1)}, f32[2,32,640]{2,1,0:T(8,128)S(1)}, u32[]{:S(2)}, u32[]{:S(2)}) collective-permute-start(f32[2,32,640]{2,1,0:T(8,128)S(1)} %get-tuple-element.52), channel_id=1, source_target_pairs={{0,28},{1,29},{2,30},{3,31},{4,8},{5,9},{6,10},{7,11},{8,4},{9,5},... | collective-permute-start | bytes 491528 | tf_op jit(solution)/shard_map/ppermute | solution.py:162
  81.6 2.4 %collective-permute-done.12 = f32[4,32,640]{2,1,0:T(8,128)S(1)} collective-permute-done((f32[4,32,640]{2,1,0:T(8,128)S(1)}, f32[4,32,640]{2,1,0:T(8,128)S(1)}, u32[]{:S(2)}, u32[]{:S(2)}) %collective-permute-start.12) | collective-permute-done | bytes 327712 | tf_op jit(solution)/shard_map/ppermute | solution.py:162
  87.0 2.6 %collective-permute-done.13 = f32[2,32,640]{2,1,0:T(8,128)S(1)} collective-permute-done((f32[2,32,640]{2,1,0:T(8,128)S(1)}, f32[2,32,640]{2,1,0:T(8,128)S(1)}, u32[]{:S(2)}, u32[]{:S(2)}) %collective-permute-start.13) | collective-permute-done | bytes 163872 | tf_op jit(solution)/shard_map/ppermute | solution.py:162
  93.0 2.6 %collective-permute-done.19 = f32[1,32,384]{2,1,0:T(8,128)S(1)} collective-permute-done((f32[1,32,384]{2,1,0:T(8,128)S(1)}, f32[1,32,384]{2,1,0:T(8,128)S(1)}, u32[]{:S(2)}, u32[]{:S(2)}) %collective-permute-start.19) | collective-permute-done | bytes 49184 | tf_op jit(solution)/shard_map/ppermute | solution.py:162
  95.6 2.4 %collective-permute-done.14 = f32[1,32,640]{2,1,0:T(8,128)S(1)} collective-permute-done((f32[1,32,640]{2,1,0:T(8,128)S(1)}, f32[1,32,640]{2,1,0:T(8,128)S(1)}, u32[]{:S(2)}, u32[]{:S(2)}) %collective-permute-start.14) | collective-permute-done | bytes 81952 | tf_op jit(solution)/shard_map/ppermute | solution.py:162
  98.6 2.3 %sample.1 = (f32[2,32,1024]{2,1,0:T(8,128)}, f32[2,32,32]{2,1,0:T(8,128)}, f32[32,8,128]{2,1,0:T(8,128)}) custom-call(f32[32,640]{1,0:T(8,128)} %get-tuple-element.60.refs_0_, f32[32,640]{1,0:T(8,128)} %bitcast.12, f32[32,384]{1,0:T(8,128)} %get-tuple-element.64.refs_2_, f32[32,384]{1,0:T(8,128)} %bitcast.14, f32[32,640]{1,0:T(8,128)} %get-tuple-element.58.refs_4_, ...), custom_call_target="tpu_custom_call" | custom-call | tf_op jit(solution)/shard_map/sample/pallas_call | solution.py:284
  101.0 15.9 %all_to_all.10.every_ref = f32[32,8,128]{2,1,0:T(8,128)} all-to-all(f32[32,8,128]{2,1,0:T(8,128)} %get-tuple-element.29), channel_id=1, replica_groups=mesh['grp'=8,'dev'=32] {'dev'}, dimensions={0} | all-to-all | bytes 262144 | tf_op jit(solution)/shard_map/all_to_all | solution.py:293
  116.9 1.5 %group.1.own_ref = f32[8,8,128]{2,1,0:T(8,128)} custom-call(f32[32,8,128]{2,1,0:T(8,128)} %all_to_all.10.every_ref), custom_call_target="tpu_custom_call" | custom-call | tf_op jit(solution)/shard_map/group/pallas_call | solution.py:302
  118.4 15.8 %all-to-all-start.1 = ((f32[8,8,128]{2,1,0:T(8,128)}), f32[8,8,128]{2,1,0:T(8,128)S(1)}, u32[]{:S(2)}, u32[]{:S(2)}) async-start(f32[8,8,128]{2,1,0:T(8,128)} %group.1.own_ref), calls=%async_computation.1 | async-start | bytes 65536 | tf_op jit(solution)/shard_map/all_to_all | solution.py:307
  134.2 5.1 %leaf.1 = (f32[2,32,1024]{2,1,0:T(8,128)}, f32[2,32,32]{2,1,0:T(8,128)}) custom-call(f32[2,32,32]{2,1,0:T(8,128)} %get-tuple-element.26.gram_ref, f32[2,32,1024]{2,1,0:T(8,128)} %get-tuple-element.27.sample_ref), custom_call_target="tpu_custom_call" | custom-call | tf_op jit(solution)/shard_map/leaf/pallas_call | solution.py:294
  139.9 4.6 %transfer.1 = (f32[2,32,32]{2,1,0:T(8,128)}, f32[1,32,32]{2,1,0:T(8,128)}) custom-call(f32[8,8,128]{2,1,0:T(8,128)} %group.1.own_ref, f32[8,8,128]{2,1,0:T(8,128)} %copy-done.5, f32[2,32,32]{2,1,0:T(8,128)} %get-tuple-element.30.upper_ref), custom_call_target="tpu_custom_call" | custom-call | tf_op jit(solution)/shard_map/transfer/pallas_call | solution.py:308
  (60 shorter events, 17.5 us)
Async XLA Ops:
  13.7 15.8 %collective-permute-start.5 = (f32[16,32,384]{2,1,0:T(8,128)S(1)}, f32[16,32,384]{2,1,0:T(8,128)S(1)}, u32[]{:S(2)}, u32[]{:S(2)}) collective-permute-start(f32[16,32,384]{2,1,0:T(8,128)S(1)} %get-tuple-element.21), channel_id=1, source_target_pairs={{0,4},{1,5},{2,6},{3,7},{4,0},{5,1},{6,2},{7,3},{8,12},{9,13},{10,... | collective-permute-start | bytes 2359304 | tf_op jit(solution)/shard_map/ppermute | solution.py:162
  20.2 21.8 %collective-permute-start.15 = (f32[16,32,384]{2,1,0:T(8,128)S(1)}, f32[16,32,384]{2,1,0:T(8,128)S(1)}, u32[]{:S(2)}, u32[]{:S(2)}) collective-permute-start(f32[16,32,384]{2,1,0:T(8,128)S(1)} %get-tuple-element.25), channel_id=1, source_target_pairs={{0,4},{1,5},{2,6},{3,7},{4,0},{5,1},{6,2},{7,3},{8,12},{9,13},{10,... | collective-permute-start | bytes 2359304 | tf_op jit(solution)/shard_map/ppermute | solution.py:162
  20.3 37.3 %collective-permute-start = (f32[16,32,640]{2,1,0:T(8,128)S(1)}, f32[16,32,640]{2,1,0:T(8,128)S(1)}, u32[]{:S(2)}, u32[]{:S(2)}) collective-permute-start(f32[16,32,640]{2,1,0:T(8,128)S(1)} %get-tuple-element.19), channel_id=1, source_target_pairs={{0,1},{1,0},{2,3},{3,2},{4,5},{5,4},{6,7},{7,6},{8,9},{9,8},{10,11... | collective-permute-start | bytes 3932168 | tf_op jit(solution)/shard_map/ppermute | solution.py:162
  22.8 36.2 %collective-permute-start.10 = (f32[16,32,640]{2,1,0:T(8,128)S(1)}, f32[16,32,640]{2,1,0:T(8,128)S(1)}, u32[]{:S(2)}, u32[]{:S(2)}) collective-permute-start(f32[16,32,640]{2,1,0:T(8,128)S(1)} %get-tuple-element.23), channel_id=1, source_target_pairs={{0,1},{1,0},{2,3},{3,2},{4,5},{5,4},{6,7},{7,6},{8,9},{9,8},{10,11... | collective-permute-start | bytes 3932168 | tf_op jit(solution)/shard_map/ppermute | solution.py:162
  29.7 12.5 %collective-permute-start.6 = (f32[8,32,384]{2,1,0:T(8,128)S(1)}, f32[8,32,384]{2,1,0:T(8,128)S(1)}, u32[]{:S(2)}, u32[]{:S(2)}) collective-permute-start(f32[8,32,384]{2,1,0:T(8,128)S(1)} %get-tuple-element.40), channel_id=1, source_target_pairs={{0,28},{1,29},{2,30},{3,31},{4,8},{5,9},{6,10},{7,11},{8,4},{9,5},... | collective-permute-start | bytes 1179656 | tf_op jit(solution)/shard_map/ppermute | solution.py:162
  42.1 9.1 %collective-permute-start.16 = (f32[8,32,384]{2,1,0:T(8,128)S(1)}, f32[8,32,384]{2,1,0:T(8,128)S(1)}, u32[]{:S(2)}, u32[]{:S(2)}) collective-permute-start(f32[8,32,384]{2,1,0:T(8,128)S(1)} %get-tuple-element.38), channel_id=1, source_target_pairs={{0,28},{1,29},{2,30},{3,31},{4,8},{5,9},{6,10},{7,11},{8,4},{9,5},... | collective-permute-start | bytes 1179656 | tf_op jit(solution)/shard_map/ppermute | solution.py:162
  42.3 17.3 %collective-permute-start.7 = (f32[4,32,384]{2,1,0:T(8,128)S(1)}, f32[4,32,384]{2,1,0:T(8,128)S(1)}, u32[]{:S(2)}, u32[]{:S(2)}) collective-permute-start(f32[4,32,384]{2,1,0:T(8,128)S(1)} %get-tuple-element.48), channel_id=1, source_target_pairs={{0,12},{1,13},{2,14},{3,15},{4,24},{5,25},{6,26},{7,27},{8,20},{9,... | collective-permute-start | bytes 589832 | tf_op jit(solution)/shard_map/ppermute | solution.py:162
  51.3 10.9 %collective-permute-start.17 = (f32[4,32,384]{2,1,0:T(8,128)S(1)}, f32[4,32,384]{2,1,0:T(8,128)S(1)}, u32[]{:S(2)}, u32[]{:S(2)}) collective-permute-start(f32[4,32,384]{2,1,0:T(8,128)S(1)} %get-tuple-element.46), channel_id=1, source_target_pairs={{0,12},{1,13},{2,14},{3,15},{4,24},{5,25},{6,26},{7,27},{8,20},{9,... | collective-permute-start | bytes 589832 | tf_op jit(solution)/shard_map/ppermute | solution.py:162
  57.7 9.8 %collective-permute-start.1 = (f32[8,32,640]{2,1,0:T(8,128)S(1)}, f32[8,32,640]{2,1,0:T(8,128)S(1)}, u32[]{:S(2)}, u32[]{:S(2)}) collective-permute-start(f32[8,32,640]{2,1,0:T(8,128)S(1)} %get-tuple-element.36), channel_id=1, source_target_pairs={{0,3},{1,2},{2,1},{3,0},{4,7},{5,6},{6,5},{7,4},{8,11},{9,10},{10,... | collective-permute-start | bytes 1966088 | tf_op jit(solution)/shard_map/ppermute | solution.py:162
  59.1 17.6 %collective-permute-start.11 = (f32[8,32,640]{2,1,0:T(8,128)S(1)}, f32[8,32,640]{2,1,0:T(8,128)S(1)}, u32[]{:S(2)}, u32[]{:S(2)}) collective-permute-start(f32[8,32,640]{2,1,0:T(8,128)S(1)} %get-tuple-element.34), channel_id=1, source_target_pairs={{0,3},{1,2},{2,1},{3,0},{4,7},{5,6},{6,5},{7,4},{8,11},{9,10},{10,... | collective-permute-start | bytes 1966088 | tf_op jit(solution)/shard_map/ppermute | solution.py:162
  59.6 17.7 %collective-permute-start.8 = (f32[2,32,384]{2,1,0:T(8,128)S(1)}, f32[2,32,384]{2,1,0:T(8,128)S(1)}, u32[]{:S(2)}, u32[]{:S(2)}) collective-permute-start(f32[2,32,384]{2,1,0:T(8,128)S(1)} %get-tuple-element.56), channel_id=1, source_target_pairs={{0,1},{1,0},{2,3},{3,2},{4,5},{5,4},{6,7},{7,6},{8,9},{9,8},{10,11... | collective-permute-start | bytes 294920 | tf_op jit(solution)/shard_map/ppermute | solution.py:162
  62.2 29.6 %collective-permute-start.18 = (f32[2,32,384]{2,1,0:T(8,128)S(1)}, f32[2,32,384]{2,1,0:T(8,128)S(1)}, u32[]{:S(2)}, u32[]{:S(2)}) collective-permute-start(f32[2,32,384]{2,1,0:T(8,128)S(1)} %get-tuple-element.54), channel_id=1, source_target_pairs={{0,1},{1,0},{2,3},{3,2},{4,5},{5,4},{6,7},{7,6},{8,9},{9,8},{10,11... | collective-permute-start | bytes 294920 | tf_op jit(solution)/shard_map/ppermute | solution.py:162
  67.6 11.5 %collective-permute-start.2 = (f32[4,32,640]{2,1,0:T(8,128)S(1)}, f32[4,32,640]{2,1,0:T(8,128)S(1)}, u32[]{:S(2)}, u32[]{:S(2)}) collective-permute-start(f32[4,32,640]{2,1,0:T(8,128)S(1)} %get-tuple-element.44), channel_id=1, source_target_pairs={{0,4},{1,5},{2,6},{3,7},{4,0},{5,1},{6,2},{7,3},{8,12},{9,13},{10,... | collective-permute-start | bytes 983048 | tf_op jit(solution)/shard_map/ppermute | solution.py:162
  76.8 7.2 %collective-permute-start.12 = (f32[4,32,640]{2,1,0:T(8,128)S(1)}, f32[4,32,640]{2,1,0:T(8,128)S(1)}, u32[]{:S(2)}, u32[]{:S(2)}) collective-permute-start(f32[4,32,640]{2,1,0:T(8,128)S(1)} %get-tuple-element.42), channel_id=1, source_target_pairs={{0,4},{1,5},{2,6},{3,7},{4,0},{5,1},{6,2},{7,3},{8,12},{9,13},{10,... | collective-permute-start | bytes 983048 | tf_op jit(solution)/shard_map/ppermute | solution.py:162
  77.9 15.1 %collective-permute-start.9 = (f32[1,32,384]{2,1,0:T(8,128)S(1)}, f32[1,32,384]{2,1,0:T(8,128)S(1)}, u32[]{:S(2)}, u32[]{:S(2)}) collective-permute-start(f32[1,32,384]{2,1,0:T(8,128)S(1)} %get-tuple-element.63), channel_id=1, source_target_pairs={{0,3},{1,2},{2,1},{3,0},{4,7},{5,6},{6,5},{7,4},{8,11},{9,10},{10,... | collective-permute-start | bytes 147464 | tf_op jit(solution)/shard_map/ppermute | solution.py:162
  79.2 6.3 %collective-permute-start.3 = (f32[2,32,640]{2,1,0:T(8,128)S(1)}, f32[2,32,640]{2,1,0:T(8,128)S(1)}, u32[]{:S(2)}, u32[]{:S(2)}) collective-permute-start(f32[2,32,640]{2,1,0:T(8,128)S(1)} %get-tuple-element.52), channel_id=1, source_target_pairs={{0,28},{1,29},{2,30},{3,31},{4,8},{5,9},{6,10},{7,11},{8,4},{9,5},... | collective-permute-start | bytes 491528 | tf_op jit(solution)/shard_map/ppermute | solution.py:162
  84.0 5.6 %collective-permute-start.13 = (f32[2,32,640]{2,1,0:T(8,128)S(1)}, f32[2,32,640]{2,1,0:T(8,128)S(1)}, u32[]{:S(2)}, u32[]{:S(2)}) collective-permute-start(f32[2,32,640]{2,1,0:T(8,128)S(1)} %get-tuple-element.50), channel_id=1, source_target_pairs={{0,28},{1,29},{2,30},{3,31},{4,8},{5,9},{6,10},{7,11},{8,4},{9,5},... | collective-permute-start | bytes 491528 | tf_op jit(solution)/shard_map/ppermute | solution.py:162
  86.1 9.5 %collective-permute-start.4 = (f32[1,32,640]{2,1,0:T(8,128)S(1)}, f32[1,32,640]{2,1,0:T(8,128)S(1)}, u32[]{:S(2)}, u32[]{:S(2)}) collective-permute-start(f32[1,32,640]{2,1,0:T(8,128)S(1)} %get-tuple-element.59), channel_id=1, source_target_pairs={{0,12},{1,13},{2,14},{3,15},{4,24},{5,25},{6,26},{7,27},{8,20},{9,... | collective-permute-start | bytes 245768 | tf_op jit(solution)/shard_map/ppermute | solution.py:162
  90.2 7.8 %collective-permute-start.14 = (f32[1,32,640]{2,1,0:T(8,128)S(1)}, f32[1,32,640]{2,1,0:T(8,128)S(1)}, u32[]{:S(2)}, u32[]{:S(2)}) collective-permute-start(f32[1,32,640]{2,1,0:T(8,128)S(1)} %get-tuple-element.57), channel_id=1, source_target_pairs={{0,12},{1,13},{2,14},{3,15},{4,24},{5,25},{6,26},{7,27},{8,20},{9,... | collective-permute-start | bytes 245768 | tf_op jit(solution)/shard_map/ppermute | solution.py:162
  92.4 3.2 %collective-permute-start.19 = (f32[1,32,384]{2,1,0:T(8,128)S(1)}, f32[1,32,384]{2,1,0:T(8,128)S(1)}, u32[]{:S(2)}, u32[]{:S(2)}) collective-permute-start(f32[1,32,384]{2,1,0:T(8,128)S(1)} %get-tuple-element.61), channel_id=1, source_target_pairs={{0,3},{1,2},{2,1},{3,0},{4,7},{5,6},{6,5},{7,4},{8,11},{9,10},{10,... | collective-permute-start | bytes 147464 | tf_op jit(solution)/shard_map/ppermute | solution.py:162
  93.0 5.0 %copy-start.8 = (f32[1,32,384]{2,1,0:T(8,128)}, f32[1,32,384]{2,1,0:T(8,128)S(1)}, u32[]{:S(2)}) copy-start(f32[1,32,384]{2,1,0:T(8,128)S(1)} %collective-permute-done.9) | copy-start | bytes 147460
  95.6 2.4 %copy-start.9 = (f32[1,32,384]{2,1,0:T(8,128)}, f32[1,32,384]{2,1,0:T(8,128)S(1)}, u32[]{:S(2)}) copy-start(f32[1,32,384]{2,1,0:T(8,128)S(1)} %collective-permute-done.19) | copy-start | bytes 147460
  95.6 2.4 %copy-start.6 = (f32[1,32,640]{2,1,0:T(8,128)}, f32[1,32,640]{2,1,0:T(8,128)S(1)}, u32[]{:S(2)}) copy-start(f32[1,32,640]{2,1,0:T(8,128)S(1)} %collective-permute-done.4) | copy-start | bytes 245764
  118.4 20.9 %all-to-all-start.1 = ((f32[8,8,128]{2,1,0:T(8,128)}), f32[8,8,128]{2,1,0:T(8,128)S(1)}, u32[]{:S(2)}, u32[]{:S(2)}) async-start(f32[8,8,128]{2,1,0:T(8,128)} %group.1.own_ref), calls=%async_computation.1 | async-start | bytes 65536 | tf_op jit(solution)/shard_map/all_to_all | solution.py:307
  (7 other events, 7.3 us)

commit v3 on v2

--- a/solution.py
+++ b/solution.py
@@ -11,7 +11,12 @@
 NZ, NX = 8, 4
 R = 32
 LEAF = 1024
-PARTS = (("x", 0, 640, 0), ("z", 640, 384, 0), ("x", 0, 640, 1), ("z", 640, 384, 1))
+PARTS = (("x", 0, 512, 0), ("z", 512, 512, 0), ("x", 0, 512, 1), ("z", 512, 512, 1))
+STEPS = {
+    "x": (("x", 0), ("x", 1), ("z", 0), ("z", 1)),
+    "z": (("z", 0), ("z", 1), ("x", 0), ("x", 1)),
+}
+BLOCK = 4
 GROUP = 4
 HIGHEST = lax.Precision.HIGHEST
 X_ORDER, Z_ORDER = (0, 2, 3, 1), (0, 4, 6, 1, 3, 7, 5, 2)
@@ -28,16 +33,16 @@
     return (jnp.int32(packed) >> (4 * index)) & 15
 
 
-def x_partner(step, core, x):
-    q = (x - core) % NX
-    return ((q ^ 1 if step == 0 else q ^ 3) + core) % NX
-
-
-def z_partner(step, core, z):
-    w = (z - core) % NZ
+def x_partner(step, which, x):
+    q = (x - which) % NX
+    return ((q ^ 1 if step == 0 else q ^ 3) + which) % NX
+
+
+def z_partner(step, which, z):
+    w = (z - which) % NZ
     odd = w % 2
     other = (w ^ 1, w - 1 + 2 * odd, w + 3 + 2 * odd)[step]
-    return (other + core) % NZ
+    return (other + which) % NZ
 
 
 def contribution_kernel(rows_hbm, count_hbm, u_hbm, v_hbm, sketch_hbm, *refs):
@@ -65,10 +70,7 @@
         copy.start()
     for ref in outs:
         ref[...] = jnp.zeros_like(ref)
-    core = lax.axis_index("grp") % 2
     me = lax.axis_index("dev")
-    own_w = (me // NX - core) & (NZ - 1)
-    own_q = (me % NX - core) & (NX - 1)
     for copy in small:
         copy.wait()
     first_count = count_ref[0]
@@ -101,38 +103,46 @@
             row = rows_ref[slot] & (2 * NZ * NX - 1)
             cluster = row & 1
             live = slot < live_count
-            to_q = (((row >> 1) & (NX - 1)) - core) & (NX - 1)
-            to_w = ((row >> 3) - core) & (NZ - 1)
+            own_w = (me // NX - cluster) & (NZ - 1)
+            own_q = (me % NX - cluster) & (NX - 1)
+            to_w = ((row >> 3) - cluster) & (NZ - 1)
+            to_q = (((row >> 1) & (NX - 1)) - cluster) & (NX - 1)
             step_z = jnp.where(own_w & 1 == 0, to_w - own_w, own_w - to_w) & (NZ - 1)
             x_slot, z_slot = lookup(X_ORDER, own_q ^ to_q), lookup(Z_ORDER, step_z)
-            index = {"x": x_slot * NZ + z_slot, "z": z_slot * NX + x_slot}
+            index = {
+                "x": x_slot * NZ + z_slot,
+                "z": (z_slot >> 1) * 2 * NX + x_slot * 2 + (z_slot & 1),
+            }
             for k, (axis, start, width, which) in enumerate(PARTS):
                 for far in range(2):
-                    here = live & (index[axis] >> 4 == far)
-                    if which >= 0:
-                        here = here & (cluster == which)
-
-                    @pl.when(here)
+
+                    @pl.when(live & (index[axis] >> 4 == far) & (cluster == which))
                     def _():
-                        at = index[axis] & 15
-                        first = pl.multiple_of(cluster * R, R) if which < 0 else 0
-                        outs[2 * k + far][at, pl.ds(first, R)] += value_ref[
+                        outs[2 * k + far][index[axis] & 15] += value_ref[
                             t, :, start : start + width
                         ]
+
+
+def in_hbm(value):
+    return pltpu.with_memory_space_constraint(value, pltpu.HBM)
+
+
+def in_vmem(count):
+    return [pl.BlockSpec(memory_space=pltpu.VMEM)] * count
 
 
 def contributions(block_row, col_count, u_blocks, v_blocks, sketch):
     slots = u_blocks.shape[0]
     shapes = [
-        jax.ShapeDtypeStruct((NZ * NX // 2, R if which >= 0 else 2 * R, width), jnp.float32)
-        for _, _, width, which in PARTS
+        jax.ShapeDtypeStruct((NZ * NX // 2, R, width), jnp.float32)
+        for _, _, width, _ in PARTS
         for _ in range(2)
     ]
     return pl.pallas_call(
         contribution_kernel,
         out_shape=shapes,
         in_specs=[pl.BlockSpec(memory_space=pltpu.HBM)] * 5,
-        out_specs=[pl.BlockSpec(memory_space=pltpu.VMEM)] * len(shapes),
+        out_specs=in_vmem(len(shapes)),
         scratch_shapes=[
             pltpu.SMEM((slots,), jnp.int32),
             pltpu.SMEM((2,), jnp.int32),
@@ -145,37 +155,35 @@
         compiler_params=pltpu.CompilerParams(vmem_limit_bytes=24 << 20),
         cost_estimate=pl.CostEstimate(flops=10**9, bytes_accessed=16 << 20, transcendentals=0),
         name="contributions",
-    )(block_row, col_count, u_blocks, v_blocks, sketch)
-
-
-def exchange(value, axis, step):
+    )(*(in_hbm(a) for a in (block_row, col_count, u_blocks, v_blocks, sketch)))
+
+
+def exchange(value, axis, step, which):
     pairs = []
-    groups = lax.axis_size("grp")
-    for g in range(groups):
-        for z in range(NZ):
-            for x in range(NX):
-                if axis == "x":
-                    to = z * NX + x_partner(step, g % 2, x)
-                else:
-                    to = z_partner(step, g % 2, z) * NX + x
-                pairs.append((g * NZ * NX + z * NX + x, g * NZ * NX + to))
-    return lax.ppermute(value, ("grp", "dev"), pairs)
+    for z in range(NZ):
+        for x in range(NX):
+            if axis == "x":
+                to = z * NX + x_partner(step, which, x)
+            else:
+                to = z_partner(step, which, z) * NX + x
+            pairs.append((z * NX + x, to))
+    return lax.ppermute(value, "dev", pairs)
 
 
 def scatter_sums(parts):
-    order = {
-        "x": (("x", 0), ("x", 1), ("z", 0), ("z", 1), ("z", 2)),
-        "z": (("z", 0), ("z", 1), ("z", 2), ("x", 0), ("x", 1)),
-    }
+    kept, last = [], []
+    for (first, _, _, which), (keep, send) in zip(PARTS, parts):
+        for axis, step in STEPS[first]:
+            got = exchange(send, axis, step, which)
+            half = keep.shape[0] // 2
+            send = keep[half:] + got[half:]
+            keep = keep[:half] + got[:half]
+        kept.append(keep[0])
+        last.append(send)
     terms = []
-    for (first, _, _, _), (keep, send) in zip(PARTS, parts):
-        for n, (axis, step) in enumerate(order[first]):
-            got = exchange(send, axis, step)
-            if n < 4:
-                half = keep.shape[0] // 2
-                send = keep[half:] + got[half:]
-                keep = keep[:half] + got[:half]
-        terms.append((keep[0], got[0]))
+    for i in range(0, len(PARTS), 2):
+        got = exchange(jnp.concatenate(last[i : i + 2], axis=2), "z", 2, PARTS[i][3])
+        terms += kept[i : i + 2] + [got[0]]
     return terms
 
 
@@ -188,35 +196,43 @@
 
 
 def eliminate(grams):
-    count = len(grams)
     eye = (
         lax.broadcasted_iota(jnp.int32, (R, R), 0) == lax.broadcasted_iota(jnp.int32, (R, R), 1)
     ).astype(jnp.float32)
+    wide = (R, 2 * R)
     work = [jnp.concatenate([gram, eye], axis=1) for gram in grams]
-    sublane = lax.broadcasted_iota(jnp.int32, (R, 2 * R), 0)
-    done = [jnp.zeros((R, 2 * R), jnp.float32) for _ in grams]
-    for j in range(R):
-        for i in range(count):
-            column = jnp.broadcast_to(work[i][:, j : j + 1], (R, 2 * R))
-            pivot = column[j : j + 1]
-            scale = lax.rsqrt(pivot)
-            scale = scale * (1.5 - 0.5 * pivot * scale * scale)
-            row = jnp.broadcast_to(work[i][j : j + 1] * scale, (R, 2 * R))
-            done[i] = jnp.where(sublane == j, row, done[i])
-            work[i] = work[i] - (column * jnp.broadcast_to(scale, (R, 2 * R))) * row
-    return [(d[:, :R], d[:, R:]) for d in done]
+    done = [[] for _ in grams]
+    for first in range(0, R, BLOCK):
+        columns = [
+            [jnp.broadcast_to(w[:, j : j + 1], wide) for j in range(first, first + BLOCK)]
+            for w in work
+        ]
+        for j in range(first, first + BLOCK):
+            for i in range(len(grams)):
+                column = columns[i][j - first]
+                pivot = column[j : j + 1]
+                scale = lax.rsqrt(pivot)
+                scale = scale * (1.5 - 0.5 * pivot * scale * scale)
+                row = work[i][j : j + 1] * scale
+                done[i].append(row)
+                factor = column * jnp.broadcast_to(scale, wide)
+                for k in range(j + 1, first + BLOCK):
+                    entry = columns[i][k - first]
+                    columns[i][k - first] = entry - factor * jnp.broadcast_to(
+                        entry[j : j + 1] * scale, wide
+                    )
+                work[i] = work[i] - factor * jnp.broadcast_to(row, wide)
+    whole = [jnp.concatenate(rows, axis=0) for rows in done]
+    return [(d[:, :R], d[:, R:]) for d in whole]
 
 
 def sample_kernel(*refs):
     terms, (diag_ref, sketch_ref, sample_ref, gram_ref, packed_ref) = refs[:-5], refs[-5:]
     for k, (_, start, width, which) in enumerate(PARTS):
-        far = terms[2 * k][...] + terms[2 * k + 1][...]
-        for i in (0, 1) if which < 0 else (which,):
-            rows = far[i * R : (i + 1) * R] if which < 0 else far
-            columns = slice(start, start + width)
-            sample_ref[i, :, columns] = (
-                rows + diag_ref[i : i + 1, columns] * sketch_ref[i, :, columns]
-            )
+        columns = slice(start, start + width)
+        far = terms[k // 2 * 3 + k % 2][...] + terms[k // 2 * 3 + 2][:, columns]
+        near = diag_ref[which : which + 1, columns] * sketch_ref[which, :, columns]
+        sample_ref[which, :, columns] = far + near
     total = jnp.zeros((R, R), jnp.float32)
     for i in range(2):
         sample = sample_ref[i]
@@ -288,8 +304,10 @@
             jax.ShapeDtypeStruct((2, R, R), jnp.float32),
             jax.ShapeDtypeStruct((members, 8, 128), jnp.float32),
         ),
+        in_specs=in_vmem(len(terms) + 2),
+        out_specs=in_vmem(3),
         name="sample",
-    )(*sum(terms, ()), near_diag, sketch)
+    )(*terms, near_diag, sketch)
     every = lax.all_to_all(packed, "dev", split_axis=0, concat_axis=0, tiled=True)
     leaf_basis, upper = pl.pallas_call(
         leaf_kernel,
@@ -297,11 +315,15 @@
             jax.ShapeDtypeStruct((2, R, LEAF), jnp.float32),
             jax.ShapeDtypeStruct((2, R, R), jnp.float32),
         ),
+        in_specs=in_vmem(2),
+        out_specs=[pl.BlockSpec((2, R, LEAF), lambda: (0, 0, 0))] + in_vmem(1),
         name="leaf",
     )(gram, sample)
     own_gram = pl.pallas_call(
         group_kernel,
         out_shape=jax.ShapeDtypeStruct((groups, 8, 128), jnp.float32),
+        in_specs=in_vmem(1),
+        out_specs=pl.BlockSpec(memory_space=pltpu.VMEM),
         name="group",
     )(every)
     every_group = lax.all_to_all(own_gram, "grp", split_axis=0, concat_axis=0, tiled=True)
@@ -311,6 +333,7 @@
             jax.ShapeDtypeStruct((2, R, R), jnp.float32),
             jax.ShapeDtypeStruct((1, R, R), jnp.float32),
         ),
+        in_specs=in_vmem(3),
         name="transfer",
     )(own_gram, every_group, upper)
     return (leaf_basis, transfer_leaf, transfer_group)

time: 145 us -> 117 us (0.81)
  starting transfers between devices: 50.6 us -> 38.2 us
  local copies, waits for them, and re-layouts: 7.27 us -> 1.25 us
  waiting for transfers between devices: 45.9 us -> 41.6 us
  Pallas kernels: 20.6 us -> 17.4 us
  blocking collectives: 15.9 us -> 13.9 us
    all_to_all x1, starting transfers between devices: 15.8 us -> 8.56 us  [body(): lax.all_to_all(own_gram, 'grp', split_axis=0, concat_axis=0, tiled=True)]
    unnamed x20 -> x6, local copies, waits for them, and re-layouts: 7.27 us -> 1.25 us
    ppermute x20 -> x18, waiting for transfers between devices: 45.9 us -> 40.3 us  [exchange(): return lax.ppermute(value, 'dev', pairs)]
    ppermute x20 -> x18, starting transfers between devices: 34.8 us -> 29.6 us  [exchange(): return lax.ppermute(value, 'dev', pairs)]
    all_to_all x1, blocking collectives: 15.9 us -> 13.9 us  [body(): lax.all_to_all(packed, 'dev', split_axis=0, concat_axis=0, tiled=True)]
    pallas_call x1, Pallas kernels: 5.09 us -> 3.42 us  [body(): pl.pallas_call(leaf_kernel, out_shape=(jax.ShapeDtypeStruct((2, R, LEAF),...]
    pallas_call x1, Pallas kernels: 4.57 us -> 2.91 us  [body(): pl.pallas_call(functools.partial(transfer_kernel, 2 * members), out_shape...]
  transfers between devices with their start and end apart: 21 -> 19, of which waited for: 10 -> 11; matrix products, arithmetic and copies ran while one was open for 2% -> 3% of each run, Pallas kernels for 4% -> 3%
where the time goes in v3:
time: 117 us
  waiting for transfers between devices  41.6 us (36%)
  starting transfers between devices  38.2 us (33%)
  Pallas kernels  17.4 us (15%)
  blocking collectives  13.9 us (12%)
  other arithmetic  3.9 us (3%)
  local copies, waits for them, and re-layouts  1.25 us (1%)
    ppermute x18, waiting for transfers between devices, exchange(): return lax.ppermute(value, 'dev', pairs)  40.3 us
    ppermute x18, starting transfers between devices, exchange(): return lax.ppermute(value, 'dev', pairs)  29.6 us
    all_to_all x1, blocking collectives, body(): lax.all_to_all(packed, 'dev', split_axis=0, concat_axis=0, tiled=True)  13.9 us
    all_to_all x1, starting transfers between devices, body(): lax.all_to_all(own_gram, 'grp', split_axis=0, concat_axis=0, tiled=True)  8.56 us
    pallas_call x1, Pallas kernels, contributions(): pl.pallas_call(contribution_kernel, out_shape=shapes, in_specs=[pl.BlockS...  7.15 us
    pallas_call x1, Pallas kernels, body(): pl.pallas_call(leaf_kernel, out_shape=(jax.ShapeDtypeStruct((2, R, LEAF),...  3.42 us
    pallas_call x1, Pallas kernels, body(): pl.pallas_call(functools.partial(transfer_kernel, 2 * members), out_shape...  2.91 us
    add x4, other arithmetic, scatter_sums(): send = keep[half:] + got[half:]  2.58 us
  transfers between devices with their start and end apart: 19, of which 11 were waited for; matrix products, arithmetic and copies ran while one was open for 3% of the time, Pallas kernels for 3%

profile of v3, /device:TPU:1, one launch (start us, length us, event | category | flops | bytes accessed | tf_op | source)
XLA Modules:
  0.0 116.9 jit_solution(9408484872076604287)
XLA Ops:
  0.6 7.1 %contributions.1 = (f32[16,32,512]{2,1,0:T(8,128)S(1)}, f32[16,32,512]{2,1,0:T(8,128)S(1)}, f32[16,32,512]{2,1,0:T(8,128)S(1)}, f32[16,32,512]{2,1,0:T(8,128)S(1...) custom-call(s32[24]{0:T(128)} %rows_hbm.1, ...), custom_call_target="tpu_custom_call" | custom-call | flops 1000000000 | bytes 16777216 | tf_op jit(solution)/shard_map/contributions/pallas_call | solution.py:141
  7.8 2.1 %collective-permute-start = (f32[16,32,512]{2,1,0:T(8,128)S(1)}, f32[16,32,512]{2,1,0:T(8,128)S(1)}, u32[]{:S(2)}, u32[]{:S(2)}) collective-permute-start(f32[16,32,512]{2,1,0:T(8,128)S(1)} %get-tuple-element.19), channel_id=1, source_target_pairs={{0,1},{1,0},{2,3},{3,2},{4,5},{5,4},{6,7},{7,6},{8,9},{9,8},{10,11... | collective-permute-start | bytes 3145736 | tf_op jit(solution)/shard_map/ppermute | solution.py:170
  9.9 1.7 %collective-permute-start.4 = (f32[16,32,512]{2,1,0:T(8,128)S(1)}, f32[16,32,512]{2,1,0:T(8,128)S(1)}, u32[]{:S(2)}, u32[]{:S(2)}) collective-permute-start(f32[16,32,512]{2,1,0:T(8,128)S(1)} %get-tuple-element.21), channel_id=1, source_target_pairs={{0,4},{1,5},{2,6},{3,7},{4,0},{5,1},{6,2},{7,3},{8,12},{9,13},{10,... | collective-permute-start | bytes 3145736 | tf_op jit(solution)/shard_map/ppermute | solution.py:170
  11.6 1.9 %collective-permute-start.9 = (f32[16,32,512]{2,1,0:T(8,128)S(1)}, f32[16,32,512]{2,1,0:T(8,128)S(1)}, u32[]{:S(2)}, u32[]{:S(2)}) collective-permute-start(f32[16,32,512]{2,1,0:T(8,128)S(1)} %get-tuple-element.23), channel_id=1, source_target_pairs={{0,3},{1,2},{2,1},{3,0},{4,7},{5,6},{6,5},{7,4},{8,11},{9,10},{10,... | collective-permute-start | bytes 3145736 | tf_op jit(solution)/shard_map/ppermute | solution.py:170
  13.4 4.6 %collective-permute-start.13 = (f32[16,32,512]{2,1,0:T(8,128)S(1)}, f32[16,32,512]{2,1,0:T(8,128)S(1)}, u32[]{:S(2)}, u32[]{:S(2)}) collective-permute-start(f32[16,32,512]{2,1,0:T(8,128)S(1)} %get-tuple-element.25), channel_id=1, source_target_pairs={{0,28},{1,29},{2,30},{3,31},{4,8},{5,9},{6,10},{7,11},{8,4},{9,5},... | collective-permute-start | bytes 3145736 | tf_op jit(solution)/shard_map/ppermute | solution.py:170
  18.0 13.4 %collective-permute-done = f32[16,32,512]{2,1,0:T(8,128)S(1)} collective-permute-done((f32[16,32,512]{2,1,0:T(8,128)S(1)}, f32[16,32,512]{2,1,0:T(8,128)S(1)}, u32[]{:S(2)}, u32[]{:S(2)}) %collective-permute-start) | collective-permute-done | bytes 1048608 | tf_op jit(solution)/shard_map/ppermute | solution.py:170
  31.6 3.8 %collective-permute-start.1 = (f32[8,32,512]{2,1,0:T(8,128)S(1)}, f32[8,32,512]{2,1,0:T(8,128)S(1)}, u32[]{:S(2)}, u32[]{:S(2)}) collective-permute-start(f32[8,32,512]{2,1,0:T(8,128)S(1)} %get-tuple-element.40), channel_id=1, source_target_pairs={{0,3},{1,2},{2,1},{3,0},{4,7},{5,6},{6,5},{7,4},{8,11},{9,10},{10,... | collective-permute-start | bytes 1572872 | tf_op jit(solution)/shard_map/ppermute | solution.py:170
  35.6 5.7 %collective-permute-start.5 = (f32[8,32,512]{2,1,0:T(8,128)S(1)}, f32[8,32,512]{2,1,0:T(8,128)S(1)}, u32[]{:S(2)}, u32[]{:S(2)}) collective-permute-start(f32[8,32,512]{2,1,0:T(8,128)S(1)} %get-tuple-element.38), channel_id=1, source_target_pairs={{0,28},{1,29},{2,30},{3,31},{4,8},{5,9},{6,10},{7,11},{8,4},{9,5},... | collective-permute-start | bytes 1572872 | tf_op jit(solution)/shard_map/ppermute | solution.py:170
  42.1 5.9 %collective-permute-done.1 = f32[8,32,512]{2,1,0:T(8,128)S(1)} collective-permute-done((f32[8,32,512]{2,1,0:T(8,128)S(1)}, f32[8,32,512]{2,1,0:T(8,128)S(1)}, u32[]{:S(2)}, u32[]{:S(2)}) %collective-permute-start.1) | collective-permute-done | bytes 524320 | tf_op jit(solution)/shard_map/ppermute | solution.py:170
  48.2 3.6 %collective-permute-done.5 = f32[8,32,512]{2,1,0:T(8,128)S(1)} collective-permute-done((f32[8,32,512]{2,1,0:T(8,128)S(1)}, f32[8,32,512]{2,1,0:T(8,128)S(1)}, u32[]{:S(2)}, u32[]{:S(2)}) %collective-permute-start.5) | collective-permute-done | bytes 524320 | tf_op jit(solution)/shard_map/ppermute | solution.py:170
  53.1 1.8 %collective-permute-start.11 = (f32[4,32,512]{2,1,0:T(8,128)S(1)}, f32[4,32,512]{2,1,0:T(8,128)S(1)}, u32[]{:S(2)}, u32[]{:S(2)}) collective-permute-start(f32[4,32,512]{2,1,0:T(8,128)S(1)} %get-tuple-element.44), channel_id=1, source_target_pairs={{0,28},{1,29},{2,30},{3,31},{4,8},{5,9},{6,10},{7,11},{8,4},{9,5},... | collective-permute-start | bytes 786440 | tf_op jit(solution)/shard_map/ppermute | solution.py:170
  55.9 3.0 %collective-permute-done.2 = f32[4,32,512]{2,1,0:T(8,128)S(1)} collective-permute-done((f32[4,32,512]{2,1,0:T(8,128)S(1)}, f32[4,32,512]{2,1,0:T(8,128)S(1)}, u32[]{:S(2)}, u32[]{:S(2)}) %collective-permute-start.2) | collective-permute-done | bytes 262176 | tf_op jit(solution)/shard_map/ppermute | solution.py:170
  58.9 1.7 %collective-permute-start.3 = (f32[2,32,512]{2,1,0:T(8,128)S(1)}, f32[2,32,512]{2,1,0:T(8,128)S(1)}, u32[]{:S(2)}, u32[]{:S(2)}) collective-permute-start(f32[2,32,512]{2,1,0:T(8,128)S(1)} %get-tuple-element.56), channel_id=1, source_target_pairs={{0,28},{1,29},{2,30},{3,31},{4,8},{5,9},{6,10},{7,11},{8,4},{9,5},... | collective-permute-start | bytes 393224 | tf_op jit(solution)/shard_map/ppermute | solution.py:170
  62.2 3.3 %collective-permute-done.3 = f32[2,32,512]{2,1,0:T(8,128)S(1)} collective-permute-done((f32[2,32,512]{2,1,0:T(8,128)S(1)}, f32[2,32,512]{2,1,0:T(8,128)S(1)}, u32[]{:S(2)}, u32[]{:S(2)}) %collective-permute-start.3) | collective-permute-done | bytes 131104 | tf_op jit(solution)/shard_map/ppermute | solution.py:170
  68.0 1.7 %collective-permute-start.8 = (f32[1,32,1024]{2,1,0:T(8,128)S(1)}, f32[1,32,1024]{2,1,0:T(8,128)S(1)}, u32[]{:S(2)}, u32[]{:S(2)}) collective-permute-start(f32[1,32,1024]{2,1,0:T(8,128)S(1)} %pad_maximum_fusion), channel_id=1, source_target_pairs={{0,12},{1,13},{2,14},{3,15},{4,24},{5,25},{6,26},{7,27},{8,20},{9,... | collective-permute-start | bytes 393224 | tf_op jit(solution)/shard_map/ppermute | solution.py:170
  71.0 1.6 %collective-permute-start.17 = (f32[1,32,1024]{2,1,0:T(8,128)S(1)}, f32[1,32,1024]{2,1,0:T(8,128)S(1)}, u32[]{:S(2)}, u32[]{:S(2)}) collective-permute-start(f32[1,32,1024]{2,1,0:T(8,128)S(1)} %pad_maximum_fusion.1), channel_id=1, source_target_pairs={{0,20},{1,21},{2,22},{3,23},{4,16},{5,17},{6,18},{7,19},{8,28},{9,... | collective-permute-start | bytes 393224 | tf_op jit(solution)/shard_map/ppermute | solution.py:170
  72.7 2.6 %collective-permute-done.8 = f32[1,32,1024]{2,1,0:T(8,128)S(1)} collective-permute-done((f32[1,32,1024]{2,1,0:T(8,128)S(1)}, f32[1,32,1024]{2,1,0:T(8,128)S(1)}, u32[]{:S(2)}, u32[]{:S(2)}) %collective-permute-start.8) | collective-permute-done | bytes 131104 | tf_op jit(solution)/shard_map/ppermute | solution.py:170
  75.2 6.4 %collective-permute-done.17 = f32[1,32,1024]{2,1,0:T(8,128)S(1)} collective-permute-done((f32[1,32,1024]{2,1,0:T(8,128)S(1)}, f32[1,32,1024]{2,1,0:T(8,128)S(1)}, u32[]{:S(2)}, u32[]{:S(2)}) %collective-permute-start.17) | collective-permute-done | bytes 131104 | tf_op jit(solution)/shard_map/ppermute | solution.py:170
  82.3 2.4 %sample.1 = (f32[2,32,1024]{2,1,0:T(8,128)}, f32[2,32,32]{2,1,0:T(8,128)}, f32[32,8,128]{2,1,0:T(8,128)}) custom-call(f32[32,512]{1,0:T(8,128)} %get-tuple-element.62.refs_0_, f32[32,512]{1,0:T(8,128)} %get-tuple-element.64.refs_1_, f32[32,1024]{1,0:T(8,128)} %bitcast.10, f32[32,512]{1,0:T(8,128)} %get-tuple-element.58.refs_3_, ...), custom_call_target="tpu_custom_call" | custom-call | tf_op jit(solution)/shard_map/sample/pallas_call | solution.py:300
  84.7 13.9 %all_to_all.10.every_ref = f32[32,8,128]{2,1,0:T(8,128)} all-to-all(f32[32,8,128]{2,1,0:T(8,128)} %get-tuple-element.29), channel_id=1, replica_groups=mesh['grp'=8,'dev'=32] {'dev'}, dimensions={0} | all-to-all | bytes 262144 | tf_op jit(solution)/shard_map/all_to_all | solution.py:311
  98.6 1.5 %group.1.own_ref = f32[8,8,128]{2,1,0:T(8,128)} custom-call(f32[32,8,128]{2,1,0:T(8,128)} %all_to_all.10.every_ref), custom_call_target="tpu_custom_call" | custom-call | tf_op jit(solution)/shard_map/group/pallas_call | solution.py:322
  100.1 8.6 %all-to-all-start.1 = ((f32[8,8,128]{2,1,0:T(8,128)}), f32[8,8,128]{2,1,0:T(8,128)S(1)}, u32[]{:S(2)}, u32[]{:S(2)}) async-start(f32[8,8,128]{2,1,0:T(8,128)} %group.1.own_ref), calls=%async_computation.1 | async-start | bytes 65536 | tf_op jit(solution)/shard_map/all_to_all | solution.py:329
  108.7 3.4 %leaf.1 = (f32[2,32,1024]{2,1,0:T(8,128)}, f32[2,32,32]{2,1,0:T(8,128)}) custom-call(f32[2,32,32]{2,1,0:T(8,128)} %get-tuple-element.26.gram_ref, f32[2,32,1024]{2,1,0:T(8,128)} %get-tuple-element.27.sample_ref), custom_call_target="tpu_custom_call" | custom-call | tf_op jit(solution)/shard_map/leaf/pallas_call | solution.py:312
  114.0 2.9 %transfer.1 = (f32[2,32,32]{2,1,0:T(8,128)}, f32[1,32,32]{2,1,0:T(8,128)}) custom-call(f32[8,8,128]{2,1,0:T(8,128)} %group.1.own_ref, f32[8,8,128]{2,1,0:T(8,128)} %copy-done.2, f32[2,32,32]{2,1,0:T(8,128)} %get-tuple-element.30.upper_ref), custom_call_target="tpu_custom_call" | custom-call | tf_op jit(solution)/shard_map/transfer/pallas_call | solution.py:330
  (44 shorter events, 11.6 us)
Async XLA Ops:
  7.8 23.6 %collective-permute-start = (f32[16,32,512]{2,1,0:T(8,128)S(1)}, f32[16,32,512]{2,1,0:T(8,128)S(1)}, u32[]{:S(2)}, u32[]{:S(2)}) collective-permute-start(f32[16,32,512]{2,1,0:T(8,128)S(1)} %get-tuple-element.19), channel_id=1, source_target_pairs={{0,1},{1,0},{2,3},{3,2},{4,5},{5,4},{6,7},{7,6},{8,9},{9,8},{10,11... | collective-permute-start | bytes 3145736 | tf_op jit(solution)/shard_map/ppermute | solution.py:170
  9.9 25.5 %collective-permute-start.4 = (f32[16,32,512]{2,1,0:T(8,128)S(1)}, f32[16,32,512]{2,1,0:T(8,128)S(1)}, u32[]{:S(2)}, u32[]{:S(2)}) collective-permute-start(f32[16,32,512]{2,1,0:T(8,128)S(1)} %get-tuple-element.21), channel_id=1, source_target_pairs={{0,4},{1,5},{2,6},{3,7},{4,0},{5,1},{6,2},{7,3},{8,12},{9,13},{10,... | collective-permute-start | bytes 3145736 | tf_op jit(solution)/shard_map/ppermute | solution.py:170
  11.6 29.8 %collective-permute-start.9 = (f32[16,32,512]{2,1,0:T(8,128)S(1)}, f32[16,32,512]{2,1,0:T(8,128)S(1)}, u32[]{:S(2)}, u32[]{:S(2)}) collective-permute-start(f32[16,32,512]{2,1,0:T(8,128)S(1)} %get-tuple-element.23), channel_id=1, source_target_pairs={{0,3},{1,2},{2,1},{3,0},{4,7},{5,6},{6,5},{7,4},{8,11},{9,10},{10,... | collective-permute-start | bytes 3145736 | tf_op jit(solution)/shard_map/ppermute | solution.py:170
  13.4 28.3 %collective-permute-start.13 = (f32[16,32,512]{2,1,0:T(8,128)S(1)}, f32[16,32,512]{2,1,0:T(8,128)S(1)}, u32[]{:S(2)}, u32[]{:S(2)}) collective-permute-start(f32[16,32,512]{2,1,0:T(8,128)S(1)} %get-tuple-element.25), channel_id=1, source_target_pairs={{0,28},{1,29},{2,30},{3,31},{4,8},{5,9},{6,10},{7,11},{8,4},{9,5},... | collective-permute-start | bytes 3145736 | tf_op jit(solution)/shard_map/ppermute | solution.py:170
  31.6 16.3 %collective-permute-start.1 = (f32[8,32,512]{2,1,0:T(8,128)S(1)}, f32[8,32,512]{2,1,0:T(8,128)S(1)}, u32[]{:S(2)}, u32[]{:S(2)}) collective-permute-start(f32[8,32,512]{2,1,0:T(8,128)S(1)} %get-tuple-element.40), channel_id=1, source_target_pairs={{0,3},{1,2},{2,1},{3,0},{4,7},{5,6},{6,5},{7,4},{8,11},{9,10},{10,... | collective-permute-start | bytes 1572872 | tf_op jit(solution)/shard_map/ppermute | solution.py:170
  35.6 16.1 %collective-permute-start.5 = (f32[8,32,512]{2,1,0:T(8,128)S(1)}, f32[8,32,512]{2,1,0:T(8,128)S(1)}, u32[]{:S(2)}, u32[]{:S(2)}) collective-permute-start(f32[8,32,512]{2,1,0:T(8,128)S(1)} %get-tuple-element.38), channel_id=1, source_target_pairs={{0,28},{1,29},{2,30},{3,31},{4,8},{5,9},{6,10},{7,11},{8,4},{9,5},... | collective-permute-start | bytes 1572872 | tf_op jit(solution)/shard_map/ppermute | solution.py:170
  41.6 11.4 %collective-permute-start.10 = (f32[8,32,512]{2,1,0:T(8,128)S(1)}, f32[8,32,512]{2,1,0:T(8,128)S(1)}, u32[]{:S(2)}, u32[]{:S(2)}) collective-permute-start(f32[8,32,512]{2,1,0:T(8,128)S(1)} %get-tuple-element.36), channel_id=1, source_target_pairs={{0,1},{1,0},{2,3},{3,2},{4,5},{5,4},{6,7},{7,6},{8,9},{9,8},{10,11... | collective-permute-start | bytes 1572872 | tf_op jit(solution)/shard_map/ppermute | solution.py:170
  42.0 12.9 %collective-permute-start.14 = (f32[8,32,512]{2,1,0:T(8,128)S(1)}, f32[8,32,512]{2,1,0:T(8,128)S(1)}, u32[]{:S(2)}, u32[]{:S(2)}) collective-permute-start(f32[8,32,512]{2,1,0:T(8,128)S(1)} %get-tuple-element.34), channel_id=1, source_target_pairs={{0,4},{1,5},{2,6},{3,7},{4,0},{5,1},{6,2},{7,3},{8,12},{9,13},{10,... | collective-permute-start | bytes 1572872 | tf_op jit(solution)/shard_map/ppermute | solution.py:170
  48.1 10.8 %collective-permute-start.2 = (f32[4,32,512]{2,1,0:T(8,128)S(1)}, f32[4,32,512]{2,1,0:T(8,128)S(1)}, u32[]{:S(2)}, u32[]{:S(2)}) collective-permute-start(f32[4,32,512]{2,1,0:T(8,128)S(1)} %get-tuple-element.48), channel_id=1, source_target_pairs={{0,4},{1,5},{2,6},{3,7},{4,0},{5,1},{6,2},{7,3},{8,12},{9,13},{10,... | collective-permute-start | bytes 786440 | tf_op jit(solution)/shard_map/ppermute | solution.py:170
  51.9 8.7 %collective-permute-start.6 = (f32[4,32,512]{2,1,0:T(8,128)S(1)}, f32[4,32,512]{2,1,0:T(8,128)S(1)}, u32[]{:S(2)}, u32[]{:S(2)}) collective-permute-start(f32[4,32,512]{2,1,0:T(8,128)S(1)} %get-tuple-element.46), channel_id=1, source_target_pairs={{0,1},{1,0},{2,3},{3,2},{4,5},{5,4},{6,7},{7,6},{8,9},{9,8},{10,11... | collective-permute-start | bytes 786440 | tf_op jit(solution)/shard_map/ppermute | solution.py:170
  53.1 7.7 %collective-permute-start.11 = (f32[4,32,512]{2,1,0:T(8,128)S(1)}, f32[4,32,512]{2,1,0:T(8,128)S(1)}, u32[]{:S(2)}, u32[]{:S(2)}) collective-permute-start(f32[4,32,512]{2,1,0:T(8,128)S(1)} %get-tuple-element.44), channel_id=1, source_target_pairs={{0,28},{1,29},{2,30},{3,31},{4,8},{5,9},{6,10},{7,11},{8,4},{9,5},... | collective-permute-start | bytes 786440 | tf_op jit(solution)/shard_map/ppermute | solution.py:170
  55.0 6.8 %collective-permute-start.15 = (f32[4,32,512]{2,1,0:T(8,128)S(1)}, f32[4,32,512]{2,1,0:T(8,128)S(1)}, u32[]{:S(2)}, u32[]{:S(2)}) collective-permute-start(f32[4,32,512]{2,1,0:T(8,128)S(1)} %get-tuple-element.42), channel_id=1, source_target_pairs={{0,3},{1,2},{2,1},{3,0},{4,7},{5,6},{6,5},{7,4},{8,11},{9,10},{10,... | collective-permute-start | bytes 786440 | tf_op jit(solution)/shard_map/ppermute | solution.py:170
  58.9 6.7 %collective-permute-start.3 = (f32[2,32,512]{2,1,0:T(8,128)S(1)}, f32[2,32,512]{2,1,0:T(8,128)S(1)}, u32[]{:S(2)}, u32[]{:S(2)}) collective-permute-start(f32[2,32,512]{2,1,0:T(8,128)S(1)} %get-tuple-element.56), channel_id=1, source_target_pairs={{0,28},{1,29},{2,30},{3,31},{4,8},{5,9},{6,10},{7,11},{8,4},{9,5},... | collective-permute-start | bytes 393224 | tf_op jit(solution)/shard_map/ppermute | solution.py:170
  60.6 6.8 %collective-permute-start.7 = (f32[2,32,512]{2,1,0:T(8,128)S(1)}, f32[2,32,512]{2,1,0:T(8,128)S(1)}, u32[]{:S(2)}, u32[]{:S(2)}) collective-permute-start(f32[2,32,512]{2,1,0:T(8,128)S(1)} %get-tuple-element.54), channel_id=1, source_target_pairs={{0,3},{1,2},{2,1},{3,0},{4,7},{5,6},{6,5},{7,4},{8,11},{9,10},{10,... | collective-permute-start | bytes 393224 | tf_op jit(solution)/shard_map/ppermute | solution.py:170
  60.8 8.9 %collective-permute-start.12 = (f32[2,32,512]{2,1,0:T(8,128)S(1)}, f32[2,32,512]{2,1,0:T(8,128)S(1)}, u32[]{:S(2)}, u32[]{:S(2)}) collective-permute-start(f32[2,32,512]{2,1,0:T(8,128)S(1)} %get-tuple-element.52), channel_id=1, source_target_pairs={{0,4},{1,5},{2,6},{3,7},{4,0},{5,1},{6,2},{7,3},{8,12},{9,13},{10,... | collective-permute-start | bytes 393224 | tf_op jit(solution)/shard_map/ppermute | solution.py:170
  61.8 8.5 %collective-permute-start.16 = (f32[2,32,512]{2,1,0:T(8,128)S(1)}, f32[2,32,512]{2,1,0:T(8,128)S(1)}, u32[]{:S(2)}, u32[]{:S(2)}) collective-permute-start(f32[2,32,512]{2,1,0:T(8,128)S(1)} %get-tuple-element.50), channel_id=1, source_target_pairs={{0,1},{1,0},{2,3},{3,2},{4,5},{5,4},{6,7},{7,6},{8,9},{9,8},{10,11... | collective-permute-start | bytes 393224 | tf_op jit(solution)/shard_map/ppermute | solution.py:170
  68.0 7.2 %collective-permute-start.8 = (f32[1,32,1024]{2,1,0:T(8,128)S(1)}, f32[1,32,1024]{2,1,0:T(8,128)S(1)}, u32[]{:S(2)}, u32[]{:S(2)}) collective-permute-start(f32[1,32,1024]{2,1,0:T(8,128)S(1)} %pad_maximum_fusion), channel_id=1, source_target_pairs={{0,12},{1,13},{2,14},{3,15},{4,24},{5,25},{6,26},{7,27},{8,20},{9,... | collective-permute-start | bytes 393224 | tf_op jit(solution)/shard_map/ppermute | solution.py:170
  71.0 10.6 %collective-permute-start.17 = (f32[1,32,1024]{2,1,0:T(8,128)S(1)}, f32[1,32,1024]{2,1,0:T(8,128)S(1)}, u32[]{:S(2)}, u32[]{:S(2)}) collective-permute-start(f32[1,32,1024]{2,1,0:T(8,128)S(1)} %pad_maximum_fusion.1), channel_id=1, source_target_pairs={{0,20},{1,21},{2,22},{3,23},{4,16},{5,17},{6,18},{7,19},{8,28},{9,... | collective-permute-start | bytes 393224 | tf_op jit(solution)/shard_map/ppermute | solution.py:170
  75.2 6.4 %copy-start = (f32[1,32,1024]{2,1,0:T(8,128)}, f32[1,32,1024]{2,1,0:T(8,128)S(1)}, u32[]{:S(2)}) copy-start(f32[1,32,1024]{2,1,0:T(8,128)S(1)} %collective-permute-done.8) | copy-start | bytes 393220
  81.7 0.7 copy-start.1
  100.1 13.3 %all-to-all-start.1 = ((f32[8,8,128]{2,1,0:T(8,128)}), f32[8,8,128]{2,1,0:T(8,128)S(1)}, u32[]{:S(2)}, u32[]{:S(2)}) async-start(f32[8,8,128]{2,1,0:T(8,128)} %group.1.own_ref), calls=%async_computation.1 | async-start | bytes 65536 | tf_op jit(solution)/shard_map/all_to_all | solution.py:329
  113.4 0.6 copy-start.2

commit v4 on v3

--- a/solution.py
+++ b/solution.py
@@ -9,6 +9,7 @@
 from jax.sharding import PartitionSpec as P
 
 NZ, NX = 8, 4
+NY = 4
 R = 32
 LEAF = 1024
 PARTS = (("x", 0, 512, 0), ("z", 512, 512, 0), ("x", 0, 512, 1), ("z", 512, 512, 1))
@@ -55,18 +56,13 @@
         pltpu.make_async_copy(count_hbm, count_ref, sems.at[1]),
         pltpu.make_async_copy(sketch_hbm, sketch_ref, sems.at[2]),
     ]
-    large = [
-        [
-            pltpu.make_async_copy(
-                hbm.at[pl.ds(g * GROUP, GROUP)],
-                ref.at[pl.ds(g * GROUP, GROUP)],
-                sems.at[3 + 2 * g + k],
-            )
-            for k, (hbm, ref) in enumerate(((v_hbm, v_ref), (u_hbm, u_ref)))
-        ]
+    large = [pltpu.make_async_copy(v_hbm, v_ref, sems.at[3])] + [
+        pltpu.make_async_copy(
+            u_hbm.at[pl.ds(g * GROUP, GROUP)], u_ref.at[pl.ds(g * GROUP, GROUP)], sems.at[4 + g]
+        )
         for g in range(groups)
     ]
-    for copy in small + sum(large, []):
+    for copy in small + large:
         copy.start()
     for ref in outs:
         ref[...] = jnp.zeros_like(ref)
@@ -78,18 +74,18 @@
     sketch_high, sketch_low = halves(sketch_ref[...].reshape(2 * R, LEAF))
     both = jnp.concatenate([sketch_high, sketch_low], axis=0)
     contract = (((1,), (1,)), ((), ()))
+    large[0].wait()
+    v_high, v_low = halves(v_ref[...].reshape(slots * R, LEAF))
+    wide = lax.dot_general(v_high, both, contract, preferred_element_type=jnp.float32)
+    couplings = (
+        wide[:, : 2 * R]
+        + wide[:, 2 * R :]
+        + lax.dot_general(v_low, sketch_high, contract, preferred_element_type=jnp.float32)
+    )
     for g in range(groups):
-        large[g][0].wait()
-        v_high, v_low = halves(v_ref[g * GROUP : (g + 1) * GROUP].reshape(GROUP * R, LEAF))
-        wide = lax.dot_general(v_high, both, contract, preferred_element_type=jnp.float32)
-        couplings = (
-            wide[:, : 2 * R]
-            + wide[:, 2 * R :]
-            + lax.dot_general(v_low, sketch_high, contract, preferred_element_type=jnp.float32)
-        )
-        large[g][1].wait()
+        large[1 + g].wait()
         for t in range(GROUP):
-            part = couplings[t * R : (t + 1) * R]
+            part = couplings[(g * GROUP + t) * R : (g * GROUP + t + 1) * R]
             coupling = jnp.where(g * GROUP + t < first_count, part[:, :R], part[:, R:])
             c_high, c_low = halves(coupling)
             u_high, u_low = halves(u_ref[g * GROUP + t])
@@ -131,6 +127,10 @@
     return [pl.BlockSpec(memory_space=pltpu.VMEM)] * count
 
 
+def pin(*values):
+    return [pltpu.with_memory_space_constraint(value, pltpu.VMEM) for value in values]
+
+
 def contributions(block_row, col_count, u_blocks, v_blocks, sketch):
     slots = u_blocks.shape[0]
     shapes = [
@@ -150,7 +150,7 @@
             pltpu.VMEM((slots, R, LEAF), jnp.float32),
             pltpu.VMEM((2, R, LEAF), jnp.float32),
             pltpu.VMEM((GROUP, R, LEAF), jnp.float32),
-            pltpu.SemaphoreType.DMA((3 + 2 * (slots // GROUP),)),
+            pltpu.SemaphoreType.DMA((4 + slots // GROUP,)),
         ],
         compiler_params=pltpu.CompilerParams(vmem_limit_bytes=24 << 20),
         cost_estimate=pl.CostEstimate(flops=10**9, bytes_accessed=16 << 20, transcendentals=0),
@@ -168,6 +168,15 @@
                 to = z_partner(step, which, z) * NX + x
             pairs.append((z * NX + x, to))
     return lax.ppermute(value, "dev", pairs)
+
+
+def across(value, step):
+    pairs = []
+    for g in range(2 * NY):
+        y, core = g // 2, g % 2
+        to = (g ^ 1, 2 * (y ^ 1) + core, 2 * (y ^ 3) + core)[step]
+        pairs.append((g, to))
+    return lax.ppermute(value, "grp", pairs)
 
 
 def scatter_sums(parts):
@@ -263,13 +272,12 @@
 
 
 def group_kernel(every_ref, packed_ref):
-    packed_ref[...] = jnp.broadcast_to(jnp.sum(every_ref[...], axis=0)[None], packed_ref.shape)
-
-
-def transfer_kernel(leaves, own_ref, every_ref, upper_ref, leaf_ref, group_ref):
-    groups = every_ref.shape[0]
-    group_gram = unpack(own_ref[0])
-    root_gram = unpack(jnp.sum(every_ref[...], axis=0))
+    packed_ref[...] = jnp.sum(every_ref[...], axis=0)
+
+
+def transfer_kernel(leaves, groups, own_ref, near_ref, far_ref, upper_ref, leaf_ref, group_ref):
+    group_gram = unpack(own_ref[...])
+    root_gram = unpack(near_ref[...] + far_ref[...])
     (group_upper, group_inverse), (_, root_inverse) = eliminate([group_gram, root_gram])
     rows = lax.broadcasted_iota(jnp.int32, (R, R), 0)
     cols = lax.broadcasted_iota(jnp.int32, (R, R), 1)
@@ -300,42 +308,45 @@
     sample, gram, packed = pl.pallas_call(
         sample_kernel,
         out_shape=(
-            jax.ShapeDtypeStruct((2, R, LEAF), jnp.float32),
-            jax.ShapeDtypeStruct((2, R, R), jnp.float32),
+            pltpu.VMEM((2, R, LEAF), jnp.float32),
+            pltpu.VMEM((2, R, R), jnp.float32),
             jax.ShapeDtypeStruct((members, 8, 128), jnp.float32),
         ),
         in_specs=in_vmem(len(terms) + 2),
         out_specs=in_vmem(3),
         name="sample",
-    )(*terms, near_diag, sketch)
+    )(*pin(*terms), near_diag, sketch)
     every = lax.all_to_all(packed, "dev", split_axis=0, concat_axis=0, tiled=True)
     leaf_basis, upper = pl.pallas_call(
         leaf_kernel,
         out_shape=(
             jax.ShapeDtypeStruct((2, R, LEAF), jnp.float32),
-            jax.ShapeDtypeStruct((2, R, R), jnp.float32),
+            pltpu.VMEM((2, R, R), jnp.float32),
         ),
         in_specs=in_vmem(2),
         out_specs=[pl.BlockSpec((2, R, LEAF), lambda: (0, 0, 0))] + in_vmem(1),
         name="leaf",
-    )(gram, sample)
+    )(*pin(gram, sample))
     own_gram = pl.pallas_call(
         group_kernel,
-        out_shape=jax.ShapeDtypeStruct((groups, 8, 128), jnp.float32),
+        out_shape=pltpu.VMEM((8, 128), jnp.float32),
         in_specs=in_vmem(1),
         out_specs=pl.BlockSpec(memory_space=pltpu.VMEM),
         name="group",
-    )(every)
-    every_group = lax.all_to_all(own_gram, "grp", split_axis=0, concat_axis=0, tiled=True)
+    )(*pin(every))
+    total, got = own_gram, across(own_gram, 0)
+    for step in range(1, 3):
+        total = total + got
+        got = across(total, step)
     transfer_leaf, transfer_group = pl.pallas_call(
-        functools.partial(transfer_kernel, 2 * members),
+        functools.partial(transfer_kernel, 2 * members, groups),
         out_shape=(
             jax.ShapeDtypeStruct((2, R, R), jnp.float32),
             jax.ShapeDtypeStruct((1, R, R), jnp.float32),
         ),
-        in_specs=in_vmem(3),
+        in_specs=in_vmem(4),
         name="transfer",
-    )(own_gram, every_group, upper)
+    )(*pin(own_gram, total, got, upper))
     return (leaf_basis, transfer_leaf, transfer_group)
 
 

time: 117 us -> 112 us (0.957)
  Pallas kernels: 17.4 us -> 13.5 us
  starting transfers between devices: 38.2 us -> 40.7 us
  other arithmetic: 3.9 us -> 1.41 us
  local copies, waits for them, and re-layouts: 1.25 us -> 0 us
    ppermute x0 -> x3, starting transfers between devices: none -> 11.6 us  [across(): return lax.ppermute(value, 'grp', pairs)]
    all_to_all x1 -> x0, starting transfers between devices: 8.56 us -> none  [body(): lax.all_to_all(own_gram, 'grp', split_axis=0, concat_axis=0, tiled=True)]
    pallas_call x3, Pallas kernels: 6.81 us -> 4.23 us  [the longest x1 2.12 us: body(): pl.pallas_call(functools.partial(transfer_kernel, 2 * members, groups), o...]
    add x4, other arithmetic: 2.58 us -> 0.08 us  [scatter_sums(): send = keep[half:] + got[half:]]
    ppermute x0 -> x3, waiting for transfers between devices: none -> 1.82 us  [across(): return lax.ppermute(value, 'grp', pairs)]
    all_to_all x1 -> x0, waiting for transfers between devices: 1.3 us -> none  [body(): lax.all_to_all(own_gram, 'grp', split_axis=0, concat_axis=0, tiled=True)]
    unnamed x6 -> x0, local copies, waits for them, and re-layouts: 1.25 us -> none
    ppermute x18, waiting for transfers between devices: 40.3 us -> 39 us  [exchange(): return lax.ppermute(value, 'dev', pairs)]
  transfers between devices with their start and end apart: 19 -> 21, of which waited for: 11 -> 11; matrix products, arithmetic and copies ran while one was open for 3% -> 1% of each run, Pallas kernels for 3% -> 2%
where the time goes in v4:
time: 112 us
  waiting for transfers between devices  40.8 us (36%)
  starting transfers between devices  40.7 us (36%)
  blocking collectives  14.7 us (13%)
  Pallas kernels  13.5 us (12%)
  other arithmetic  1.41 us (1%)
    ppermute x18, waiting for transfers between devices, exchange(): return lax.ppermute(value, 'dev', pairs)  39 us
    ppermute x18, starting transfers between devices, exchange(): return lax.ppermute(value, 'dev', pairs)  29 us
    all_to_all x1, blocking collectives, body(): lax.all_to_all(packed, 'dev', split_axis=0, concat_axis=0, tiled=True)  14.7 us
    ppermute x3, starting transfers between devices, across(): return lax.ppermute(value, 'grp', pairs)  11.6 us
    pallas_call x1, Pallas kernels, contributions(): pl.pallas_call(contribution_kernel, out_shape=shapes, in_specs=[pl.BlockS...  6.81 us
    pallas_call x1, Pallas kernels, body(): pl.pallas_call(leaf_kernel, out_shape=(jax.ShapeDtypeStruct((2, R, LEAF),...  2.45 us
  transfers between devices with their start and end apart: 21, of which 11 were waited for; matrix products, arithmetic and copies ran while one was open for 1% of the time, Pallas kernels for 2%

profile of v4, /device:TPU:1, one launch (start us, length us, event | category | flops | bytes accessed | tf_op | source)
XLA Modules:
  0.0 111.9 jit_solution(10827770451739748520)
XLA Ops:
  0.6 6.8 %contributions.1 = (f32[16,32,512]{2,1,0:T(8,128)S(1)}, f32[16,32,512]{2,1,0:T(8,128)S(1)}, f32[16,32,512]{2,1,0:T(8,128)S(1)}, f32[16,32,512]{2,1,0:T(8,128)S(1...) custom-call(s32[24]{0:T(128)} %rows_hbm.1, ...), custom_call_target="tpu_custom_call" | custom-call | flops 1000000000 | bytes 16777216 | tf_op jit(solution)/shard_map/contributions/pallas_call | solution.py:141
  7.4 2.1 %collective-permute-start = (f32[16,32,512]{2,1,0:T(8,128)S(1)}, f32[16,32,512]{2,1,0:T(8,128)S(1)}, u32[]{:S(2)}, u32[]{:S(2)}) collective-permute-start(f32[16,32,512]{2,1,0:T(8,128)S(1)} %get-tuple-element.19), channel_id=1, source_target_pairs={{0,1},{1,0},{2,3},{3,2},{4,5},{5,4},{6,7},{7,6},{8,9},{9,8},{10,11... | collective-permute-start | bytes 3145736 | tf_op jit(solution)/shard_map/ppermute | solution.py:170
  9.6 1.6 %collective-permute-start.4 = (f32[16,32,512]{2,1,0:T(8,128)S(1)}, f32[16,32,512]{2,1,0:T(8,128)S(1)}, u32[]{:S(2)}, u32[]{:S(2)}) collective-permute-start(f32[16,32,512]{2,1,0:T(8,128)S(1)} %get-tuple-element.21), channel_id=1, source_target_pairs={{0,4},{1,5},{2,6},{3,7},{4,0},{5,1},{6,2},{7,3},{8,12},{9,13},{10,... | collective-permute-start | bytes 3145736 | tf_op jit(solution)/shard_map/ppermute | solution.py:170
  11.2 1.8 %collective-permute-start.9 = (f32[16,32,512]{2,1,0:T(8,128)S(1)}, f32[16,32,512]{2,1,0:T(8,128)S(1)}, u32[]{:S(2)}, u32[]{:S(2)}) collective-permute-start(f32[16,32,512]{2,1,0:T(8,128)S(1)} %get-tuple-element.23), channel_id=1, source_target_pairs={{0,3},{1,2},{2,1},{3,0},{4,7},{5,6},{6,5},{7,4},{8,11},{9,10},{10,... | collective-permute-start | bytes 3145736 | tf_op jit(solution)/shard_map/ppermute | solution.py:170
  13.0 4.7 %collective-permute-start.13 = (f32[16,32,512]{2,1,0:T(8,128)S(1)}, f32[16,32,512]{2,1,0:T(8,128)S(1)}, u32[]{:S(2)}, u32[]{:S(2)}) collective-permute-start(f32[16,32,512]{2,1,0:T(8,128)S(1)} %get-tuple-element.25), channel_id=1, source_target_pairs={{0,28},{1,29},{2,30},{3,31},{4,8},{5,9},{6,10},{7,11},{8,4},{9,5},... | collective-permute-start | bytes 3145736 | tf_op jit(solution)/shard_map/ppermute | solution.py:170
  17.7 13.4 %collective-permute-done = f32[16,32,512]{2,1,0:T(8,128)S(1)} collective-permute-done((f32[16,32,512]{2,1,0:T(8,128)S(1)}, f32[16,32,512]{2,1,0:T(8,128)S(1)}, u32[]{:S(2)}, u32[]{:S(2)}) %collective-permute-start) | collective-permute-done | bytes 1048608 | tf_op jit(solution)/shard_map/ppermute | solution.py:170
  31.3 3.9 %collective-permute-start.1 = (f32[8,32,512]{2,1,0:T(8,128)S(1)}, f32[8,32,512]{2,1,0:T(8,128)S(1)}, u32[]{:S(2)}, u32[]{:S(2)}) collective-permute-start(f32[8,32,512]{2,1,0:T(8,128)S(1)} %get-tuple-element.40), channel_id=1, source_target_pairs={{0,3},{1,2},{2,1},{3,0},{4,7},{5,6},{6,5},{7,4},{8,11},{9,10},{10,... | collective-permute-start | bytes 1572872 | tf_op jit(solution)/shard_map/ppermute | solution.py:170
  35.4 5.6 %collective-permute-start.5 = (f32[8,32,512]{2,1,0:T(8,128)S(1)}, f32[8,32,512]{2,1,0:T(8,128)S(1)}, u32[]{:S(2)}, u32[]{:S(2)}) collective-permute-start(f32[8,32,512]{2,1,0:T(8,128)S(1)} %get-tuple-element.38), channel_id=1, source_target_pairs={{0,28},{1,29},{2,30},{3,31},{4,8},{5,9},{6,10},{7,11},{8,4},{9,5},... | collective-permute-start | bytes 1572872 | tf_op jit(solution)/shard_map/ppermute | solution.py:170
  41.6 6.1 %collective-permute-done.1 = f32[8,32,512]{2,1,0:T(8,128)S(1)} collective-permute-done((f32[8,32,512]{2,1,0:T(8,128)S(1)}, f32[8,32,512]{2,1,0:T(8,128)S(1)}, u32[]{:S(2)}, u32[]{:S(2)}) %collective-permute-start.1) | collective-permute-done | bytes 524320 | tf_op jit(solution)/shard_map/ppermute | solution.py:170
  47.9 3.5 %collective-permute-done.5 = f32[8,32,512]{2,1,0:T(8,128)S(1)} collective-permute-done((f32[8,32,512]{2,1,0:T(8,128)S(1)}, f32[8,32,512]{2,1,0:T(8,128)S(1)}, u32[]{:S(2)}, u32[]{:S(2)}) %collective-permute-start.5) | collective-permute-done | bytes 524320 | tf_op jit(solution)/shard_map/ppermute | solution.py:170
  52.7 1.7 %collective-permute-start.11 = (f32[4,32,512]{2,1,0:T(8,128)S(1)}, f32[4,32,512]{2,1,0:T(8,128)S(1)}, u32[]{:S(2)}, u32[]{:S(2)}) collective-permute-start(f32[4,32,512]{2,1,0:T(8,128)S(1)} %get-tuple-element.44), channel_id=1, source_target_pairs={{0,28},{1,29},{2,30},{3,31},{4,8},{5,9},{6,10},{7,11},{8,4},{9,5},... | collective-permute-start | bytes 786440 | tf_op jit(solution)/shard_map/ppermute | solution.py:170
  55.4 2.9 %collective-permute-done.2 = f32[4,32,512]{2,1,0:T(8,128)S(1)} collective-permute-done((f32[4,32,512]{2,1,0:T(8,128)S(1)}, f32[4,32,512]{2,1,0:T(8,128)S(1)}, u32[]{:S(2)}, u32[]{:S(2)}) %collective-permute-start.2) | collective-permute-done | bytes 262176 | tf_op jit(solution)/shard_map/ppermute | solution.py:170
  58.4 1.9 %collective-permute-start.3 = (f32[2,32,512]{2,1,0:T(8,128)S(1)}, f32[2,32,512]{2,1,0:T(8,128)S(1)}, u32[]{:S(2)}, u32[]{:S(2)}) collective-permute-start(f32[2,32,512]{2,1,0:T(8,128)S(1)} %get-tuple-element.56), channel_id=1, source_target_pairs={{0,28},{1,29},{2,30},{3,31},{4,8},{5,9},{6,10},{7,11},{8,4},{9,5},... | collective-permute-start | bytes 393224 | tf_op jit(solution)/shard_map/ppermute | solution.py:170
  61.7 3.5 %collective-permute-done.3 = f32[2,32,512]{2,1,0:T(8,128)S(1)} collective-permute-done((f32[2,32,512]{2,1,0:T(8,128)S(1)}, f32[2,32,512]{2,1,0:T(8,128)S(1)}, u32[]{:S(2)}, u32[]{:S(2)}) %collective-permute-start.3) | collective-permute-done | bytes 131104 | tf_op jit(solution)/shard_map/ppermute | solution.py:170
  65.2 1.9 %collective-permute-done.7 = f32[2,32,512]{2,1,0:T(8,128)S(1)} collective-permute-done((f32[2,32,512]{2,1,0:T(8,128)S(1)}, f32[2,32,512]{2,1,0:T(8,128)S(1)}, u32[]{:S(2)}, u32[]{:S(2)}) %collective-permute-start.7) | collective-permute-done | bytes 131104 | tf_op jit(solution)/shard_map/ppermute | solution.py:170
  70.3 4.3 %collective-permute-done.8 = f32[1,32,1024]{2,1,0:T(8,128)S(1)} collective-permute-done((f32[1,32,1024]{2,1,0:T(8,128)S(1)}, f32[1,32,1024]{2,1,0:T(8,128)S(1)}, u32[]{:S(2)}, u32[]{:S(2)}) %collective-permute-start.8) | collective-permute-done | bytes 131104 | tf_op jit(solution)/shard_map/ppermute | solution.py:170
  74.6 2.4 %collective-permute-done.17 = f32[1,32,1024]{2,1,0:T(8,128)S(1)} collective-permute-done((f32[1,32,1024]{2,1,0:T(8,128)S(1)}, f32[1,32,1024]{2,1,0:T(8,128)S(1)}, u32[]{:S(2)}, u32[]{:S(2)}) %collective-permute-start.17) | collective-permute-done | bytes 131104 | tf_op jit(solution)/shard_map/ppermute | solution.py:170
  77.0 2.1 %sample.1 = (f32[2,32,1024]{2,1,0:T(8,128)S(1)}, f32[2,32,32]{2,1,0:T(8,128)S(1)}, f32[32,8,128]{2,1,0:T(8,128)}) custom-call(f32[32,512]{1,0:T(8,128)S(1)} %get-tuple-element.62.refs_0_, f32[32,512]{1,0:T(8,128)S(1)} %get-tuple-element.64.refs_1_, f32[32,1024]{1,0:T(8,128)S(1)} %bitcast.10, f32[32,512]{1,0:T(8,128)S(1)} %get-tuple-element.58.refs_3_, ...), custom_call_target="tpu_custom_call" | custom-call | tf_op jit(solution)/shard_map/sample/pallas_call | solution.py:308
  79.1 14.7 %all_to_all.5.every_ref = f32[32,8,128]{2,1,0:T(8,128)S(1)} all-to-all(f32[32,8,128]{2,1,0:T(8,128)} %get-tuple-element.29), channel_id=1, replica_groups=mesh['grp'=8,'dev'=32] {'dev'}, dimensions={0} | all-to-all | bytes 262144 | tf_op jit(solution)/shard_map/all_to_all | solution.py:319
  93.8 7.4 %collective-permute-start.18 = (f32[8,128]{1,0:T(8,128)S(1)}, f32[8,128]{1,0:T(8,128)S(1)}, u32[]{:S(2)}, u32[]{:S(2)}) collective-permute-start(f32[8,128]{1,0:T(8,128)S(1)} %group.1.own_ref), channel_id=1, source_target_pairs={{0,32},{32,0},{64,96},{96,64},{128,160},{160,128},{192,224},{224,1... | collective-permute-start | bytes 12296 | tf_op jit(solution)/shard_map/ppermute | solution.py:179
  102.1 2.6 %collective-permute-start.19 = (f32[8,128]{1,0:T(8,128)S(1)}, f32[8,128]{1,0:T(8,128)S(1)}, u32[]{:S(2)}, u32[]{:S(2)}) collective-permute-start(f32[8,128]{1,0:T(8,128)S(1)} %add.134), channel_id=1, source_target_pairs={{0,64},{32,96},{64,0},{96,32},{128,192},{160,224},{192,128},{224,1... | collective-permute-start | bytes 12296 | tf_op jit(solution)/shard_map/ppermute | solution.py:179
  105.7 1.6 %collective-permute-start.20 = (f32[8,128]{1,0:T(8,128)S(1)}, f32[8,128]{1,0:T(8,128)S(1)}, u32[]{:S(2)}, u32[]{:S(2)}) collective-permute-start(f32[8,128]{1,0:T(8,128)S(1)} %add.135.near_ref), channel_id=1, source_target_pairs={{0,192},{32,224},{64,128},{96,160},{128,64},{160,96},{192,0},{224,... | collective-permute-start | bytes 12296 | tf_op jit(solution)/shard_map/ppermute | solution.py:179
  107.3 2.5 %leaf.1 = (f32[2,32,1024]{2,1,0:T(8,128)}, f32[2,32,32]{2,1,0:T(8,128)S(1)}) custom-call(f32[2,32,32]{2,1,0:T(8,128)S(1)} %get-tuple-element.26.gram_ref, f32[2,32,1024]{2,1,0:T(8,128)S(1)} %get-tuple-element.27.sample_ref), custom_call_target="tpu_custom_call" | custom-call | tf_op jit(solution)/shard_map/leaf/pallas_call | solution.py:320
  109.7 2.1 %transfer.1 = (f32[2,32,32]{2,1,0:T(8,128)}, f32[1,32,32]{2,1,0:T(8,128)}) custom-call(f32[8,128]{1,0:T(8,128)S(1)} %group.1.own_ref, f32[8,128]{1,0:T(8,128)S(1)} %add.135.near_ref, f32[8,128]{1,0:T(8,128)S(1)} %collective-permute-done.20.far_ref, f32[2,32,32]{2,1,0:T(8,128)S(1)} %get-tuple-element.30.upper_ref), custom_call_target="tpu_custom_call" | custom-call | tf_op jit(solution)/shard_map/transfer/pallas_call | solution.py:341
  (44 shorter events, 10.1 us)
Async XLA Ops:
  7.4 23.6 %collective-permute-start = (f32[16,32,512]{2,1,0:T(8,128)S(1)}, f32[16,32,512]{2,1,0:T(8,128)S(1)}, u32[]{:S(2)}, u32[]{:S(2)}) collective-permute-start(f32[16,32,512]{2,1,0:T(8,128)S(1)} %get-tuple-element.19), channel_id=1, source_target_pairs={{0,1},{1,0},{2,3},{3,2},{4,5},{5,4},{6,7},{7,6},{8,9},{9,8},{10,11... | collective-permute-start | bytes 3145736 | tf_op jit(solution)/shard_map/ppermute | solution.py:170
  9.6 25.6 %collective-permute-start.4 = (f32[16,32,512]{2,1,0:T(8,128)S(1)}, f32[16,32,512]{2,1,0:T(8,128)S(1)}, u32[]{:S(2)}, u32[]{:S(2)}) collective-permute-start(f32[16,32,512]{2,1,0:T(8,128)S(1)} %get-tuple-element.21), channel_id=1, source_target_pairs={{0,4},{1,5},{2,6},{3,7},{4,0},{5,1},{6,2},{7,3},{8,12},{9,13},{10,... | collective-permute-start | bytes 3145736 | tf_op jit(solution)/shard_map/ppermute | solution.py:170
  11.2 29.8 %collective-permute-start.9 = (f32[16,32,512]{2,1,0:T(8,128)S(1)}, f32[16,32,512]{2,1,0:T(8,128)S(1)}, u32[]{:S(2)}, u32[]{:S(2)}) collective-permute-start(f32[16,32,512]{2,1,0:T(8,128)S(1)} %get-tuple-element.23), channel_id=1, source_target_pairs={{0,3},{1,2},{2,1},{3,0},{4,7},{5,6},{6,5},{7,4},{8,11},{9,10},{10,... | collective-permute-start | bytes 3145736 | tf_op jit(solution)/shard_map/ppermute | solution.py:170
  13.0 28.3 %collective-permute-start.13 = (f32[16,32,512]{2,1,0:T(8,128)S(1)}, f32[16,32,512]{2,1,0:T(8,128)S(1)}, u32[]{:S(2)}, u32[]{:S(2)}) collective-permute-start(f32[16,32,512]{2,1,0:T(8,128)S(1)} %get-tuple-element.25), channel_id=1, source_target_pairs={{0,28},{1,29},{2,30},{3,31},{4,8},{5,9},{6,10},{7,11},{8,4},{9,5},... | collective-permute-start | bytes 3145736 | tf_op jit(solution)/shard_map/ppermute | solution.py:170
  31.3 16.4 %collective-permute-start.1 = (f32[8,32,512]{2,1,0:T(8,128)S(1)}, f32[8,32,512]{2,1,0:T(8,128)S(1)}, u32[]{:S(2)}, u32[]{:S(2)}) collective-permute-start(f32[8,32,512]{2,1,0:T(8,128)S(1)} %get-tuple-element.40), channel_id=1, source_target_pairs={{0,3},{1,2},{2,1},{3,0},{4,7},{5,6},{6,5},{7,4},{8,11},{9,10},{10,... | collective-permute-start | bytes 1572872 | tf_op jit(solution)/shard_map/ppermute | solution.py:170
  35.4 16.0 %collective-permute-start.5 = (f32[8,32,512]{2,1,0:T(8,128)S(1)}, f32[8,32,512]{2,1,0:T(8,128)S(1)}, u32[]{:S(2)}, u32[]{:S(2)}) collective-permute-start(f32[8,32,512]{2,1,0:T(8,128)S(1)} %get-tuple-element.38), channel_id=1, source_target_pairs={{0,28},{1,29},{2,30},{3,31},{4,8},{5,9},{6,10},{7,11},{8,4},{9,5},... | collective-permute-start | bytes 1572872 | tf_op jit(solution)/shard_map/ppermute | solution.py:170
  41.2 11.4 %collective-permute-start.10 = (f32[8,32,512]{2,1,0:T(8,128)S(1)}, f32[8,32,512]{2,1,0:T(8,128)S(1)}, u32[]{:S(2)}, u32[]{:S(2)}) collective-permute-start(f32[8,32,512]{2,1,0:T(8,128)S(1)} %get-tuple-element.36), channel_id=1, source_target_pairs={{0,1},{1,0},{2,3},{3,2},{4,5},{5,4},{6,7},{7,6},{8,9},{9,8},{10,11... | collective-permute-start | bytes 1572872 | tf_op jit(solution)/shard_map/ppermute | solution.py:170
  41.5 12.8 %collective-permute-start.14 = (f32[8,32,512]{2,1,0:T(8,128)S(1)}, f32[8,32,512]{2,1,0:T(8,128)S(1)}, u32[]{:S(2)}, u32[]{:S(2)}) collective-permute-start(f32[8,32,512]{2,1,0:T(8,128)S(1)} %get-tuple-element.34), channel_id=1, source_target_pairs={{0,4},{1,5},{2,6},{3,7},{4,0},{5,1},{6,2},{7,3},{8,12},{9,13},{10,... | collective-permute-start | bytes 1572872 | tf_op jit(solution)/shard_map/ppermute | solution.py:170
  47.8 10.5 %collective-permute-start.2 = (f32[4,32,512]{2,1,0:T(8,128)S(1)}, f32[4,32,512]{2,1,0:T(8,128)S(1)}, u32[]{:S(2)}, u32[]{:S(2)}) collective-permute-start(f32[4,32,512]{2,1,0:T(8,128)S(1)} %get-tuple-element.48), channel_id=1, source_target_pairs={{0,4},{1,5},{2,6},{3,7},{4,0},{5,1},{6,2},{7,3},{8,12},{9,13},{10,... | collective-permute-start | bytes 786440 | tf_op jit(solution)/shard_map/ppermute | solution.py:170
  51.5 8.8 %collective-permute-start.6 = (f32[4,32,512]{2,1,0:T(8,128)S(1)}, f32[4,32,512]{2,1,0:T(8,128)S(1)}, u32[]{:S(2)}, u32[]{:S(2)}) collective-permute-start(f32[4,32,512]{2,1,0:T(8,128)S(1)} %get-tuple-element.46), channel_id=1, source_target_pairs={{0,1},{1,0},{2,3},{3,2},{4,5},{5,4},{6,7},{7,6},{8,9},{9,8},{10,11... | collective-permute-start | bytes 786440 | tf_op jit(solution)/shard_map/ppermute | solution.py:170
  52.7 7.9 %collective-permute-start.11 = (f32[4,32,512]{2,1,0:T(8,128)S(1)}, f32[4,32,512]{2,1,0:T(8,128)S(1)}, u32[]{:S(2)}, u32[]{:S(2)}) collective-permute-start(f32[4,32,512]{2,1,0:T(8,128)S(1)} %get-tuple-element.44), channel_id=1, source_target_pairs={{0,28},{1,29},{2,30},{3,31},{4,8},{5,9},{6,10},{7,11},{8,4},{9,5},... | collective-permute-start | bytes 786440 | tf_op jit(solution)/shard_map/ppermute | solution.py:170
  54.4 6.8 %collective-permute-start.15 = (f32[4,32,512]{2,1,0:T(8,128)S(1)}, f32[4,32,512]{2,1,0:T(8,128)S(1)}, u32[]{:S(2)}, u32[]{:S(2)}) collective-permute-start(f32[4,32,512]{2,1,0:T(8,128)S(1)} %get-tuple-element.42), channel_id=1, source_target_pairs={{0,3},{1,2},{2,1},{3,0},{4,7},{5,6},{6,5},{7,4},{8,11},{9,10},{10,... | collective-permute-start | bytes 786440 | tf_op jit(solution)/shard_map/ppermute | solution.py:170
  58.4 6.8 %collective-permute-start.3 = (f32[2,32,512]{2,1,0:T(8,128)S(1)}, f32[2,32,512]{2,1,0:T(8,128)S(1)}, u32[]{:S(2)}, u32[]{:S(2)}) collective-permute-start(f32[2,32,512]{2,1,0:T(8,128)S(1)} %get-tuple-element.56), channel_id=1, source_target_pairs={{0,28},{1,29},{2,30},{3,31},{4,8},{5,9},{6,10},{7,11},{8,4},{9,5},... | collective-permute-start | bytes 393224 | tf_op jit(solution)/shard_map/ppermute | solution.py:170
  60.3 6.8 %collective-permute-start.7 = (f32[2,32,512]{2,1,0:T(8,128)S(1)}, f32[2,32,512]{2,1,0:T(8,128)S(1)}, u32[]{:S(2)}, u32[]{:S(2)}) collective-permute-start(f32[2,32,512]{2,1,0:T(8,128)S(1)} %get-tuple-element.54), channel_id=1, source_target_pairs={{0,3},{1,2},{2,1},{3,0},{4,7},{5,6},{6,5},{7,4},{8,11},{9,10},{10,... | collective-permute-start | bytes 393224 | tf_op jit(solution)/shard_map/ppermute | solution.py:170
  60.6 8.1 %collective-permute-start.12 = (f32[2,32,512]{2,1,0:T(8,128)S(1)}, f32[2,32,512]{2,1,0:T(8,128)S(1)}, u32[]{:S(2)}, u32[]{:S(2)}) collective-permute-start(f32[2,32,512]{2,1,0:T(8,128)S(1)} %get-tuple-element.52), channel_id=1, source_target_pairs={{0,4},{1,5},{2,6},{3,7},{4,0},{5,1},{6,2},{7,3},{8,12},{9,13},{10,... | collective-permute-start | bytes 393224 | tf_op jit(solution)/shard_map/ppermute | solution.py:170
  61.2 7.5 %collective-permute-start.16 = (f32[2,32,512]{2,1,0:T(8,128)S(1)}, f32[2,32,512]{2,1,0:T(8,128)S(1)}, u32[]{:S(2)}, u32[]{:S(2)}) collective-permute-start(f32[2,32,512]{2,1,0:T(8,128)S(1)} %get-tuple-element.50), channel_id=1, source_target_pairs={{0,1},{1,0},{2,3},{3,2},{4,5},{5,4},{6,7},{7,6},{8,9},{9,8},{10,11... | collective-permute-start | bytes 393224 | tf_op jit(solution)/shard_map/ppermute | solution.py:170
  67.1 7.5 %collective-permute-start.8 = (f32[1,32,1024]{2,1,0:T(8,128)S(1)}, f32[1,32,1024]{2,1,0:T(8,128)S(1)}, u32[]{:S(2)}, u32[]{:S(2)}) collective-permute-start(f32[1,32,1024]{2,1,0:T(8,128)S(1)} %pad_maximum_fusion), channel_id=1, source_target_pairs={{0,12},{1,13},{2,14},{3,15},{4,24},{5,25},{6,26},{7,27},{8,20},{9,... | collective-permute-start | bytes 393224 | tf_op jit(solution)/shard_map/ppermute | solution.py:170
  68.8 8.3 %collective-permute-start.17 = (f32[1,32,1024]{2,1,0:T(8,128)S(1)}, f32[1,32,1024]{2,1,0:T(8,128)S(1)}, u32[]{:S(2)}, u32[]{:S(2)}) collective-permute-start(f32[1,32,1024]{2,1,0:T(8,128)S(1)} %pad_maximum_fusion.1), channel_id=1, source_target_pairs={{0,20},{1,21},{2,22},{3,23},{4,16},{5,17},{6,18},{7,19},{8,28},{9,... | collective-permute-start | bytes 393224 | tf_op jit(solution)/shard_map/ppermute | solution.py:170
  93.8 8.3 %collective-permute-start.18 = (f32[8,128]{1,0:T(8,128)S(1)}, f32[8,128]{1,0:T(8,128)S(1)}, u32[]{:S(2)}, u32[]{:S(2)}) collective-permute-start(f32[8,128]{1,0:T(8,128)S(1)} %group.1.own_ref), channel_id=1, source_target_pairs={{0,32},{32,0},{64,96},{96,64},{128,160},{160,128},{192,224},{224,1... | collective-permute-start | bytes 12296 | tf_op jit(solution)/shard_map/ppermute | solution.py:179
  102.1 3.6 %collective-permute-start.19 = (f32[8,128]{1,0:T(8,128)S(1)}, f32[8,128]{1,0:T(8,128)S(1)}, u32[]{:S(2)}, u32[]{:S(2)}) collective-permute-start(f32[8,128]{1,0:T(8,128)S(1)} %add.134), channel_id=1, source_target_pairs={{0,64},{32,96},{64,0},{96,32},{128,192},{160,224},{192,128},{224,1... | collective-permute-start | bytes 12296 | tf_op jit(solution)/shard_map/ppermute | solution.py:179
  105.7 4.1 %collective-permute-start.20 = (f32[8,128]{1,0:T(8,128)S(1)}, f32[8,128]{1,0:T(8,128)S(1)}, u32[]{:S(2)}, u32[]{:S(2)}) collective-permute-start(f32[8,128]{1,0:T(8,128)S(1)} %add.135.near_ref), channel_id=1, source_target_pairs={{0,192},{32,224},{64,128},{96,160},{128,64},{160,96},{192,0},{224,... | collective-permute-start | bytes 12296 | tf_op jit(solution)/shard_map/ppermute | solution.py:179

commit v5 on v4

--- a/solution.py
+++ b/solution.py
@@ -17,8 +17,8 @@
     "x": (("x", 0), ("x", 1), ("z", 0), ("z", 1)),
     "z": (("z", 0), ("z", 1), ("x", 0), ("x", 1)),
 }
-BLOCK = 4
-GROUP = 4
+BLOCK = 8
+GROUP = 24
 HIGHEST = lax.Precision.HIGHEST
 X_ORDER, Z_ORDER = (0, 2, 3, 1), (0, 4, 6, 1, 3, 7, 5, 2)
 
@@ -260,9 +260,7 @@
 def leaf_kernel(gram_ref, sample_ref, basis_ref, upper_ref):
     factors = eliminate([gram_ref[0], gram_ref[1]])
     for i, (upper, inverse) in enumerate(factors):
-        rows = lax.broadcasted_iota(jnp.int32, (R, R), 0)
-        cols = lax.broadcasted_iota(jnp.int32, (R, R), 1)
-        upper_ref[i] = jnp.where(rows <= cols, upper, 0.0)
+        upper_ref[i] = upper_part(upper)
         basis_ref[i] = jnp.dot(
             inverse * math.sqrt(LEAF),
             sample_ref[i],
@@ -275,29 +273,32 @@
     packed_ref[...] = jnp.sum(every_ref[...], axis=0)
 
 
-def transfer_kernel(leaves, groups, own_ref, near_ref, far_ref, upper_ref, leaf_ref, group_ref):
-    group_gram = unpack(own_ref[...])
-    root_gram = unpack(near_ref[...] + far_ref[...])
-    (group_upper, group_inverse), (_, root_inverse) = eliminate([group_gram, root_gram])
+def upper_part(square):
     rows = lax.broadcasted_iota(jnp.int32, (R, R), 0)
     cols = lax.broadcasted_iota(jnp.int32, (R, R), 1)
-    group_upper = jnp.where(rows <= cols, group_upper, 0.0)
-    contract = (((1,), (1,)), ((), ()))
-    for i in range(2):
-        leaf_ref[i] = lax.dot_general(
-            upper_ref[i],
-            group_inverse * math.sqrt(leaves),
-            contract,
-            precision=HIGHEST,
-            preferred_element_type=jnp.float32,
-        )
-    group_ref[0] = lax.dot_general(
-        group_upper,
-        root_inverse * math.sqrt(groups),
-        contract,
+    return jnp.where(rows <= cols, square, 0.0)
+
+
+def right_solve(upper, inverse):
+    return lax.dot_general(
+        upper,
+        inverse,
+        (((1,), (1,)), ((), ())),
         precision=HIGHEST,
         preferred_element_type=jnp.float32,
     )
+
+
+def transfer_leaf_kernel(leaves, own_ref, upper_ref, leaf_ref, group_ref):
+    ((group_upper, group_inverse),) = eliminate([unpack(own_ref[...])])
+    for i in range(2):
+        leaf_ref[i] = right_solve(upper_ref[i], group_inverse * math.sqrt(leaves))
+    group_ref[...] = upper_part(group_upper)
+
+
+def transfer_group_kernel(groups, near_ref, far_ref, upper_ref, out_ref):
+    ((_, root_inverse),) = eliminate([unpack(near_ref[...] + far_ref[...])])
+    out_ref[0] = right_solve(upper_ref[...], root_inverse * math.sqrt(groups))
 
 
 def body(u_blocks, v_blocks, sketch, near_diag, block_row, col_count):
@@ -315,7 +316,7 @@
         in_specs=in_vmem(len(terms) + 2),
         out_specs=in_vmem(3),
         name="sample",
-    )(*pin(*terms), near_diag, sketch)
+    )(*pin(*terms, near_diag, sketch))
     every = lax.all_to_all(packed, "dev", split_axis=0, concat_axis=0, tiled=True)
     leaf_basis, upper = pl.pallas_call(
         leaf_kernel,
@@ -327,6 +328,7 @@
         out_specs=[pl.BlockSpec((2, R, LEAF), lambda: (0, 0, 0))] + in_vmem(1),
         name="leaf",
     )(*pin(gram, sample))
+    every, upper = lax.optimization_barrier((every, upper))
     own_gram = pl.pallas_call(
         group_kernel,
         out_shape=pltpu.VMEM((8, 128), jnp.float32),
@@ -338,15 +340,21 @@
     for step in range(1, 3):
         total = total + got
         got = across(total, step)
-    transfer_leaf, transfer_group = pl.pallas_call(
-        functools.partial(transfer_kernel, 2 * members, groups),
+    transfer_leaf, group_upper = pl.pallas_call(
+        functools.partial(transfer_leaf_kernel, 2 * members),
         out_shape=(
             jax.ShapeDtypeStruct((2, R, R), jnp.float32),
-            jax.ShapeDtypeStruct((1, R, R), jnp.float32),
+            pltpu.VMEM((R, R), jnp.float32),
         ),
-        in_specs=in_vmem(4),
-        name="transfer",
-    )(*pin(own_gram, total, got, upper))
+        in_specs=in_vmem(2),
+        name="transfer_leaf",
+    )(*pin(own_gram, upper))
+    transfer_group = pl.pallas_call(
+        functools.partial(transfer_group_kernel, groups),
+        out_shape=jax.ShapeDtypeStruct((1, R, R), jnp.float32),
+        in_specs=in_vmem(3),
+        name="transfer_group",
+    )(*pin(total, got, group_upper))
     return (leaf_basis, transfer_leaf, transfer_group)
 
 

time: 112 us -> 110 us (0.982)
  blocking collectives: 14.7 us -> 0 us
  waiting for transfers between devices: 40.8 us -> 49.6 us
  starting transfers between devices: 40.7 us -> 45.9 us
  Pallas kernels: 13.5 us -> 12.2 us
    all_to_all x1 -> x0, blocking collectives: 14.7 us -> none  [body(): lax.all_to_all(packed, 'dev', split_axis=0, concat_axis=0, tiled=True)]
    all_to_all x0 -> x1, waiting for transfers between devices: none -> 7.31 us  [body(): lax.all_to_all(packed, 'dev', split_axis=0, concat_axis=0, tiled=True)]
    all_to_all x0 -> x1, starting transfers between devices: none -> 4.94 us  [body(): lax.all_to_all(packed, 'dev', split_axis=0, concat_axis=0, tiled=True)]
    pallas_call x1 -> x2, Pallas kernels: 2.12 us -> 3.32 us  [the longest x1 1.68 us: body(): pl.pallas_call(functools.partial(transfer_leaf_kernel, 2 * members), out_...]
    ppermute x18, waiting for transfers between devices: 39 us -> 40.2 us  [exchange(): return lax.ppermute(value, 'dev', pairs)]
  transfers between devices with their start and end apart: 21 -> 22, of which waited for: 11 -> 13; matrix products, arithmetic and copies ran while one was open for 1% -> 1% of each run, Pallas kernels for 2% -> 3%
where the time goes in v5:
time: 110 us
  waiting for transfers between devices  49.6 us (45%)
  starting transfers between devices  45.9 us (42%)
  Pallas kernels  12.2 us (11%)
  other arithmetic  1.41 us (1%)
    ppermute x18, waiting for transfers between devices, exchange(): return lax.ppermute(value, 'dev', pairs)  40.2 us
    ppermute x18, starting transfers between devices, exchange(): return lax.ppermute(value, 'dev', pairs)  28.8 us
    ppermute x3, starting transfers between devices, across(): return lax.ppermute(value, 'grp', pairs)  12.2 us
    all_to_all x1, waiting for transfers between devices, body(): lax.all_to_all(packed, 'dev', split_axis=0, concat_axis=0, tiled=True)  7.31 us
    pallas_call x1, Pallas kernels, contributions(): pl.pallas_call(contribution_kernel, out_shape=shapes, in_specs=[pl.BlockS...  5.72 us
    all_to_all x1, starting transfers between devices, body(): lax.all_to_all(packed, 'dev', split_axis=0, concat_axis=0, tiled=True)  4.94 us
  transfers between devices with their start and end apart: 22, of which 13 were waited for; matrix products, arithmetic and copies ran while one was open for 1% of the time, Pallas kernels for 3%

profile of v5, /device:TPU:1, one launch (start us, length us, event | category | flops | bytes accessed | tf_op | source)
XLA Modules:
  0.0 109.9 jit_solution(7985935186715729903)
XLA Ops:
  0.6 5.7 %contributions.1 = (f32[16,32,512]{2,1,0:T(8,128)S(1)}, f32[16,32,512]{2,1,0:T(8,128)S(1)}, f32[16,32,512]{2,1,0:T(8,128)S(1)}, f32[16,32,512]{2,1,0:T(8,128)S(1...) custom-call(s32[24]{0:T(128)} %rows_hbm.1, ...), custom_call_target="tpu_custom_call" | custom-call | flops 1000000000 | bytes 16777216 | tf_op jit(solution)/shard_map/contributions/pallas_call | solution.py:141
  6.4 2.1 %collective-permute-start = (f32[16,32,512]{2,1,0:T(8,128)S(1)}, f32[16,32,512]{2,1,0:T(8,128)S(1)}, u32[]{:S(2)}, u32[]{:S(2)}) collective-permute-start(f32[16,32,512]{2,1,0:T(8,128)S(1)} %get-tuple-element.21), channel_id=1, source_target_pairs={{0,1},{1,0},{2,3},{3,2},{4,5},{5,4},{6,7},{7,6},{8,9},{9,8},{10,11... | collective-permute-start | bytes 3145736 | tf_op jit(solution)/shard_map/ppermute | solution.py:170
  8.5 1.6 %collective-permute-start.4 = (f32[16,32,512]{2,1,0:T(8,128)S(1)}, f32[16,32,512]{2,1,0:T(8,128)S(1)}, u32[]{:S(2)}, u32[]{:S(2)}) collective-permute-start(f32[16,32,512]{2,1,0:T(8,128)S(1)} %get-tuple-element.23), channel_id=1, source_target_pairs={{0,4},{1,5},{2,6},{3,7},{4,0},{5,1},{6,2},{7,3},{8,12},{9,13},{10,... | collective-permute-start | bytes 3145736 | tf_op jit(solution)/shard_map/ppermute | solution.py:170
  10.1 1.8 %collective-permute-start.9 = (f32[16,32,512]{2,1,0:T(8,128)S(1)}, f32[16,32,512]{2,1,0:T(8,128)S(1)}, u32[]{:S(2)}, u32[]{:S(2)}) collective-permute-start(f32[16,32,512]{2,1,0:T(8,128)S(1)} %get-tuple-element.25), channel_id=1, source_target_pairs={{0,3},{1,2},{2,1},{3,0},{4,7},{5,6},{6,5},{7,4},{8,11},{9,10},{10,... | collective-permute-start | bytes 3145736 | tf_op jit(solution)/shard_map/ppermute | solution.py:170
  11.9 4.7 %collective-permute-start.13 = (f32[16,32,512]{2,1,0:T(8,128)S(1)}, f32[16,32,512]{2,1,0:T(8,128)S(1)}, u32[]{:S(2)}, u32[]{:S(2)}) collective-permute-start(f32[16,32,512]{2,1,0:T(8,128)S(1)} %get-tuple-element.27), channel_id=1, source_target_pairs={{0,28},{1,29},{2,30},{3,31},{4,8},{5,9},{6,10},{7,11},{8,4},{9,5},... | collective-permute-start | bytes 3145736 | tf_op jit(solution)/shard_map/ppermute | solution.py:170
  16.6 13.4 %collective-permute-done = f32[16,32,512]{2,1,0:T(8,128)S(1)} collective-permute-done((f32[16,32,512]{2,1,0:T(8,128)S(1)}, f32[16,32,512]{2,1,0:T(8,128)S(1)}, u32[]{:S(2)}, u32[]{:S(2)}) %collective-permute-start) | collective-permute-done | bytes 1048608 | tf_op jit(solution)/shard_map/ppermute | solution.py:170
  30.3 3.8 %collective-permute-start.1 = (f32[8,32,512]{2,1,0:T(8,128)S(1)}, f32[8,32,512]{2,1,0:T(8,128)S(1)}, u32[]{:S(2)}, u32[]{:S(2)}) collective-permute-start(f32[8,32,512]{2,1,0:T(8,128)S(1)} %get-tuple-element.44), channel_id=1, source_target_pairs={{0,3},{1,2},{2,1},{3,0},{4,7},{5,6},{6,5},{7,4},{8,11},{9,10},{10,... | collective-permute-start | bytes 1572872 | tf_op jit(solution)/shard_map/ppermute | solution.py:170
  34.3 5.7 %collective-permute-start.5 = (f32[8,32,512]{2,1,0:T(8,128)S(1)}, f32[8,32,512]{2,1,0:T(8,128)S(1)}, u32[]{:S(2)}, u32[]{:S(2)}) collective-permute-start(f32[8,32,512]{2,1,0:T(8,128)S(1)} %get-tuple-element.42), channel_id=1, source_target_pairs={{0,28},{1,29},{2,30},{3,31},{4,8},{5,9},{6,10},{7,11},{8,4},{9,5},... | collective-permute-start | bytes 1572872 | tf_op jit(solution)/shard_map/ppermute | solution.py:170
  40.6 6.0 %collective-permute-done.1 = f32[8,32,512]{2,1,0:T(8,128)S(1)} collective-permute-done((f32[8,32,512]{2,1,0:T(8,128)S(1)}, f32[8,32,512]{2,1,0:T(8,128)S(1)}, u32[]{:S(2)}, u32[]{:S(2)}) %collective-permute-start.1) | collective-permute-done | bytes 524320 | tf_op jit(solution)/shard_map/ppermute | solution.py:170
  46.8 3.6 %collective-permute-done.5 = f32[8,32,512]{2,1,0:T(8,128)S(1)} collective-permute-done((f32[8,32,512]{2,1,0:T(8,128)S(1)}, f32[8,32,512]{2,1,0:T(8,128)S(1)}, u32[]{:S(2)}, u32[]{:S(2)}) %collective-permute-start.5) | collective-permute-done | bytes 524320 | tf_op jit(solution)/shard_map/ppermute | solution.py:170
  54.4 3.0 %collective-permute-done.2 = f32[4,32,512]{2,1,0:T(8,128)S(1)} collective-permute-done((f32[4,32,512]{2,1,0:T(8,128)S(1)}, f32[4,32,512]{2,1,0:T(8,128)S(1)}, u32[]{:S(2)}, u32[]{:S(2)}) %collective-permute-start.2) | collective-permute-done | bytes 262176 | tf_op jit(solution)/shard_map/ppermute | solution.py:170
  57.4 1.7 %collective-permute-start.3 = (f32[2,32,512]{2,1,0:T(8,128)S(1)}, f32[2,32,512]{2,1,0:T(8,128)S(1)}, u32[]{:S(2)}, u32[]{:S(2)}) collective-permute-start(f32[2,32,512]{2,1,0:T(8,128)S(1)} %get-tuple-element.60), channel_id=1, source_target_pairs={{0,28},{1,29},{2,30},{3,31},{4,8},{5,9},{6,10},{7,11},{8,4},{9,5},... | collective-permute-start | bytes 393224 | tf_op jit(solution)/shard_map/ppermute | solution.py:170
  60.6 3.6 %collective-permute-done.3 = f32[2,32,512]{2,1,0:T(8,128)S(1)} collective-permute-done((f32[2,32,512]{2,1,0:T(8,128)S(1)}, f32[2,32,512]{2,1,0:T(8,128)S(1)}, u32[]{:S(2)}, u32[]{:S(2)}) %collective-permute-start.3) | collective-permute-done | bytes 131104 | tf_op jit(solution)/shard_map/ppermute | solution.py:170
  64.3 1.7 %collective-permute-done.7 = f32[2,32,512]{2,1,0:T(8,128)S(1)} collective-permute-done((f32[2,32,512]{2,1,0:T(8,128)S(1)}, f32[2,32,512]{2,1,0:T(8,128)S(1)}, u32[]{:S(2)}, u32[]{:S(2)}) %collective-permute-start.7) | collective-permute-done | bytes 131104 | tf_op jit(solution)/shard_map/ppermute | solution.py:170
  66.0 1.7 %collective-permute-start.8 = (f32[1,32,1024]{2,1,0:T(8,128)S(1)}, f32[1,32,1024]{2,1,0:T(8,128)S(1)}, u32[]{:S(2)}, u32[]{:S(2)}) collective-permute-start(f32[1,32,1024]{2,1,0:T(8,128)S(1)} %pad_maximum_fusion), channel_id=1, source_target_pairs={{0,12},{1,13},{2,14},{3,15},{4,24},{5,25},{6,26},{7,27},{8,20},{9,... | collective-permute-start | bytes 393224 | tf_op jit(solution)/shard_map/ppermute | solution.py:170
  69.4 3.9 %collective-permute-done.8 = f32[1,32,1024]{2,1,0:T(8,128)S(1)} collective-permute-done((f32[1,32,1024]{2,1,0:T(8,128)S(1)}, f32[1,32,1024]{2,1,0:T(8,128)S(1)}, u32[]{:S(2)}, u32[]{:S(2)}) %collective-permute-start.8) | collective-permute-done | bytes 131104 | tf_op jit(solution)/shard_map/ppermute | solution.py:170
  73.3 3.6 %collective-permute-done.17 = f32[1,32,1024]{2,1,0:T(8,128)S(1)} collective-permute-done((f32[1,32,1024]{2,1,0:T(8,128)S(1)}, f32[1,32,1024]{2,1,0:T(8,128)S(1)}, u32[]{:S(2)}, u32[]{:S(2)}) %collective-permute-start.17) | collective-permute-done | bytes 131104 | tf_op jit(solution)/shard_map/ppermute | solution.py:170
  78.0 4.9 %all-to-all-start = ((f32[32,8,128]{2,1,0:T(8,128)}), f32[32,8,128]{2,1,0:T(8,128)S(1)}, u32[]{:S(2)}, u32[]{:S(2)}) async-start(f32[32,8,128]{2,1,0:T(8,128)} %get-tuple-element.31), calls=%async_computation | async-start | bytes 262144 | tf_op jit(solution)/shard_map/all_to_all | solution.py:320
  82.9 2.0 %leaf.1 = (f32[2,32,1024]{2,1,0:T(8,128)}, f32[2,32,32]{2,1,0:T(8,128)S(1)}) custom-call(f32[2,32,32]{2,1,0:T(8,128)S(1)} %get-tuple-element.28.gram_ref, f32[2,32,1024]{2,1,0:T(8,128)S(1)} %get-tuple-element.29.sample_ref), custom_call_target="tpu_custom_call" | custom-call | tf_op jit(solution)/shard_map/leaf/pallas_call | solution.py:321
  85.0 7.3 %all-to-all-done.every_ref = f32[32,8,128]{2,1,0:T(8,128)S(1)} async-done(((f32[32,8,128]{2,1,0:T(8,128)}), f32[32,8,128]{2,1,0:T(8,128)S(1)}, u32[]{:S(2)}, u32[]{:S(2)}) %all-to-all-start) | async-done | bytes 131104 | tf_op jit(solution)/shard_map/all_to_all | solution.py:320
  92.3 6.9 %collective-permute-start.18 = (f32[8,128]{1,0:T(8,128)S(1)}, f32[8,128]{1,0:T(8,128)S(1)}, u32[]{:S(2)}, u32[]{:S(2)}) collective-permute-start(f32[8,128]{1,0:T(8,128)S(1)} %group.1.own_ref), channel_id=1, source_target_pairs={{0,32},{32,0},{64,96},{96,64},{128,160},{160,128},{192,224},{224,1... | collective-permute-start | bytes 12296 | tf_op jit(solution)/shard_map/ppermute | solution.py:179
  102.5 4.1 %collective-permute-start.20 = (f32[8,128]{1,0:T(8,128)S(1)}, f32[8,128]{1,0:T(8,128)S(1)}, u32[]{:S(2)}, u32[]{:S(2)}) collective-permute-start(f32[8,128]{1,0:T(8,128)S(1)} %add.135.near_ref), channel_id=1, source_target_pairs={{0,192},{32,224},{64,128},{96,160},{128,64},{160,96},{192,0},{224,... | collective-permute-start | bytes 12296 | tf_op jit(solution)/shard_map/ppermute | solution.py:179
  106.6 1.7 %transfer_leaf.1 = (f32[2,32,32]{2,1,0:T(8,128)}, f32[32,32]{1,0:T(8,128)S(1)}) custom-call(f32[8,128]{1,0:T(8,128)S(1)} %group.1.own_ref, f32[2,32,32]{2,1,0:T(8,128)S(1)} %get-tuple-element.34.upper_ref), custom_call_target="tpu_custom_call" | custom-call | tf_op jit(solution)/shard_map/transfer_leaf/pallas_call | solution.py:343
  108.3 1.6 %transfer_group.1 = f32[1,32,32]{2,1,0:T(8,128)} custom-call(f32[8,128]{1,0:T(8,128)S(1)} %add.135.near_ref, f32[8,128]{1,0:T(8,128)S(1)} %collective-permute-done.20.far_ref, f32[32,32]{1,0:T(8,128)S(1)} %get-tuple-element.36.upper_ref), custom_call_target="tpu_custom_call" | custom-call | tf_op jit(solution)/shard_map/transfer_group/pallas_call | solution.py:352
  (50 shorter events, 12.7 us)
Async XLA Ops:
  6.4 23.7 %collective-permute-start = (f32[16,32,512]{2,1,0:T(8,128)S(1)}, f32[16,32,512]{2,1,0:T(8,128)S(1)}, u32[]{:S(2)}, u32[]{:S(2)}) collective-permute-start(f32[16,32,512]{2,1,0:T(8,128)S(1)} %get-tuple-element.21), channel_id=1, source_target_pairs={{0,1},{1,0},{2,3},{3,2},{4,5},{5,4},{6,7},{7,6},{8,9},{9,8},{10,11... | collective-permute-start | bytes 3145736 | tf_op jit(solution)/shard_map/ppermute | solution.py:170
  8.5 25.6 %collective-permute-start.4 = (f32[16,32,512]{2,1,0:T(8,128)S(1)}, f32[16,32,512]{2,1,0:T(8,128)S(1)}, u32[]{:S(2)}, u32[]{:S(2)}) collective-permute-start(f32[16,32,512]{2,1,0:T(8,128)S(1)} %get-tuple-element.23), channel_id=1, source_target_pairs={{0,4},{1,5},{2,6},{3,7},{4,0},{5,1},{6,2},{7,3},{8,12},{9,13},{10,... | collective-permute-start | bytes 3145736 | tf_op jit(solution)/shard_map/ppermute | solution.py:170
  10.1 29.9 %collective-permute-start.9 = (f32[16,32,512]{2,1,0:T(8,128)S(1)}, f32[16,32,512]{2,1,0:T(8,128)S(1)}, u32[]{:S(2)}, u32[]{:S(2)}) collective-permute-start(f32[16,32,512]{2,1,0:T(8,128)S(1)} %get-tuple-element.25), channel_id=1, source_target_pairs={{0,3},{1,2},{2,1},{3,0},{4,7},{5,6},{6,5},{7,4},{8,11},{9,10},{10,... | collective-permute-start | bytes 3145736 | tf_op jit(solution)/shard_map/ppermute | solution.py:170
  11.9 28.4 %collective-permute-start.13 = (f32[16,32,512]{2,1,0:T(8,128)S(1)}, f32[16,32,512]{2,1,0:T(8,128)S(1)}, u32[]{:S(2)}, u32[]{:S(2)}) collective-permute-start(f32[16,32,512]{2,1,0:T(8,128)S(1)} %get-tuple-element.27), channel_id=1, source_target_pairs={{0,28},{1,29},{2,30},{3,31},{4,8},{5,9},{6,10},{7,11},{8,4},{9,5},... | collective-permute-start | bytes 3145736 | tf_op jit(solution)/shard_map/ppermute | solution.py:170
  30.3 16.4 %collective-permute-start.1 = (f32[8,32,512]{2,1,0:T(8,128)S(1)}, f32[8,32,512]{2,1,0:T(8,128)S(1)}, u32[]{:S(2)}, u32[]{:S(2)}) collective-permute-start(f32[8,32,512]{2,1,0:T(8,128)S(1)} %get-tuple-element.44), channel_id=1, source_target_pairs={{0,3},{1,2},{2,1},{3,0},{4,7},{5,6},{6,5},{7,4},{8,11},{9,10},{10,... | collective-permute-start | bytes 1572872 | tf_op jit(solution)/shard_map/ppermute | solution.py:170
  34.3 16.1 %collective-permute-start.5 = (f32[8,32,512]{2,1,0:T(8,128)S(1)}, f32[8,32,512]{2,1,0:T(8,128)S(1)}, u32[]{:S(2)}, u32[]{:S(2)}) collective-permute-start(f32[8,32,512]{2,1,0:T(8,128)S(1)} %get-tuple-element.42), channel_id=1, source_target_pairs={{0,28},{1,29},{2,30},{3,31},{4,8},{5,9},{6,10},{7,11},{8,4},{9,5},... | collective-permute-start | bytes 1572872 | tf_op jit(solution)/shard_map/ppermute | solution.py:170
  40.2 11.4 %collective-permute-start.10 = (f32[8,32,512]{2,1,0:T(8,128)S(1)}, f32[8,32,512]{2,1,0:T(8,128)S(1)}, u32[]{:S(2)}, u32[]{:S(2)}) collective-permute-start(f32[8,32,512]{2,1,0:T(8,128)S(1)} %get-tuple-element.40), channel_id=1, source_target_pairs={{0,1},{1,0},{2,3},{3,2},{4,5},{5,4},{6,7},{7,6},{8,9},{9,8},{10,11... | collective-permute-start | bytes 1572872 | tf_op jit(solution)/shard_map/ppermute | solution.py:170
  40.5 12.7 %collective-permute-start.14 = (f32[8,32,512]{2,1,0:T(8,128)S(1)}, f32[8,32,512]{2,1,0:T(8,128)S(1)}, u32[]{:S(2)}, u32[]{:S(2)}) collective-permute-start(f32[8,32,512]{2,1,0:T(8,128)S(1)} %get-tuple-element.38), channel_id=1, source_target_pairs={{0,4},{1,5},{2,6},{3,7},{4,0},{5,1},{6,2},{7,3},{8,12},{9,13},{10,... | collective-permute-start | bytes 1572872 | tf_op jit(solution)/shard_map/ppermute | solution.py:170
  46.7 10.7 %collective-permute-start.2 = (f32[4,32,512]{2,1,0:T(8,128)S(1)}, f32[4,32,512]{2,1,0:T(8,128)S(1)}, u32[]{:S(2)}, u32[]{:S(2)}) collective-permute-start(f32[4,32,512]{2,1,0:T(8,128)S(1)} %get-tuple-element.52), channel_id=1, source_target_pairs={{0,4},{1,5},{2,6},{3,7},{4,0},{5,1},{6,2},{7,3},{8,12},{9,13},{10,... | collective-permute-start | bytes 786440 | tf_op jit(solution)/shard_map/ppermute | solution.py:170
  50.5 8.7 %collective-permute-start.6 = (f32[4,32,512]{2,1,0:T(8,128)S(1)}, f32[4,32,512]{2,1,0:T(8,128)S(1)}, u32[]{:S(2)}, u32[]{:S(2)}) collective-permute-start(f32[4,32,512]{2,1,0:T(8,128)S(1)} %get-tuple-element.50), channel_id=1, source_target_pairs={{0,1},{1,0},{2,3},{3,2},{4,5},{5,4},{6,7},{7,6},{8,9},{9,8},{10,11... | collective-permute-start | bytes 786440 | tf_op jit(solution)/shard_map/ppermute | solution.py:170
  51.7 7.7 %collective-permute-start.11 = (f32[4,32,512]{2,1,0:T(8,128)S(1)}, f32[4,32,512]{2,1,0:T(8,128)S(1)}, u32[]{:S(2)}, u32[]{:S(2)}) collective-permute-start(f32[4,32,512]{2,1,0:T(8,128)S(1)} %get-tuple-element.48), channel_id=1, source_target_pairs={{0,28},{1,29},{2,30},{3,31},{4,8},{5,9},{6,10},{7,11},{8,4},{9,5},... | collective-permute-start | bytes 786440 | tf_op jit(solution)/shard_map/ppermute | solution.py:170
  53.2 23.7 %copy-start = (f32[2,32,1024]{2,1,0:T(8,128)S(1)}, f32[2,32,1024]{2,1,0:T(8,128)}, u32[]{:S(2)}) copy-start(f32[2,32,1024]{2,1,0:T(8,128)} %refs_7_.1) | copy-start | bytes 786436
  53.2 23.7 %copy-start.1 = (f32[2,1024]{1,0:T(2,128)S(1)}, f32[2,1024]{1,0:T(2,128)}, u32[]{:S(2)}) copy-start(f32[2,1024]{1,0:T(2,128)} %refs_6_.1) | copy-start | bytes 24580
  53.3 7.0 %collective-permute-start.15 = (f32[4,32,512]{2,1,0:T(8,128)S(1)}, f32[4,32,512]{2,1,0:T(8,128)S(1)}, u32[]{:S(2)}, u32[]{:S(2)}) collective-permute-start(f32[4,32,512]{2,1,0:T(8,128)S(1)} %get-tuple-element.46), channel_id=1, source_target_pairs={{0,3},{1,2},{2,1},{3,0},{4,7},{5,6},{6,5},{7,4},{8,11},{9,10},{10,... | collective-permute-start | bytes 786440 | tf_op jit(solution)/shard_map/ppermute | solution.py:170
  57.4 6.8 %collective-permute-start.3 = (f32[2,32,512]{2,1,0:T(8,128)S(1)}, f32[2,32,512]{2,1,0:T(8,128)S(1)}, u32[]{:S(2)}, u32[]{:S(2)}) collective-permute-start(f32[2,32,512]{2,1,0:T(8,128)S(1)} %get-tuple-element.60), channel_id=1, source_target_pairs={{0,28},{1,29},{2,30},{3,31},{4,8},{5,9},{6,10},{7,11},{8,4},{9,5},... | collective-permute-start | bytes 393224 | tf_op jit(solution)/shard_map/ppermute | solution.py:170
  59.2 6.8 %collective-permute-start.7 = (f32[2,32,512]{2,1,0:T(8,128)S(1)}, f32[2,32,512]{2,1,0:T(8,128)S(1)}, u32[]{:S(2)}, u32[]{:S(2)}) collective-permute-start(f32[2,32,512]{2,1,0:T(8,128)S(1)} %get-tuple-element.58), channel_id=1, source_target_pairs={{0,3},{1,2},{2,1},{3,0},{4,7},{5,6},{6,5},{7,4},{8,11},{9,10},{10,... | collective-permute-start | bytes 393224 | tf_op jit(solution)/shard_map/ppermute | solution.py:170
  59.5 8.2 %collective-permute-start.12 = (f32[2,32,512]{2,1,0:T(8,128)S(1)}, f32[2,32,512]{2,1,0:T(8,128)S(1)}, u32[]{:S(2)}, u32[]{:S(2)}) collective-permute-start(f32[2,32,512]{2,1,0:T(8,128)S(1)} %get-tuple-element.56), channel_id=1, source_target_pairs={{0,4},{1,5},{2,6},{3,7},{4,0},{5,1},{6,2},{7,3},{8,12},{9,13},{10,... | collective-permute-start | bytes 393224 | tf_op jit(solution)/shard_map/ppermute | solution.py:170
  60.3 7.4 %collective-permute-start.16 = (f32[2,32,512]{2,1,0:T(8,128)S(1)}, f32[2,32,512]{2,1,0:T(8,128)S(1)}, u32[]{:S(2)}, u32[]{:S(2)}) collective-permute-start(f32[2,32,512]{2,1,0:T(8,128)S(1)} %get-tuple-element.54), channel_id=1, source_target_pairs={{0,1},{1,0},{2,3},{3,2},{4,5},{5,4},{6,7},{7,6},{8,9},{9,8},{10,11... | collective-permute-start | bytes 393224 | tf_op jit(solution)/shard_map/ppermute | solution.py:170
  66.0 7.3 %collective-permute-start.8 = (f32[1,32,1024]{2,1,0:T(8,128)S(1)}, f32[1,32,1024]{2,1,0:T(8,128)S(1)}, u32[]{:S(2)}, u32[]{:S(2)}) collective-permute-start(f32[1,32,1024]{2,1,0:T(8,128)S(1)} %pad_maximum_fusion), channel_id=1, source_target_pairs={{0,12},{1,13},{2,14},{3,15},{4,24},{5,25},{6,26},{7,27},{8,20},{9,... | collective-permute-start | bytes 393224 | tf_op jit(solution)/shard_map/ppermute | solution.py:170
  67.8 9.1 %collective-permute-start.17 = (f32[1,32,1024]{2,1,0:T(8,128)S(1)}, f32[1,32,1024]{2,1,0:T(8,128)S(1)}, u32[]{:S(2)}, u32[]{:S(2)}) collective-permute-start(f32[1,32,1024]{2,1,0:T(8,128)S(1)} %pad_maximum_fusion.1), channel_id=1, source_target_pairs={{0,20},{1,21},{2,22},{3,23},{4,16},{5,17},{6,18},{7,19},{8,28},{9,... | collective-permute-start | bytes 393224 | tf_op jit(solution)/shard_map/ppermute | solution.py:170
  78.0 14.3 %all-to-all-start = ((f32[32,8,128]{2,1,0:T(8,128)}), f32[32,8,128]{2,1,0:T(8,128)S(1)}, u32[]{:S(2)}, u32[]{:S(2)}) async-start(f32[32,8,128]{2,1,0:T(8,128)} %get-tuple-element.31), calls=%async_computation | async-start | bytes 262144 | tf_op jit(solution)/shard_map/all_to_all | solution.py:320
  92.3 7.7 %collective-permute-start.18 = (f32[8,128]{1,0:T(8,128)S(1)}, f32[8,128]{1,0:T(8,128)S(1)}, u32[]{:S(2)}, u32[]{:S(2)}) collective-permute-start(f32[8,128]{1,0:T(8,128)S(1)} %group.1.own_ref), channel_id=1, source_target_pairs={{0,32},{32,0},{64,96},{96,64},{128,160},{160,128},{192,224},{224,1... | collective-permute-start | bytes 12296 | tf_op jit(solution)/shard_map/ppermute | solution.py:179
  100.0 2.5 %collective-permute-start.19 = (f32[8,128]{1,0:T(8,128)S(1)}, f32[8,128]{1,0:T(8,128)S(1)}, u32[]{:S(2)}, u32[]{:S(2)}) collective-permute-start(f32[8,128]{1,0:T(8,128)S(1)} %add.134), channel_id=1, source_target_pairs={{0,64},{32,96},{64,0},{96,32},{128,192},{160,224},{192,128},{224,1... | collective-permute-start | bytes 12296 | tf_op jit(solution)/shard_map/ppermute | solution.py:179
  102.5 5.8 %collective-permute-start.20 = (f32[8,128]{1,0:T(8,128)S(1)}, f32[8,128]{1,0:T(8,128)S(1)}, u32[]{:S(2)}, u32[]{:S(2)}) collective-permute-start(f32[8,128]{1,0:T(8,128)S(1)} %add.135.near_ref), channel_id=1, source_target_pairs={{0,192},{32,224},{64,128},{96,160},{128,64},{160,96},{192,0},{224,... | collective-permute-start | bytes 12296 | tf_op jit(solution)/shard_map/ppermute | solution.py:179

commit v6 on v5

--- a/solution.py
+++ b/solution.py
@@ -17,7 +17,7 @@
     "x": (("x", 0), ("x", 1), ("z", 0), ("z", 1)),
     "z": (("z", 0), ("z", 1), ("x", 0), ("x", 1)),
 }
-BLOCK = 8
+BLOCK = 16
 GROUP = 24
 HIGHEST = lax.Precision.HIGHEST
 X_ORDER, Z_ORDER = (0, 2, 3, 1), (0, 4, 6, 1, 3, 7, 5, 2)
@@ -40,10 +40,10 @@
 
 
 def z_partner(step, which, z):
-    w = (z - which) % NZ
+    w = (z - 1 + which) % NZ
     odd = w % 2
     other = (w ^ 1, w - 1 + 2 * odd, w + 3 + 2 * odd)[step]
-    return (other + which) % NZ
+    return (other + 1 - which) % NZ
 
 
 def contribution_kernel(rows_hbm, count_hbm, u_hbm, v_hbm, sketch_hbm, *refs):
@@ -99,9 +99,9 @@
             row = rows_ref[slot] & (2 * NZ * NX - 1)
             cluster = row & 1
             live = slot < live_count
-            own_w = (me // NX - cluster) & (NZ - 1)
+            own_w = (me // NX - 1 + cluster) & (NZ - 1)
             own_q = (me % NX - cluster) & (NX - 1)
-            to_w = ((row >> 3) - cluster) & (NZ - 1)
+            to_w = ((row >> 3) - 1 + cluster) & (NZ - 1)
             to_q = (((row >> 1) & (NX - 1)) - cluster) & (NX - 1)
             step_z = jnp.where(own_w & 1 == 0, to_w - own_w, own_w - to_w) & (NZ - 1)
             x_slot, z_slot = lookup(X_ORDER, own_q ^ to_q), lookup(Z_ORDER, step_z)
@@ -311,7 +311,7 @@
         out_shape=(
             pltpu.VMEM((2, R, LEAF), jnp.float32),
             pltpu.VMEM((2, R, R), jnp.float32),
-            jax.ShapeDtypeStruct((members, 8, 128), jnp.float32),
+            pltpu.VMEM((members, 8, 128), jnp.float32),
         ),
         in_specs=in_vmem(len(terms) + 2),
         out_specs=in_vmem(3),

time: 110 us -> 108 us (0.982)
  waiting for transfers between devices: 49.6 us -> 47.4 us
    all_to_all x1, starting transfers between devices: 4.94 us -> 10.2 us  [body(): lax.all_to_all(packed, 'dev', split_axis=0, concat_axis=0, tiled=True)]
    ppermute x3, starting transfers between devices: 12.2 us -> 7.62 us  [across(): return lax.ppermute(value, 'grp', pairs)]
    ppermute x18, waiting for transfers between devices: 40.2 us -> 37.3 us  [exchange(): return lax.ppermute(value, 'dev', pairs)]
  transfers between devices with their start and end apart: 22 -> 22, of which waited for: 13 -> 12; matrix products, arithmetic and copies ran while one was open for 1% -> 1% of each run, Pallas kernels for 3% -> 3%
where the time goes in v6:
time: 108 us; the launch traced here: 107 us
  waiting for transfers between devices  47.4 us (44%)
  starting transfers between devices  45.5 us (42%)
  Pallas kernels  12 us (11%)
  other arithmetic  1.41 us (1%)
    ppermute x18, waiting for transfers between devices, exchange(): return lax.ppermute(value, 'dev', pairs)  37.3 us
    ppermute x18, starting transfers between devices, exchange(): return lax.ppermute(value, 'dev', pairs)  27.7 us
    all_to_all x1, starting transfers between devices, body(): lax.all_to_all(packed, 'dev', split_axis=0, concat_axis=0, tiled=True)  10.2 us
    ppermute x3, starting transfers between devices, across(): return lax.ppermute(value, 'grp', pairs)  7.62 us
    all_to_all x1, waiting for transfers between devices, body(): lax.all_to_all(packed, 'dev', split_axis=0, concat_axis=0, tiled=True)  7.3 us
    pallas_call x1, Pallas kernels, contributions(): pl.pallas_call(contribution_kernel, out_shape=shapes, in_specs=[pl.BlockS...  5.71 us
    ppermute x3, waiting for transfers between devices, across(): return lax.ppermute(value, 'grp', pairs)  2.82 us
  transfers between devices with their start and end apart: 22, of which 12 were waited for; matrix products, arithmetic and copies ran while one was open for 1% of the time, Pallas kernels for 3%

profile of v6, /device:TPU:1, one launch (start us, length us, event | category | flops | bytes accessed | tf_op | source)
XLA Modules:
  0.0 107.2 jit_solution(16926368471034614497)
XLA Ops:
  0.6 5.7 %contributions.1 = (f32[16,32,512]{2,1,0:T(8,128)S(1)}, f32[16,32,512]{2,1,0:T(8,128)S(1)}, f32[16,32,512]{2,1,0:T(8,128)S(1)}, f32[16,32,512]{2,1,0:T(8,128)S(1...) custom-call(s32[24]{0:T(128)} %rows_hbm.1, ...), custom_call_target="tpu_custom_call" | custom-call | flops 1000000000 | bytes 16777216 | tf_op jit(solution)/shard_map/contributions/pallas_call | solution.py:141
  6.3 2.1 %collective-permute-start = (f32[16,32,512]{2,1,0:T(8,128)S(1)}, f32[16,32,512]{2,1,0:T(8,128)S(1)}, u32[]{:S(2)}, u32[]{:S(2)}) collective-permute-start(f32[16,32,512]{2,1,0:T(8,128)S(1)} %get-tuple-element.21), channel_id=1, source_target_pairs={{0,1},{1,0},{2,3},{3,2},{4,5},{5,4},{6,7},{7,6},{8,9},{9,8},{10,11... | collective-permute-start | bytes 3145736 | tf_op jit(solution)/shard_map/ppermute | solution.py:170
  8.5 5.6 %collective-permute-start.4 = (f32[16,32,512]{2,1,0:T(8,128)S(1)}, f32[16,32,512]{2,1,0:T(8,128)S(1)}, u32[]{:S(2)}, u32[]{:S(2)}) collective-permute-start(f32[16,32,512]{2,1,0:T(8,128)S(1)} %get-tuple-element.23), channel_id=1, source_target_pairs={{0,28},{1,29},{2,30},{3,31},{4,8},{5,9},{6,10},{7,11},{8,4},{9,5},... | collective-permute-start | bytes 3145736 | tf_op jit(solution)/shard_map/ppermute | solution.py:170
  14.1 1.8 %collective-permute-start.9 = (f32[16,32,512]{2,1,0:T(8,128)S(1)}, f32[16,32,512]{2,1,0:T(8,128)S(1)}, u32[]{:S(2)}, u32[]{:S(2)}) collective-permute-start(f32[16,32,512]{2,1,0:T(8,128)S(1)} %get-tuple-element.25), channel_id=1, source_target_pairs={{0,3},{1,2},{2,1},{3,0},{4,7},{5,6},{6,5},{7,4},{8,11},{9,10},{10,... | collective-permute-start | bytes 3145736 | tf_op jit(solution)/shard_map/ppermute | solution.py:170
  15.9 14.2 %collective-permute-done = f32[16,32,512]{2,1,0:T(8,128)S(1)} collective-permute-done((f32[16,32,512]{2,1,0:T(8,128)S(1)}, f32[16,32,512]{2,1,0:T(8,128)S(1)}, u32[]{:S(2)}, u32[]{:S(2)}) %collective-permute-start) | collective-permute-done | bytes 1048608 | tf_op jit(solution)/shard_map/ppermute | solution.py:170
  30.3 3.8 %collective-permute-start.1 = (f32[8,32,512]{2,1,0:T(8,128)S(1)}, f32[8,32,512]{2,1,0:T(8,128)S(1)}, u32[]{:S(2)}, u32[]{:S(2)}) collective-permute-start(f32[8,32,512]{2,1,0:T(8,128)S(1)} %get-tuple-element.44), channel_id=1, source_target_pairs={{0,3},{1,2},{2,1},{3,0},{4,7},{5,6},{6,5},{7,4},{8,11},{9,10},{10,... | collective-permute-start | bytes 1572872 | tf_op jit(solution)/shard_map/ppermute | solution.py:170
  34.1 2.6 %collective-permute-done.4 = f32[16,32,512]{2,1,0:T(8,128)S(1)} collective-permute-done((f32[16,32,512]{2,1,0:T(8,128)S(1)}, f32[16,32,512]{2,1,0:T(8,128)S(1)}, u32[]{:S(2)}, u32[]{:S(2)}) %collective-permute-start.4) | collective-permute-done | bytes 1048608 | tf_op jit(solution)/shard_map/ppermute | solution.py:170
  37.0 1.8 %collective-permute-done.9 = f32[16,32,512]{2,1,0:T(8,128)S(1)} collective-permute-done((f32[16,32,512]{2,1,0:T(8,128)S(1)}, f32[16,32,512]{2,1,0:T(8,128)S(1)}, u32[]{:S(2)}, u32[]{:S(2)}) %collective-permute-start.9) | collective-permute-done | bytes 1048608 | tf_op jit(solution)/shard_map/ppermute | solution.py:170
  39.2 2.1 %collective-permute-start.14 = (f32[8,32,512]{2,1,0:T(8,128)S(1)}, f32[8,32,512]{2,1,0:T(8,128)S(1)}, u32[]{:S(2)}, u32[]{:S(2)}) collective-permute-start(f32[8,32,512]{2,1,0:T(8,128)S(1)} %get-tuple-element.38), channel_id=1, source_target_pairs={{0,28},{1,29},{2,30},{3,31},{4,8},{5,9},{6,10},{7,11},{8,4},{9,5},... | collective-permute-start | bytes 1572872 | tf_op jit(solution)/shard_map/ppermute | solution.py:170
  41.3 8.6 %collective-permute-done.1 = f32[8,32,512]{2,1,0:T(8,128)S(1)} collective-permute-done((f32[8,32,512]{2,1,0:T(8,128)S(1)}, f32[8,32,512]{2,1,0:T(8,128)S(1)}, u32[]{:S(2)}, u32[]{:S(2)}) %collective-permute-start.1) | collective-permute-done | bytes 524320 | tf_op jit(solution)/shard_map/ppermute | solution.py:170
  51.8 2.0 %collective-permute-start.15 = (f32[4,32,512]{2,1,0:T(8,128)S(1)}, f32[4,32,512]{2,1,0:T(8,128)S(1)}, u32[]{:S(2)}, u32[]{:S(2)}) collective-permute-start(f32[4,32,512]{2,1,0:T(8,128)S(1)} %get-tuple-element.46), channel_id=1, source_target_pairs={{0,3},{1,2},{2,1},{3,0},{4,7},{5,6},{6,5},{7,4},{8,11},{9,10},{10,... | collective-permute-start | bytes 786440 | tf_op jit(solution)/shard_map/ppermute | solution.py:170
  53.8 4.1 %collective-permute-done.2 = f32[4,32,512]{2,1,0:T(8,128)S(1)} collective-permute-done((f32[4,32,512]{2,1,0:T(8,128)S(1)}, f32[4,32,512]{2,1,0:T(8,128)S(1)}, u32[]{:S(2)}, u32[]{:S(2)}) %collective-permute-start.2) | collective-permute-done | bytes 262176 | tf_op jit(solution)/shard_map/ppermute | solution.py:170
  58.1 1.8 %collective-permute-start.7 = (f32[2,32,512]{2,1,0:T(8,128)S(1)}, f32[2,32,512]{2,1,0:T(8,128)S(1)}, u32[]{:S(2)}, u32[]{:S(2)}) collective-permute-start(f32[2,32,512]{2,1,0:T(8,128)S(1)} %get-tuple-element.58), channel_id=1, source_target_pairs={{0,3},{1,2},{2,1},{3,0},{4,7},{5,6},{6,5},{7,4},{8,11},{9,10},{10,... | collective-permute-start | bytes 393224 | tf_op jit(solution)/shard_map/ppermute | solution.py:170
  59.9 2.5 %collective-permute-start.12 = (f32[2,32,512]{2,1,0:T(8,128)S(1)}, f32[2,32,512]{2,1,0:T(8,128)S(1)}, u32[]{:S(2)}, u32[]{:S(2)}) collective-permute-start(f32[2,32,512]{2,1,0:T(8,128)S(1)} %get-tuple-element.56), channel_id=1, source_target_pairs={{0,28},{1,29},{2,30},{3,31},{4,8},{5,9},{6,10},{7,11},{8,4},{9,5},... | collective-permute-start | bytes 393224 | tf_op jit(solution)/shard_map/ppermute | solution.py:170
  64.2 2.8 %collective-permute-start.8 = (f32[1,32,1024]{2,1,0:T(8,128)S(1)}, f32[1,32,1024]{2,1,0:T(8,128)S(1)}, u32[]{:S(2)}, u32[]{:S(2)}) collective-permute-start(f32[1,32,1024]{2,1,0:T(8,128)S(1)} %pad_maximum_fusion), channel_id=1, source_target_pairs={{0,20},{1,21},{2,22},{3,23},{4,16},{5,17},{6,18},{7,19},{8,28},{9,... | collective-permute-start | bytes 393224 | tf_op jit(solution)/shard_map/ppermute | solution.py:170
  67.0 2.0 %collective-permute-start.17 = (f32[1,32,1024]{2,1,0:T(8,128)S(1)}, f32[1,32,1024]{2,1,0:T(8,128)S(1)}, u32[]{:S(2)}, u32[]{:S(2)}) collective-permute-start(f32[1,32,1024]{2,1,0:T(8,128)S(1)} %pad_maximum_fusion.1), channel_id=1, source_target_pairs={{0,12},{1,13},{2,14},{3,15},{4,24},{5,25},{6,26},{7,27},{8,20},{9,... | collective-permute-start | bytes 393224 | tf_op jit(solution)/shard_map/ppermute | solution.py:170
  69.0 2.5 %collective-permute-done.8 = f32[1,32,1024]{2,1,0:T(8,128)S(1)} collective-permute-done((f32[1,32,1024]{2,1,0:T(8,128)S(1)}, f32[1,32,1024]{2,1,0:T(8,128)S(1)}, u32[]{:S(2)}, u32[]{:S(2)}) %collective-permute-start.8) | collective-permute-done | bytes 131104 | tf_op jit(solution)/shard_map/ppermute | solution.py:170
  74.0 10.2 %all-to-all-start = ((f32[32,8,128]{2,1,0:T(8,128)}), f32[32,8,128]{2,1,0:T(8,128)S(1)}, u32[]{:S(2)}, u32[]{:S(2)}) async-start(f32[32,8,128]{2,1,0:T(8,128)} %get-tuple-element.31), calls=%async_computation | async-start | bytes 262144 | tf_op jit(solution)/shard_map/all_to_all | solution.py:320
  84.2 2.0 %leaf.1 = (f32[2,32,1024]{2,1,0:T(8,128)}, f32[2,32,32]{2,1,0:T(8,128)S(1)}) custom-call(f32[2,32,32]{2,1,0:T(8,128)S(1)} %get-tuple-element.28.gram_ref, f32[2,32,1024]{2,1,0:T(8,128)S(1)} %get-tuple-element.29.sample_ref), custom_call_target="tpu_custom_call" | custom-call | tf_op jit(solution)/shard_map/leaf/pallas_call | solution.py:321
  86.2 7.3 %all-to-all-done.every_ref = f32[32,8,128]{2,1,0:T(8,128)S(1)} async-done(((f32[32,8,128]{2,1,0:T(8,128)}), f32[32,8,128]{2,1,0:T(8,128)S(1)}, u32[]{:S(2)}, u32[]{:S(2)}) %all-to-all-start) | async-done | bytes 131104 | tf_op jit(solution)/shard_map/all_to_all | solution.py:320
  93.6 4.9 %collective-permute-start.18 = (f32[8,128]{1,0:T(8,128)S(1)}, f32[8,128]{1,0:T(8,128)S(1)}, u32[]{:S(2)}, u32[]{:S(2)}) collective-permute-start(f32[8,128]{1,0:T(8,128)S(1)} %group.1.own_ref), channel_id=1, source_target_pairs={{0,32},{32,0},{64,96},{96,64},{128,160},{160,128},{192,224},{224,1... | collective-permute-start | bytes 12296 | tf_op jit(solution)/shard_map/ppermute | solution.py:179
  99.8 2.0 %collective-permute-done.19 = f32[8,128]{1,0:T(8,128)S(1)} collective-permute-done((f32[8,128]{1,0:T(8,128)S(1)}, f32[8,128]{1,0:T(8,128)S(1)}, u32[]{:S(2)}, u32[]{:S(2)}) %collective-permute-start.19) | collective-permute-done | bytes 4128 | tf_op jit(solution)/shard_map/ppermute | solution.py:179
  101.8 2.3 %collective-permute-start.20 = (f32[8,128]{1,0:T(8,128)S(1)}, f32[8,128]{1,0:T(8,128)S(1)}, u32[]{:S(2)}, u32[]{:S(2)}) collective-permute-start(f32[8,128]{1,0:T(8,128)S(1)} %add.135.near_ref), channel_id=1, source_target_pairs={{0,192},{32,224},{64,128},{96,160},{128,64},{160,96},{192,0},{224,... | collective-permute-start | bytes 12296 | tf_op jit(solution)/shard_map/ppermute | solution.py:179
  104.0 1.6 %transfer_leaf.1 = (f32[2,32,32]{2,1,0:T(8,128)}, f32[32,32]{1,0:T(8,128)S(1)}) custom-call(f32[8,128]{1,0:T(8,128)S(1)} %group.1.own_ref, f32[2,32,32]{2,1,0:T(8,128)S(1)} %get-tuple-element.34.upper_ref), custom_call_target="tpu_custom_call" | custom-call | tf_op jit(solution)/shard_map/transfer_leaf/pallas_call | solution.py:343
  (50 shorter events, 10.2 us)
Async XLA Ops:
  6.3 23.7 %collective-permute-start = (f32[16,32,512]{2,1,0:T(8,128)S(1)}, f32[16,32,512]{2,1,0:T(8,128)S(1)}, u32[]{:S(2)}, u32[]{:S(2)}) collective-permute-start(f32[16,32,512]{2,1,0:T(8,128)S(1)} %get-tuple-element.21), channel_id=1, source_target_pairs={{0,1},{1,0},{2,3},{3,2},{4,5},{5,4},{6,7},{7,6},{8,9},{9,8},{10,11... | collective-permute-start | bytes 3145736 | tf_op jit(solution)/shard_map/ppermute | solution.py:170
  8.5 28.1 %collective-permute-start.4 = (f32[16,32,512]{2,1,0:T(8,128)S(1)}, f32[16,32,512]{2,1,0:T(8,128)S(1)}, u32[]{:S(2)}, u32[]{:S(2)}) collective-permute-start(f32[16,32,512]{2,1,0:T(8,128)S(1)} %get-tuple-element.23), channel_id=1, source_target_pairs={{0,28},{1,29},{2,30},{3,31},{4,8},{5,9},{6,10},{7,11},{8,4},{9,5},... | collective-permute-start | bytes 3145736 | tf_op jit(solution)/shard_map/ppermute | solution.py:170
  14.1 24.6 %collective-permute-start.9 = (f32[16,32,512]{2,1,0:T(8,128)S(1)}, f32[16,32,512]{2,1,0:T(8,128)S(1)}, u32[]{:S(2)}, u32[]{:S(2)}) collective-permute-start(f32[16,32,512]{2,1,0:T(8,128)S(1)} %get-tuple-element.25), channel_id=1, source_target_pairs={{0,3},{1,2},{2,1},{3,0},{4,7},{5,6},{6,5},{7,4},{8,11},{9,10},{10,... | collective-permute-start | bytes 3145736 | tf_op jit(solution)/shard_map/ppermute | solution.py:170
  15.9 23.1 %collective-permute-start.13 = (f32[16,32,512]{2,1,0:T(8,128)S(1)}, f32[16,32,512]{2,1,0:T(8,128)S(1)}, u32[]{:S(2)}, u32[]{:S(2)}) collective-permute-start(f32[16,32,512]{2,1,0:T(8,128)S(1)} %get-tuple-element.27), channel_id=1, source_target_pairs={{0,4},{1,5},{2,6},{3,7},{4,0},{5,1},{6,2},{7,3},{8,12},{9,13},{10,... | collective-permute-start | bytes 3145736 | tf_op jit(solution)/shard_map/ppermute | solution.py:170
  30.3 19.7 %collective-permute-start.1 = (f32[8,32,512]{2,1,0:T(8,128)S(1)}, f32[8,32,512]{2,1,0:T(8,128)S(1)}, u32[]{:S(2)}, u32[]{:S(2)}) collective-permute-start(f32[8,32,512]{2,1,0:T(8,128)S(1)} %get-tuple-element.44), channel_id=1, source_target_pairs={{0,3},{1,2},{2,1},{3,0},{4,7},{5,6},{6,5},{7,4},{8,11},{9,10},{10,... | collective-permute-start | bytes 1572872 | tf_op jit(solution)/shard_map/ppermute | solution.py:170
  36.9 14.1 %collective-permute-start.5 = (f32[8,32,512]{2,1,0:T(8,128)S(1)}, f32[8,32,512]{2,1,0:T(8,128)S(1)}, u32[]{:S(2)}, u32[]{:S(2)}) collective-permute-start(f32[8,32,512]{2,1,0:T(8,128)S(1)} %get-tuple-element.42), channel_id=1, source_target_pairs={{0,4},{1,5},{2,6},{3,7},{4,0},{5,1},{6,2},{7,3},{8,12},{9,13},{10,... | collective-permute-start | bytes 1572872 | tf_op jit(solution)/shard_map/ppermute | solution.py:170
  38.9 12.4 %collective-permute-start.10 = (f32[8,32,512]{2,1,0:T(8,128)S(1)}, f32[8,32,512]{2,1,0:T(8,128)S(1)}, u32[]{:S(2)}, u32[]{:S(2)}) collective-permute-start(f32[8,32,512]{2,1,0:T(8,128)S(1)} %get-tuple-element.40), channel_id=1, source_target_pairs={{0,1},{1,0},{2,3},{3,2},{4,5},{5,4},{6,7},{7,6},{8,9},{9,8},{10,11... | collective-permute-start | bytes 1572872 | tf_op jit(solution)/shard_map/ppermute | solution.py:170
  39.2 12.4 %collective-permute-start.14 = (f32[8,32,512]{2,1,0:T(8,128)S(1)}, f32[8,32,512]{2,1,0:T(8,128)S(1)}, u32[]{:S(2)}, u32[]{:S(2)}) collective-permute-start(f32[8,32,512]{2,1,0:T(8,128)S(1)} %get-tuple-element.38), channel_id=1, source_target_pairs={{0,28},{1,29},{2,30},{3,31},{4,8},{5,9},{6,10},{7,11},{8,4},{9,5},... | collective-permute-start | bytes 1572872 | tf_op jit(solution)/shard_map/ppermute | solution.py:170
  50.0 7.9 %collective-permute-start.2 = (f32[4,32,512]{2,1,0:T(8,128)S(1)}, f32[4,32,512]{2,1,0:T(8,128)S(1)}, u32[]{:S(2)}, u32[]{:S(2)}) collective-permute-start(f32[4,32,512]{2,1,0:T(8,128)S(1)} %get-tuple-element.52), channel_id=1, source_target_pairs={{0,28},{1,29},{2,30},{3,31},{4,8},{5,9},{6,10},{7,11},{8,4},{9,5},... | collective-permute-start | bytes 786440 | tf_op jit(solution)/shard_map/ppermute | solution.py:170
  51.0 7.0 %collective-permute-start.6 = (f32[4,32,512]{2,1,0:T(8,128)S(1)}, f32[4,32,512]{2,1,0:T(8,128)S(1)}, u32[]{:S(2)}, u32[]{:S(2)}) collective-permute-start(f32[4,32,512]{2,1,0:T(8,128)S(1)} %get-tuple-element.50), channel_id=1, source_target_pairs={{0,1},{1,0},{2,3},{3,2},{4,5},{5,4},{6,7},{7,6},{8,9},{9,8},{10,11... | collective-permute-start | bytes 786440 | tf_op jit(solution)/shard_map/ppermute | solution.py:170
  51.4 8.5 %collective-permute-start.11 = (f32[4,32,512]{2,1,0:T(8,128)S(1)}, f32[4,32,512]{2,1,0:T(8,128)S(1)}, u32[]{:S(2)}, u32[]{:S(2)}) collective-permute-start(f32[4,32,512]{2,1,0:T(8,128)S(1)} %get-tuple-element.48), channel_id=1, source_target_pairs={{0,4},{1,5},{2,6},{3,7},{4,0},{5,1},{6,2},{7,3},{8,12},{9,13},{10,... | collective-permute-start | bytes 786440 | tf_op jit(solution)/shard_map/ppermute | solution.py:170
  51.7 21.2 %copy-start = (f32[2,32,1024]{2,1,0:T(8,128)S(1)}, f32[2,32,1024]{2,1,0:T(8,128)}, u32[]{:S(2)}) copy-start(f32[2,32,1024]{2,1,0:T(8,128)} %refs_7_.1) | copy-start | bytes 786436
  51.7 21.2 %copy-start.1 = (f32[2,1024]{1,0:T(2,128)S(1)}, f32[2,1024]{1,0:T(2,128)}, u32[]{:S(2)}) copy-start(f32[2,1024]{1,0:T(2,128)} %refs_6_.1) | copy-start | bytes 24580
  51.8 10.6 %collective-permute-start.15 = (f32[4,32,512]{2,1,0:T(8,128)S(1)}, f32[4,32,512]{2,1,0:T(8,128)S(1)}, u32[]{:S(2)}, u32[]{:S(2)}) collective-permute-start(f32[4,32,512]{2,1,0:T(8,128)S(1)} %get-tuple-element.46), channel_id=1, source_target_pairs={{0,3},{1,2},{2,1},{3,0},{4,7},{5,6},{6,5},{7,4},{8,11},{9,10},{10,... | collective-permute-start | bytes 786440 | tf_op jit(solution)/shard_map/ppermute | solution.py:170
  57.9 4.7 %collective-permute-start.3 = (f32[2,32,512]{2,1,0:T(8,128)S(1)}, f32[2,32,512]{2,1,0:T(8,128)S(1)}, u32[]{:S(2)}, u32[]{:S(2)}) collective-permute-start(f32[2,32,512]{2,1,0:T(8,128)S(1)} %get-tuple-element.60), channel_id=1, source_target_pairs={{0,4},{1,5},{2,6},{3,7},{4,0},{5,1},{6,2},{7,3},{8,12},{9,13},{10,... | collective-permute-start | bytes 393224 | tf_op jit(solution)/shard_map/ppermute | solution.py:170
  58.1 6.1 %collective-permute-start.7 = (f32[2,32,512]{2,1,0:T(8,128)S(1)}, f32[2,32,512]{2,1,0:T(8,128)S(1)}, u32[]{:S(2)}, u32[]{:S(2)}) collective-permute-start(f32[2,32,512]{2,1,0:T(8,128)S(1)} %get-tuple-element.58), channel_id=1, source_target_pairs={{0,3},{1,2},{2,1},{3,0},{4,7},{5,6},{6,5},{7,4},{8,11},{9,10},{10,... | collective-permute-start | bytes 393224 | tf_op jit(solution)/shard_map/ppermute | solution.py:170
  59.9 7.0 %collective-permute-start.12 = (f32[2,32,512]{2,1,0:T(8,128)S(1)}, f32[2,32,512]{2,1,0:T(8,128)S(1)}, u32[]{:S(2)}, u32[]{:S(2)}) collective-permute-start(f32[2,32,512]{2,1,0:T(8,128)S(1)} %get-tuple-element.56), channel_id=1, source_target_pairs={{0,28},{1,29},{2,30},{3,31},{4,8},{5,9},{6,10},{7,11},{8,4},{9,5},... | collective-permute-start | bytes 393224 | tf_op jit(solution)/shard_map/ppermute | solution.py:170
  62.5 4.5 %collective-permute-start.16 = (f32[2,32,512]{2,1,0:T(8,128)S(1)}, f32[2,32,512]{2,1,0:T(8,128)S(1)}, u32[]{:S(2)}, u32[]{:S(2)}) collective-permute-start(f32[2,32,512]{2,1,0:T(8,128)S(1)} %get-tuple-element.54), channel_id=1, source_target_pairs={{0,1},{1,0},{2,3},{3,2},{4,5},{5,4},{6,7},{7,6},{8,9},{9,8},{10,11... | collective-permute-start | bytes 393224 | tf_op jit(solution)/shard_map/ppermute | solution.py:170
  64.2 7.3 %collective-permute-start.8 = (f32[1,32,1024]{2,1,0:T(8,128)S(1)}, f32[1,32,1024]{2,1,0:T(8,128)S(1)}, u32[]{:S(2)}, u32[]{:S(2)}) collective-permute-start(f32[1,32,1024]{2,1,0:T(8,128)S(1)} %pad_maximum_fusion), channel_id=1, source_target_pairs={{0,20},{1,21},{2,22},{3,23},{4,16},{5,17},{6,18},{7,19},{8,28},{9,... | collective-permute-start | bytes 393224 | tf_op jit(solution)/shard_map/ppermute | solution.py:170
  67.0 5.9 %collective-permute-start.17 = (f32[1,32,1024]{2,1,0:T(8,128)S(1)}, f32[1,32,1024]{2,1,0:T(8,128)S(1)}, u32[]{:S(2)}, u32[]{:S(2)}) collective-permute-start(f32[1,32,1024]{2,1,0:T(8,128)S(1)} %pad_maximum_fusion.1), channel_id=1, source_target_pairs={{0,12},{1,13},{2,14},{3,15},{4,24},{5,25},{6,26},{7,27},{8,20},{9,... | collective-permute-start | bytes 393224 | tf_op jit(solution)/shard_map/ppermute | solution.py:170
  74.0 19.5 %all-to-all-start = ((f32[32,8,128]{2,1,0:T(8,128)}), f32[32,8,128]{2,1,0:T(8,128)S(1)}, u32[]{:S(2)}, u32[]{:S(2)}) async-start(f32[32,8,128]{2,1,0:T(8,128)} %get-tuple-element.31), calls=%async_computation | async-start | bytes 262144 | tf_op jit(solution)/shard_map/all_to_all | solution.py:320
  93.6 5.7 %collective-permute-start.18 = (f32[8,128]{1,0:T(8,128)S(1)}, f32[8,128]{1,0:T(8,128)S(1)}, u32[]{:S(2)}, u32[]{:S(2)}) collective-permute-start(f32[8,128]{1,0:T(8,128)S(1)} %group.1.own_ref), channel_id=1, source_target_pairs={{0,32},{32,0},{64,96},{96,64},{128,160},{160,128},{192,224},{224,1... | collective-permute-start | bytes 12296 | tf_op jit(solution)/shard_map/ppermute | solution.py:179
  99.3 2.5 %collective-permute-start.19 = (f32[8,128]{1,0:T(8,128)S(1)}, f32[8,128]{1,0:T(8,128)S(1)}, u32[]{:S(2)}, u32[]{:S(2)}) collective-permute-start(f32[8,128]{1,0:T(8,128)S(1)} %add.134), channel_id=1, source_target_pairs={{0,64},{32,96},{64,0},{96,32},{128,192},{160,224},{192,128},{224,1... | collective-permute-start | bytes 12296 | tf_op jit(solution)/shard_map/ppermute | solution.py:179
  101.8 3.9 %collective-permute-start.20 = (f32[8,128]{1,0:T(8,128)S(1)}, f32[8,128]{1,0:T(8,128)S(1)}, u32[]{:S(2)}, u32[]{:S(2)}) collective-permute-start(f32[8,128]{1,0:T(8,128)S(1)} %add.135.near_ref), channel_id=1, source_target_pairs={{0,192},{32,224},{64,128},{96,160},{128,64},{160,96},{192,0},{224,... | collective-permute-start | bytes 12296 | tf_op jit(solution)/shard_map/ppermute | solution.py:179

commit v7 on v6

--- a/solution.py
+++ b/solution.py
@@ -12,7 +12,7 @@
 NY = 4
 R = 32
 LEAF = 1024
-PARTS = (("x", 0, 512, 0), ("z", 512, 512, 0), ("x", 0, 512, 1), ("z", 512, 512, 1))
+PARTS = (("x", 0, 512, 0), ("z", 512, 512, 0), ("z", 512, 512, 1), ("x", 0, 512, 1))
 STEPS = {
     "x": (("x", 0), ("x", 1), ("z", 0), ("z", 1)),
     "z": (("z", 0), ("z", 1), ("x", 0), ("x", 1)),
@@ -174,25 +174,24 @@
     pairs = []
     for g in range(2 * NY):
         y, core = g // 2, g % 2
-        to = (g ^ 1, 2 * (y ^ 1) + core, 2 * (y ^ 3) + core)[step]
+        to = (g ^ 1, 2 * (y ^ 3) + core, 2 * (y ^ 1) + core)[step]
         pairs.append((g, to))
     return lax.ppermute(value, "grp", pairs)
 
 
 def scatter_sums(parts):
-    kept, last = [], []
+    kept, last = {}, {}
     for (first, _, _, which), (keep, send) in zip(PARTS, parts):
         for axis, step in STEPS[first]:
             got = exchange(send, axis, step, which)
             half = keep.shape[0] // 2
             send = keep[half:] + got[half:]
             keep = keep[:half] + got[:half]
-        kept.append(keep[0])
-        last.append(send)
+        kept[first, which], last[first, which] = keep[0], send
     terms = []
-    for i in range(0, len(PARTS), 2):
-        got = exchange(jnp.concatenate(last[i : i + 2], axis=2), "z", 2, PARTS[i][3])
-        terms += kept[i : i + 2] + [got[0]]
+    for which in range(2):
+        got = exchange(jnp.concatenate([last["x", which], last["z", which]], axis=2), "z", 2, which)
+        terms += [kept["x", which], kept["z", which], got[0]]
     return terms
 
 
@@ -237,9 +236,9 @@
 
 def sample_kernel(*refs):
     terms, (diag_ref, sketch_ref, sample_ref, gram_ref, packed_ref) = refs[:-5], refs[-5:]
-    for k, (_, start, width, which) in enumerate(PARTS):
+    for first, start, width, which in PARTS:
         columns = slice(start, start + width)
-        far = terms[k // 2 * 3 + k % 2][...] + terms[k // 2 * 3 + 2][:, columns]
+        far = terms[3 * which + (first == "z")][...] + terms[3 * which + 2][:, columns]
         near = diag_ref[which : which + 1, columns] * sketch_ref[which, :, columns]
         sample_ref[which, :, columns] = far + near
     total = jnp.zeros((R, R), jnp.float32)

time: 108 us -> 108 us (level)
  transfers between devices with their start and end apart: 22 -> 22, of which waited for: 12 -> 13; matrix products, arithmetic and copies ran while one was open for 1% -> 1% of each run, Pallas kernels for 3% -> 3%
where the time goes in v7:
time: 108 us; the launch traced here: 107 us
  waiting for transfers between devices  48.1 us (45%)
  starting transfers between devices  44.5 us (41%)
  Pallas kernels  12.1 us (11%)
  other arithmetic  1.41 us (1%)
    ppermute x18, waiting for transfers between devices, exchange(): return lax.ppermute(value, 'dev', pairs)  38.1 us
    ppermute x18, starting transfers between devices, exchange(): return lax.ppermute(value, 'dev', pairs)  27.4 us
    all_to_all x1, starting transfers between devices, body(): lax.all_to_all(packed, 'dev', split_axis=0, concat_axis=0, tiled=True)  9.77 us
    ppermute x3, starting transfers between devices, across(): return lax.ppermute(value, 'grp', pairs)  7.39 us
    all_to_all x1, waiting for transfers between devices, body(): lax.all_to_all(packed, 'dev', split_axis=0, concat_axis=0, tiled=True)  7.31 us
    pallas_call x1, Pallas kernels, contributions(): pl.pallas_call(contribution_kernel, out_shape=shapes, in_specs=[pl.BlockS...  5.75 us
    ppermute x3, waiting for transfers between devices, across(): return lax.ppermute(value, 'grp', pairs)  2.68 us
  transfers between devices with their start and end apart: 22, of which 13 were waited for; matrix products, arithmetic and copies ran while one was open for 1% of the time, Pallas kernels for 3%

profile of v7, /device:TPU:1, one launch (start us, length us, event | category | flops | bytes accessed | tf_op | source)
XLA Modules:
  0.0 107.0 jit_solution(10279797738032356610)
XLA Ops:
  0.6 5.7 %contributions.1 = (f32[16,32,512]{2,1,0:T(8,128)S(1)}, f32[16,32,512]{2,1,0:T(8,128)S(1)}, f32[16,32,512]{2,1,0:T(8,128)S(1)}, f32[16,32,512]{2,1,0:T(8,128)S(1...) custom-call(s32[24]{0:T(128)} %rows_hbm.1, ...), custom_call_target="tpu_custom_call" | custom-call | flops 1000000000 | bytes 16777216 | tf_op jit(solution)/shard_map/contributions/pallas_call | solution.py:141
  6.4 2.1 %collective-permute-start = (f32[16,32,512]{2,1,0:T(8,128)S(1)}, f32[16,32,512]{2,1,0:T(8,128)S(1)}, u32[]{:S(2)}, u32[]{:S(2)}) collective-permute-start(f32[16,32,512]{2,1,0:T(8,128)S(1)} %get-tuple-element.21), channel_id=1, source_target_pairs={{0,1},{1,0},{2,3},{3,2},{4,5},{5,4},{6,7},{7,6},{8,9},{9,8},{10,11... | collective-permute-start | bytes 3145736 | tf_op jit(solution)/shard_map/ppermute | solution.py:170
  8.5 5.6 %collective-permute-start.4 = (f32[16,32,512]{2,1,0:T(8,128)S(1)}, f32[16,32,512]{2,1,0:T(8,128)S(1)}, u32[]{:S(2)}, u32[]{:S(2)}) collective-permute-start(f32[16,32,512]{2,1,0:T(8,128)S(1)} %get-tuple-element.23), channel_id=1, source_target_pairs={{0,28},{1,29},{2,30},{3,31},{4,8},{5,9},{6,10},{7,11},{8,4},{9,5},... | collective-permute-start | bytes 3145736 | tf_op jit(solution)/shard_map/ppermute | solution.py:170
  14.1 1.8 %collective-permute-start.9 = (f32[16,32,512]{2,1,0:T(8,128)S(1)}, f32[16,32,512]{2,1,0:T(8,128)S(1)}, u32[]{:S(2)}, u32[]{:S(2)}) collective-permute-start(f32[16,32,512]{2,1,0:T(8,128)S(1)} %get-tuple-element.25), channel_id=1, source_target_pairs={{0,3},{1,2},{2,1},{3,0},{4,7},{5,6},{6,5},{7,4},{8,11},{9,10},{10,... | collective-permute-start | bytes 3145736 | tf_op jit(solution)/shard_map/ppermute | solution.py:170
  15.9 14.1 %collective-permute-done = f32[16,32,512]{2,1,0:T(8,128)S(1)} collective-permute-done((f32[16,32,512]{2,1,0:T(8,128)S(1)}, f32[16,32,512]{2,1,0:T(8,128)S(1)}, u32[]{:S(2)}, u32[]{:S(2)}) %collective-permute-start) | collective-permute-done | bytes 1048608 | tf_op jit(solution)/shard_map/ppermute | solution.py:170
  30.2 3.9 %collective-permute-start.1 = (f32[8,32,512]{2,1,0:T(8,128)S(1)}, f32[8,32,512]{2,1,0:T(8,128)S(1)}, u32[]{:S(2)}, u32[]{:S(2)}) collective-permute-start(f32[8,32,512]{2,1,0:T(8,128)S(1)} %get-tuple-element.44), channel_id=1, source_target_pairs={{0,3},{1,2},{2,1},{3,0},{4,7},{5,6},{6,5},{7,4},{8,11},{9,10},{10,... | collective-permute-start | bytes 1572872 | tf_op jit(solution)/shard_map/ppermute | solution.py:170
  34.1 2.5 %collective-permute-done.4 = f32[16,32,512]{2,1,0:T(8,128)S(1)} collective-permute-done((f32[16,32,512]{2,1,0:T(8,128)S(1)}, f32[16,32,512]{2,1,0:T(8,128)S(1)}, u32[]{:S(2)}, u32[]{:S(2)}) %collective-permute-start.4) | collective-permute-done | bytes 1048608 | tf_op jit(solution)/shard_map/ppermute | solution.py:170
  36.9 1.8 %collective-permute-done.9 = f32[16,32,512]{2,1,0:T(8,128)S(1)} collective-permute-done((f32[16,32,512]{2,1,0:T(8,128)S(1)}, f32[16,32,512]{2,1,0:T(8,128)S(1)}, u32[]{:S(2)}, u32[]{:S(2)}) %collective-permute-start.9) | collective-permute-done | bytes 1048608 | tf_op jit(solution)/shard_map/ppermute | solution.py:170
  39.2 2.1 %collective-permute-start.14 = (f32[8,32,512]{2,1,0:T(8,128)S(1)}, f32[8,32,512]{2,1,0:T(8,128)S(1)}, u32[]{:S(2)}, u32[]{:S(2)}) collective-permute-start(f32[8,32,512]{2,1,0:T(8,128)S(1)} %get-tuple-element.38), channel_id=1, source_target_pairs={{0,28},{1,29},{2,30},{3,31},{4,8},{5,9},{6,10},{7,11},{8,4},{9,5},... | collective-permute-start | bytes 1572872 | tf_op jit(solution)/shard_map/ppermute | solution.py:170
  41.3 8.6 %collective-permute-done.1 = f32[8,32,512]{2,1,0:T(8,128)S(1)} collective-permute-done((f32[8,32,512]{2,1,0:T(8,128)S(1)}, f32[8,32,512]{2,1,0:T(8,128)S(1)}, u32[]{:S(2)}, u32[]{:S(2)}) %collective-permute-start.1) | collective-permute-done | bytes 524320 | tf_op jit(solution)/shard_map/ppermute | solution.py:170
  51.8 1.8 %collective-permute-start.15 = (f32[4,32,512]{2,1,0:T(8,128)S(1)}, f32[4,32,512]{2,1,0:T(8,128)S(1)}, u32[]{:S(2)}, u32[]{:S(2)}) collective-permute-start(f32[4,32,512]{2,1,0:T(8,128)S(1)} %get-tuple-element.46), channel_id=1, source_target_pairs={{0,3},{1,2},{2,1},{3,0},{4,7},{5,6},{6,5},{7,4},{8,11},{9,10},{10,... | collective-permute-start | bytes 786440 | tf_op jit(solution)/shard_map/ppermute | solution.py:170
  53.6 4.2 %collective-permute-done.2 = f32[4,32,512]{2,1,0:T(8,128)S(1)} collective-permute-done((f32[4,32,512]{2,1,0:T(8,128)S(1)}, f32[4,32,512]{2,1,0:T(8,128)S(1)}, u32[]{:S(2)}, u32[]{:S(2)}) %collective-permute-start.2) | collective-permute-done | bytes 262176 | tf_op jit(solution)/shard_map/ppermute | solution.py:170
  58.1 1.9 %collective-permute-start.7 = (f32[2,32,512]{2,1,0:T(8,128)S(1)}, f32[2,32,512]{2,1,0:T(8,128)S(1)}, u32[]{:S(2)}, u32[]{:S(2)}) collective-permute-start(f32[2,32,512]{2,1,0:T(8,128)S(1)} %get-tuple-element.58), channel_id=1, source_target_pairs={{0,3},{1,2},{2,1},{3,0},{4,7},{5,6},{6,5},{7,4},{8,11},{9,10},{10,... | collective-permute-start | bytes 393224 | tf_op jit(solution)/shard_map/ppermute | solution.py:170
  60.0 2.3 %collective-permute-start.12 = (f32[2,32,512]{2,1,0:T(8,128)S(1)}, f32[2,32,512]{2,1,0:T(8,128)S(1)}, u32[]{:S(2)}, u32[]{:S(2)}) collective-permute-start(f32[2,32,512]{2,1,0:T(8,128)S(1)} %get-tuple-element.56), channel_id=1, source_target_pairs={{0,28},{1,29},{2,30},{3,31},{4,8},{5,9},{6,10},{7,11},{8,4},{9,5},... | collective-permute-start | bytes 393224 | tf_op jit(solution)/shard_map/ppermute | solution.py:170
  62.5 1.6 %collective-permute-done.7 = f32[2,32,512]{2,1,0:T(8,128)S(1)} collective-permute-done((f32[2,32,512]{2,1,0:T(8,128)S(1)}, f32[2,32,512]{2,1,0:T(8,128)S(1)}, u32[]{:S(2)}, u32[]{:S(2)}) %collective-permute-start.7) | collective-permute-done | bytes 131104 | tf_op jit(solution)/shard_map/ppermute | solution.py:170
  64.2 3.1 %collective-permute-start.8 = (f32[1,32,1024]{2,1,0:T(8,128)S(1)}, f32[1,32,1024]{2,1,0:T(8,128)S(1)}, u32[]{:S(2)}, u32[]{:S(2)}) collective-permute-start(f32[1,32,1024]{2,1,0:T(8,128)S(1)} %pad_maximum_fusion), channel_id=1, source_target_pairs={{0,20},{1,21},{2,22},{3,23},{4,16},{5,17},{6,18},{7,19},{8,28},{9,... | collective-permute-start | bytes 393224 | tf_op jit(solution)/shard_map/ppermute | solution.py:170
  68.9 2.5 %collective-permute-done.8 = f32[1,32,1024]{2,1,0:T(8,128)S(1)} collective-permute-done((f32[1,32,1024]{2,1,0:T(8,128)S(1)}, f32[1,32,1024]{2,1,0:T(8,128)S(1)}, u32[]{:S(2)}, u32[]{:S(2)}) %collective-permute-start.8) | collective-permute-done | bytes 131104 | tf_op jit(solution)/shard_map/ppermute | solution.py:170
  71.4 2.1 %collective-permute-done.17 = f32[1,32,1024]{2,1,0:T(8,128)S(1)} collective-permute-done((f32[1,32,1024]{2,1,0:T(8,128)S(1)}, f32[1,32,1024]{2,1,0:T(8,128)S(1)}, u32[]{:S(2)}, u32[]{:S(2)}) %collective-permute-start.17) | collective-permute-done | bytes 131104 | tf_op jit(solution)/shard_map/ppermute | solution.py:170
  74.6 9.8 %all-to-all-start = ((f32[32,8,128]{2,1,0:T(8,128)}), f32[32,8,128]{2,1,0:T(8,128)S(1)}, u32[]{:S(2)}, u32[]{:S(2)}) async-start(f32[32,8,128]{2,1,0:T(8,128)} %get-tuple-element.31), calls=%async_computation | async-start | bytes 262144 | tf_op jit(solution)/shard_map/all_to_all | solution.py:319
  84.4 2.0 %leaf.1 = (f32[2,32,1024]{2,1,0:T(8,128)}, f32[2,32,32]{2,1,0:T(8,128)S(1)}) custom-call(f32[2,32,32]{2,1,0:T(8,128)S(1)} %get-tuple-element.28.gram_ref, f32[2,32,1024]{2,1,0:T(8,128)S(1)} %get-tuple-element.29.sample_ref), custom_call_target="tpu_custom_call" | custom-call | tf_op jit(solution)/shard_map/leaf/pallas_call | solution.py:320
  86.4 7.3 %all-to-all-done.every_ref = f32[32,8,128]{2,1,0:T(8,128)S(1)} async-done(((f32[32,8,128]{2,1,0:T(8,128)}), f32[32,8,128]{2,1,0:T(8,128)S(1)}, u32[]{:S(2)}, u32[]{:S(2)}) %all-to-all-start) | async-done | bytes 131104 | tf_op jit(solution)/shard_map/all_to_all | solution.py:319
  93.8 3.9 %collective-permute-start.18 = (f32[8,128]{1,0:T(8,128)S(1)}, f32[8,128]{1,0:T(8,128)S(1)}, u32[]{:S(2)}, u32[]{:S(2)}) collective-permute-start(f32[8,128]{1,0:T(8,128)S(1)} %group.1.own_ref), channel_id=1, source_target_pairs={{0,32},{32,0},{64,96},{96,64},{128,160},{160,128},{192,224},{224,1... | collective-permute-start | bytes 12296 | tf_op jit(solution)/shard_map/ppermute | solution.py:179
  98.5 3.5 %collective-permute-start.19 = (f32[8,128]{1,0:T(8,128)S(1)}, f32[8,128]{1,0:T(8,128)S(1)}, u32[]{:S(2)}, u32[]{:S(2)}) collective-permute-start(f32[8,128]{1,0:T(8,128)S(1)} %add.134), channel_id=1, source_target_pairs={{0,192},{32,224},{64,128},{96,160},{128,64},{160,96},{192,0},{224,... | collective-permute-start | bytes 12296 | tf_op jit(solution)/shard_map/ppermute | solution.py:179
  103.0 1.6 %transfer_leaf.1 = (f32[2,32,32]{2,1,0:T(8,128)}, f32[32,32]{1,0:T(8,128)S(1)}) custom-call(f32[8,128]{1,0:T(8,128)S(1)} %group.1.own_ref, f32[2,32,32]{2,1,0:T(8,128)S(1)} %get-tuple-element.34.upper_ref), custom_call_target="tpu_custom_call" | custom-call | tf_op jit(solution)/shard_map/transfer_leaf/pallas_call | solution.py:342
  (50 shorter events, 10.3 us)
Async XLA Ops:
  6.4 23.6 %collective-permute-start = (f32[16,32,512]{2,1,0:T(8,128)S(1)}, f32[16,32,512]{2,1,0:T(8,128)S(1)}, u32[]{:S(2)}, u32[]{:S(2)}) collective-permute-start(f32[16,32,512]{2,1,0:T(8,128)S(1)} %get-tuple-element.21), channel_id=1, source_target_pairs={{0,1},{1,0},{2,3},{3,2},{4,5},{5,4},{6,7},{7,6},{8,9},{9,8},{10,11... | collective-permute-start | bytes 3145736 | tf_op jit(solution)/shard_map/ppermute | solution.py:170
  8.5 28.1 %collective-permute-start.4 = (f32[16,32,512]{2,1,0:T(8,128)S(1)}, f32[16,32,512]{2,1,0:T(8,128)S(1)}, u32[]{:S(2)}, u32[]{:S(2)}) collective-permute-start(f32[16,32,512]{2,1,0:T(8,128)S(1)} %get-tuple-element.23), channel_id=1, source_target_pairs={{0,28},{1,29},{2,30},{3,31},{4,8},{5,9},{6,10},{7,11},{8,4},{9,5},... | collective-permute-start | bytes 3145736 | tf_op jit(solution)/shard_map/ppermute | solution.py:170
  14.1 24.6 %collective-permute-start.9 = (f32[16,32,512]{2,1,0:T(8,128)S(1)}, f32[16,32,512]{2,1,0:T(8,128)S(1)}, u32[]{:S(2)}, u32[]{:S(2)}) collective-permute-start(f32[16,32,512]{2,1,0:T(8,128)S(1)} %get-tuple-element.25), channel_id=1, source_target_pairs={{0,3},{1,2},{2,1},{3,0},{4,7},{5,6},{6,5},{7,4},{8,11},{9,10},{10,... | collective-permute-start | bytes 3145736 | tf_op jit(solution)/shard_map/ppermute | solution.py:170
  15.9 23.1 %collective-permute-start.13 = (f32[16,32,512]{2,1,0:T(8,128)S(1)}, f32[16,32,512]{2,1,0:T(8,128)S(1)}, u32[]{:S(2)}, u32[]{:S(2)}) collective-permute-start(f32[16,32,512]{2,1,0:T(8,128)S(1)} %get-tuple-element.27), channel_id=1, source_target_pairs={{0,4},{1,5},{2,6},{3,7},{4,0},{5,1},{6,2},{7,3},{8,12},{9,13},{10,... | collective-permute-start | bytes 3145736 | tf_op jit(solution)/shard_map/ppermute | solution.py:170
  30.2 19.7 %collective-permute-start.1 = (f32[8,32,512]{2,1,0:T(8,128)S(1)}, f32[8,32,512]{2,1,0:T(8,128)S(1)}, u32[]{:S(2)}, u32[]{:S(2)}) collective-permute-start(f32[8,32,512]{2,1,0:T(8,128)S(1)} %get-tuple-element.44), channel_id=1, source_target_pairs={{0,3},{1,2},{2,1},{3,0},{4,7},{5,6},{6,5},{7,4},{8,11},{9,10},{10,... | collective-permute-start | bytes 1572872 | tf_op jit(solution)/shard_map/ppermute | solution.py:170
  36.8 14.1 %collective-permute-start.5 = (f32[8,32,512]{2,1,0:T(8,128)S(1)}, f32[8,32,512]{2,1,0:T(8,128)S(1)}, u32[]{:S(2)}, u32[]{:S(2)}) collective-permute-start(f32[8,32,512]{2,1,0:T(8,128)S(1)} %get-tuple-element.42), channel_id=1, source_target_pairs={{0,4},{1,5},{2,6},{3,7},{4,0},{5,1},{6,2},{7,3},{8,12},{9,13},{10,... | collective-permute-start | bytes 1572872 | tf_op jit(solution)/shard_map/ppermute | solution.py:170
  38.9 12.4 %collective-permute-start.10 = (f32[8,32,512]{2,1,0:T(8,128)S(1)}, f32[8,32,512]{2,1,0:T(8,128)S(1)}, u32[]{:S(2)}, u32[]{:S(2)}) collective-permute-start(f32[8,32,512]{2,1,0:T(8,128)S(1)} %get-tuple-element.40), channel_id=1, source_target_pairs={{0,1},{1,0},{2,3},{3,2},{4,5},{5,4},{6,7},{7,6},{8,9},{9,8},{10,11... | collective-permute-start | bytes 1572872 | tf_op jit(solution)/shard_map/ppermute | solution.py:170
  39.2 12.4 %collective-permute-start.14 = (f32[8,32,512]{2,1,0:T(8,128)S(1)}, f32[8,32,512]{2,1,0:T(8,128)S(1)}, u32[]{:S(2)}, u32[]{:S(2)}) collective-permute-start(f32[8,32,512]{2,1,0:T(8,128)S(1)} %get-tuple-element.38), channel_id=1, source_target_pairs={{0,28},{1,29},{2,30},{3,31},{4,8},{5,9},{6,10},{7,11},{8,4},{9,5},... | collective-permute-start | bytes 1572872 | tf_op jit(solution)/shard_map/ppermute | solution.py:170
  50.0 7.9 %collective-permute-start.2 = (f32[4,32,512]{2,1,0:T(8,128)S(1)}, f32[4,32,512]{2,1,0:T(8,128)S(1)}, u32[]{:S(2)}, u32[]{:S(2)}) collective-permute-start(f32[4,32,512]{2,1,0:T(8,128)S(1)} %get-tuple-element.52), channel_id=1, source_target_pairs={{0,28},{1,29},{2,30},{3,31},{4,8},{5,9},{6,10},{7,11},{8,4},{9,5},... | collective-permute-start | bytes 786440 | tf_op jit(solution)/shard_map/ppermute | solution.py:170
  51.0 7.0 %collective-permute-start.6 = (f32[4,32,512]{2,1,0:T(8,128)S(1)}, f32[4,32,512]{2,1,0:T(8,128)S(1)}, u32[]{:S(2)}, u32[]{:S(2)}) collective-permute-start(f32[4,32,512]{2,1,0:T(8,128)S(1)} %get-tuple-element.50), channel_id=1, source_target_pairs={{0,1},{1,0},{2,3},{3,2},{4,5},{5,4},{6,7},{7,6},{8,9},{9,8},{10,11... | collective-permute-start | bytes 786440 | tf_op jit(solution)/shard_map/ppermute | solution.py:170
  51.4 8.6 %collective-permute-start.11 = (f32[4,32,512]{2,1,0:T(8,128)S(1)}, f32[4,32,512]{2,1,0:T(8,128)S(1)}, u32[]{:S(2)}, u32[]{:S(2)}) collective-permute-start(f32[4,32,512]{2,1,0:T(8,128)S(1)} %get-tuple-element.48), channel_id=1, source_target_pairs={{0,4},{1,5},{2,6},{3,7},{4,0},{5,1},{6,2},{7,3},{8,12},{9,13},{10,... | collective-permute-start | bytes 786440 | tf_op jit(solution)/shard_map/ppermute | solution.py:170
  51.7 21.8 %copy-start = (f32[2,32,1024]{2,1,0:T(8,128)S(1)}, f32[2,32,1024]{2,1,0:T(8,128)}, u32[]{:S(2)}) copy-start(f32[2,32,1024]{2,1,0:T(8,128)} %refs_7_.1) | copy-start | bytes 786436
  51.7 21.8 %copy-start.1 = (f32[2,1024]{1,0:T(2,128)S(1)}, f32[2,1024]{1,0:T(2,128)}, u32[]{:S(2)}) copy-start(f32[2,1024]{1,0:T(2,128)} %refs_6_.1) | copy-start | bytes 24580
  51.8 10.6 %collective-permute-start.15 = (f32[4,32,512]{2,1,0:T(8,128)S(1)}, f32[4,32,512]{2,1,0:T(8,128)S(1)}, u32[]{:S(2)}, u32[]{:S(2)}) collective-permute-start(f32[4,32,512]{2,1,0:T(8,128)S(1)} %get-tuple-element.46), channel_id=1, source_target_pairs={{0,3},{1,2},{2,1},{3,0},{4,7},{5,6},{6,5},{7,4},{8,11},{9,10},{10,... | collective-permute-start | bytes 786440 | tf_op jit(solution)/shard_map/ppermute | solution.py:170
  57.9 4.6 %collective-permute-start.3 = (f32[2,32,512]{2,1,0:T(8,128)S(1)}, f32[2,32,512]{2,1,0:T(8,128)S(1)}, u32[]{:S(2)}, u32[]{:S(2)}) collective-permute-start(f32[2,32,512]{2,1,0:T(8,128)S(1)} %get-tuple-element.60), channel_id=1, source_target_pairs={{0,4},{1,5},{2,6},{3,7},{4,0},{5,1},{6,2},{7,3},{8,12},{9,13},{10,... | collective-permute-start | bytes 393224 | tf_op jit(solution)/shard_map/ppermute | solution.py:170
  58.1 6.1 %collective-permute-start.7 = (f32[2,32,512]{2,1,0:T(8,128)S(1)}, f32[2,32,512]{2,1,0:T(8,128)S(1)}, u32[]{:S(2)}, u32[]{:S(2)}) collective-permute-start(f32[2,32,512]{2,1,0:T(8,128)S(1)} %get-tuple-element.58), channel_id=1, source_target_pairs={{0,3},{1,2},{2,1},{3,0},{4,7},{5,6},{6,5},{7,4},{8,11},{9,10},{10,... | collective-permute-start | bytes 393224 | tf_op jit(solution)/shard_map/ppermute | solution.py:170
  60.0 7.2 %collective-permute-start.12 = (f32[2,32,512]{2,1,0:T(8,128)S(1)}, f32[2,32,512]{2,1,0:T(8,128)S(1)}, u32[]{:S(2)}, u32[]{:S(2)}) collective-permute-start(f32[2,32,512]{2,1,0:T(8,128)S(1)} %get-tuple-element.56), channel_id=1, source_target_pairs={{0,28},{1,29},{2,30},{3,31},{4,8},{5,9},{6,10},{7,11},{8,4},{9,5},... | collective-permute-start | bytes 393224 | tf_op jit(solution)/shard_map/ppermute | solution.py:170
  62.4 4.9 %collective-permute-start.16 = (f32[2,32,512]{2,1,0:T(8,128)S(1)}, f32[2,32,512]{2,1,0:T(8,128)S(1)}, u32[]{:S(2)}, u32[]{:S(2)}) collective-permute-start(f32[2,32,512]{2,1,0:T(8,128)S(1)} %get-tuple-element.54), channel_id=1, source_target_pairs={{0,1},{1,0},{2,3},{3,2},{4,5},{5,4},{6,7},{7,6},{8,9},{9,8},{10,11... | collective-permute-start | bytes 393224 | tf_op jit(solution)/shard_map/ppermute | solution.py:170
  64.2 7.3 %collective-permute-start.8 = (f32[1,32,1024]{2,1,0:T(8,128)S(1)}, f32[1,32,1024]{2,1,0:T(8,128)S(1)}, u32[]{:S(2)}, u32[]{:S(2)}) collective-permute-start(f32[1,32,1024]{2,1,0:T(8,128)S(1)} %pad_maximum_fusion), channel_id=1, source_target_pairs={{0,20},{1,21},{2,22},{3,23},{4,16},{5,17},{6,18},{7,19},{8,28},{9,... | collective-permute-start | bytes 393224 | tf_op jit(solution)/shard_map/ppermute | solution.py:170
  67.3 6.2 %collective-permute-start.17 = (f32[1,32,1024]{2,1,0:T(8,128)S(1)}, f32[1,32,1024]{2,1,0:T(8,128)S(1)}, u32[]{:S(2)}, u32[]{:S(2)}) collective-permute-start(f32[1,32,1024]{2,1,0:T(8,128)S(1)} %pad_maximum_fusion.1), channel_id=1, source_target_pairs={{0,12},{1,13},{2,14},{3,15},{4,24},{5,25},{6,26},{7,27},{8,20},{9,... | collective-permute-start | bytes 393224 | tf_op jit(solution)/shard_map/ppermute | solution.py:170
  74.6 19.1 %all-to-all-start = ((f32[32,8,128]{2,1,0:T(8,128)}), f32[32,8,128]{2,1,0:T(8,128)S(1)}, u32[]{:S(2)}, u32[]{:S(2)}) async-start(f32[32,8,128]{2,1,0:T(8,128)} %get-tuple-element.31), calls=%async_computation | async-start | bytes 262144 | tf_op jit(solution)/shard_map/all_to_all | solution.py:319
  93.8 4.8 %collective-permute-start.18 = (f32[8,128]{1,0:T(8,128)S(1)}, f32[8,128]{1,0:T(8,128)S(1)}, u32[]{:S(2)}, u32[]{:S(2)}) collective-permute-start(f32[8,128]{1,0:T(8,128)S(1)} %group.1.own_ref), channel_id=1, source_target_pairs={{0,32},{32,0},{64,96},{96,64},{128,160},{160,128},{192,224},{224,1... | collective-permute-start | bytes 12296 | tf_op jit(solution)/shard_map/ppermute | solution.py:179
  98.5 4.5 %collective-permute-start.19 = (f32[8,128]{1,0:T(8,128)S(1)}, f32[8,128]{1,0:T(8,128)S(1)}, u32[]{:S(2)}, u32[]{:S(2)}) collective-permute-start(f32[8,128]{1,0:T(8,128)S(1)} %add.134), channel_id=1, source_target_pairs={{0,192},{32,224},{64,128},{96,160},{128,64},{160,96},{192,0},{224,... | collective-permute-start | bytes 12296 | tf_op jit(solution)/shard_map/ppermute | solution.py:179
  103.0 2.5 %collective-permute-start.20 = (f32[8,128]{1,0:T(8,128)S(1)}, f32[8,128]{1,0:T(8,128)S(1)}, u32[]{:S(2)}, u32[]{:S(2)}) collective-permute-start(f32[8,128]{1,0:T(8,128)S(1)} %add.135.near_ref), channel_id=1, source_target_pairs={{0,64},{32,96},{64,0},{96,32},{128,192},{160,224},{192,128},{224,1... | collective-permute-start | bytes 12296 | tf_op jit(solution)/shard_map/ppermute | solution.py:179

commit v8 on v6

--- a/solution.py
+++ b/solution.py
@@ -100,14 +100,16 @@
             cluster = row & 1
             live = slot < live_count
             own_w = (me // NX - 1 + cluster) & (NZ - 1)
-            own_q = (me % NX - cluster) & (NX - 1)
             to_w = ((row >> 3) - 1 + cluster) & (NZ - 1)
-            to_q = (((row >> 1) & (NX - 1)) - cluster) & (NX - 1)
             step_z = jnp.where(own_w & 1 == 0, to_w - own_w, own_w - to_w) & (NZ - 1)
-            x_slot, z_slot = lookup(X_ORDER, own_q ^ to_q), lookup(Z_ORDER, step_z)
+            z_slot = lookup(Z_ORDER, step_z)
+            x_slot, x_late = (
+                lookup(X_ORDER, ((me - colour) & (NX - 1)) ^ (((row >> 1) - colour) & (NX - 1)))
+                for colour in (cluster, 1 - cluster)
+            )
             index = {
                 "x": x_slot * NZ + z_slot,
-                "z": (z_slot >> 1) * 2 * NX + x_slot * 2 + (z_slot & 1),
+                "z": (z_slot >> 1) * 2 * NX + x_late * 2 + (z_slot & 1),
             }
             for k, (axis, start, width, which) in enumerate(PARTS):
                 for far in range(2):
@@ -183,7 +185,8 @@
     kept, last = [], []
     for (first, _, _, which), (keep, send) in zip(PARTS, parts):
         for axis, step in STEPS[first]:
-            got = exchange(send, axis, step, which)
+            late = first == "z" and axis == "x"
+            got = exchange(send, axis, step, 1 - which if late else which)
             half = keep.shape[0] // 2
             send = keep[half:] + got[half:]
             keep = keep[:half] + got[:half]

time: 108 us -> 108 us (level)
  starting transfers between devices: 45.5 us -> 43.3 us
  waiting for transfers between devices: 47.4 us -> 49.2 us
    all_to_all x1, starting transfers between devices: 10.2 us -> 7.26 us  [body(): lax.all_to_all(packed, 'dev', split_axis=0, concat_axis=0, tiled=True)]
    ppermute x18, waiting for transfers between devices: 37.3 us -> 39.9 us  [exchange(): return lax.ppermute(value, 'dev', pairs)]
  transfers between devices with their start and end apart: 22 -> 22, of which waited for: 12 -> 13; matrix products, arithmetic and copies ran while one was open for 1% -> 1% of each run, Pallas kernels for 3% -> 3%
where the time goes in v8:
time: 108 us; the launch traced here: 107 us
  waiting for transfers between devices  49.2 us (46%)
  starting transfers between devices  43.3 us (40%)
  Pallas kernels  12.1 us (11%)
  other arithmetic  1.4 us (1%)
    ppermute x18, waiting for transfers between devices, exchange(): return lax.ppermute(value, 'dev', pairs)  39.9 us
    ppermute x18, starting transfers between devices, exchange(): return lax.ppermute(value, 'dev', pairs)  28 us
    ppermute x3, starting transfers between devices, across(): return lax.ppermute(value, 'grp', pairs)  8.02 us
    all_to_all x1, waiting for transfers between devices, body(): lax.all_to_all(packed, 'dev', split_axis=0, concat_axis=0, tiled=True)  7.3 us
    all_to_all x1, starting transfers between devices, body(): lax.all_to_all(packed, 'dev', split_axis=0, concat_axis=0, tiled=True)  7.26 us
    pallas_call x1, Pallas kernels, contributions(): pl.pallas_call(contribution_kernel, out_shape=shapes, in_specs=[pl.BlockS...  5.83 us
  transfers between devices with their start and end apart: 22, of which 13 were waited for; matrix products, arithmetic and copies ran while one was open for 1% of the time, Pallas kernels for 3%

profile of v8, /device:TPU:1, one launch (start us, length us, event | category | flops | bytes accessed | tf_op | source)
XLA Modules:
  0.0 106.9 jit_solution(6798217733773717532)
XLA Ops:
  0.6 5.8 %contributions.1 = (f32[16,32,512]{2,1,0:T(8,128)S(1)}, f32[16,32,512]{2,1,0:T(8,128)S(1)}, f32[16,32,512]{2,1,0:T(8,128)S(1)}, f32[16,32,512]{2,1,0:T(8,128)S(1...) custom-call(s32[24]{0:T(128)} %rows_hbm.1, ...), custom_call_target="tpu_custom_call" | custom-call | flops 1000000000 | bytes 16777216 | tf_op jit(solution)/shard_map/contributions/pallas_call | solution.py:143
  6.5 2.1 %collective-permute-start = (f32[16,32,512]{2,1,0:T(8,128)S(1)}, f32[16,32,512]{2,1,0:T(8,128)S(1)}, u32[]{:S(2)}, u32[]{:S(2)}) collective-permute-start(f32[16,32,512]{2,1,0:T(8,128)S(1)} %get-tuple-element.21), channel_id=1, source_target_pairs={{0,1},{1,0},{2,3},{3,2},{4,5},{5,4},{6,7},{7,6},{8,9},{9,8},{10,11... | collective-permute-start | bytes 3145736 | tf_op jit(solution)/shard_map/ppermute | solution.py:172
  8.6 5.6 %collective-permute-start.4 = (f32[16,32,512]{2,1,0:T(8,128)S(1)}, f32[16,32,512]{2,1,0:T(8,128)S(1)}, u32[]{:S(2)}, u32[]{:S(2)}) collective-permute-start(f32[16,32,512]{2,1,0:T(8,128)S(1)} %get-tuple-element.23), channel_id=1, source_target_pairs={{0,28},{1,29},{2,30},{3,31},{4,8},{5,9},{6,10},{7,11},{8,4},{9,5},... | collective-permute-start | bytes 3145736 | tf_op jit(solution)/shard_map/ppermute | solution.py:172
  14.2 1.8 %collective-permute-start.9 = (f32[16,32,512]{2,1,0:T(8,128)S(1)}, f32[16,32,512]{2,1,0:T(8,128)S(1)}, u32[]{:S(2)}, u32[]{:S(2)}) collective-permute-start(f32[16,32,512]{2,1,0:T(8,128)S(1)} %get-tuple-element.25), channel_id=1, source_target_pairs={{0,3},{1,2},{2,1},{3,0},{4,7},{5,6},{6,5},{7,4},{8,11},{9,10},{10,... | collective-permute-start | bytes 3145736 | tf_op jit(solution)/shard_map/ppermute | solution.py:172
  15.9 14.1 %collective-permute-done = f32[16,32,512]{2,1,0:T(8,128)S(1)} collective-permute-done((f32[16,32,512]{2,1,0:T(8,128)S(1)}, f32[16,32,512]{2,1,0:T(8,128)S(1)}, u32[]{:S(2)}, u32[]{:S(2)}) %collective-permute-start) | collective-permute-done | bytes 1048608 | tf_op jit(solution)/shard_map/ppermute | solution.py:172
  30.3 3.8 %collective-permute-start.1 = (f32[8,32,512]{2,1,0:T(8,128)S(1)}, f32[8,32,512]{2,1,0:T(8,128)S(1)}, u32[]{:S(2)}, u32[]{:S(2)}) collective-permute-start(f32[8,32,512]{2,1,0:T(8,128)S(1)} %get-tuple-element.44), channel_id=1, source_target_pairs={{0,3},{1,2},{2,1},{3,0},{4,7},{5,6},{6,5},{7,4},{8,11},{9,10},{10,... | collective-permute-start | bytes 1572872 | tf_op jit(solution)/shard_map/ppermute | solution.py:172
  34.1 2.6 %collective-permute-done.4 = f32[16,32,512]{2,1,0:T(8,128)S(1)} collective-permute-done((f32[16,32,512]{2,1,0:T(8,128)S(1)}, f32[16,32,512]{2,1,0:T(8,128)S(1)}, u32[]{:S(2)}, u32[]{:S(2)}) %collective-permute-start.4) | collective-permute-done | bytes 1048608 | tf_op jit(solution)/shard_map/ppermute | solution.py:172
  37.0 1.7 %collective-permute-done.9 = f32[16,32,512]{2,1,0:T(8,128)S(1)} collective-permute-done((f32[16,32,512]{2,1,0:T(8,128)S(1)}, f32[16,32,512]{2,1,0:T(8,128)S(1)}, u32[]{:S(2)}, u32[]{:S(2)}) %collective-permute-start.9) | collective-permute-done | bytes 1048608 | tf_op jit(solution)/shard_map/ppermute | solution.py:172
  39.3 2.1 %collective-permute-start.14 = (f32[8,32,512]{2,1,0:T(8,128)S(1)}, f32[8,32,512]{2,1,0:T(8,128)S(1)}, u32[]{:S(2)}, u32[]{:S(2)}) collective-permute-start(f32[8,32,512]{2,1,0:T(8,128)S(1)} %get-tuple-element.38), channel_id=1, source_target_pairs={{0,28},{1,29},{2,30},{3,31},{4,8},{5,9},{6,10},{7,11},{8,4},{9,5},... | collective-permute-start | bytes 1572872 | tf_op jit(solution)/shard_map/ppermute | solution.py:172
  41.4 8.6 %collective-permute-done.1 = f32[8,32,512]{2,1,0:T(8,128)S(1)} collective-permute-done((f32[8,32,512]{2,1,0:T(8,128)S(1)}, f32[8,32,512]{2,1,0:T(8,128)S(1)}, u32[]{:S(2)}, u32[]{:S(2)}) %collective-permute-start.1) | collective-permute-done | bytes 524320 | tf_op jit(solution)/shard_map/ppermute | solution.py:172
  51.1 2.1 %collective-permute-start.6 = (f32[4,32,512]{2,1,0:T(8,128)S(1)}, f32[4,32,512]{2,1,0:T(8,128)S(1)}, u32[]{:S(2)}, u32[]{:S(2)}) collective-permute-start(f32[4,32,512]{2,1,0:T(8,128)S(1)} %get-tuple-element.50), channel_id=1, source_target_pairs={{0,3},{1,2},{2,1},{3,0},{4,7},{5,6},{6,5},{7,4},{8,11},{9,10},{10,... | collective-permute-start | bytes 786440 | tf_op jit(solution)/shard_map/ppermute | solution.py:172
  53.9 4.1 %collective-permute-done.2 = f32[4,32,512]{2,1,0:T(8,128)S(1)} collective-permute-done((f32[4,32,512]{2,1,0:T(8,128)S(1)}, f32[4,32,512]{2,1,0:T(8,128)S(1)}, u32[]{:S(2)}, u32[]{:S(2)}) %collective-permute-start.2) | collective-permute-done | bytes 262176 | tf_op jit(solution)/shard_map/ppermute | solution.py:172
  58.2 1.7 %collective-permute-start.7 = (f32[2,32,512]{2,1,0:T(8,128)S(1)}, f32[2,32,512]{2,1,0:T(8,128)S(1)}, u32[]{:S(2)}, u32[]{:S(2)}) collective-permute-start(f32[2,32,512]{2,1,0:T(8,128)S(1)} %get-tuple-element.58), channel_id=1, source_target_pairs={{0,1},{1,0},{2,3},{3,2},{4,5},{5,4},{6,7},{7,6},{8,9},{9,8},{10,11... | collective-permute-start | bytes 393224 | tf_op jit(solution)/shard_map/ppermute | solution.py:172
  61.1 1.5 %collective-permute-start.16 = (f32[2,32,512]{2,1,0:T(8,128)S(1)}, f32[2,32,512]{2,1,0:T(8,128)S(1)}, u32[]{:S(2)}, u32[]{:S(2)}) collective-permute-start(f32[2,32,512]{2,1,0:T(8,128)S(1)} %get-tuple-element.54), channel_id=1, source_target_pairs={{0,3},{1,2},{2,1},{3,0},{4,7},{5,6},{6,5},{7,4},{8,11},{9,10},{10,... | collective-permute-start | bytes 393224 | tf_op jit(solution)/shard_map/ppermute | solution.py:172
  64.0 3.5 %collective-permute-start.8 = (f32[1,32,1024]{2,1,0:T(8,128)S(1)}, f32[1,32,1024]{2,1,0:T(8,128)S(1)}, u32[]{:S(2)}, u32[]{:S(2)}) collective-permute-start(f32[1,32,1024]{2,1,0:T(8,128)S(1)} %pad_maximum_fusion), channel_id=1, source_target_pairs={{0,20},{1,21},{2,22},{3,23},{4,16},{5,17},{6,18},{7,19},{8,28},{9,... | collective-permute-start | bytes 393224 | tf_op jit(solution)/shard_map/ppermute | solution.py:172
  69.1 4.5 %collective-permute-done.8 = f32[1,32,1024]{2,1,0:T(8,128)S(1)} collective-permute-done((f32[1,32,1024]{2,1,0:T(8,128)S(1)}, f32[1,32,1024]{2,1,0:T(8,128)S(1)}, u32[]{:S(2)}, u32[]{:S(2)}) %collective-permute-start.8) | collective-permute-done | bytes 131104 | tf_op jit(solution)/shard_map/ppermute | solution.py:172
  73.6 2.4 %collective-permute-done.17 = f32[1,32,1024]{2,1,0:T(8,128)S(1)} collective-permute-done((f32[1,32,1024]{2,1,0:T(8,128)S(1)}, f32[1,32,1024]{2,1,0:T(8,128)S(1)}, u32[]{:S(2)}, u32[]{:S(2)}) %collective-permute-start.17) | collective-permute-done | bytes 131104 | tf_op jit(solution)/shard_map/ppermute | solution.py:172
  77.1 7.3 %all-to-all-start = ((f32[32,8,128]{2,1,0:T(8,128)}), f32[32,8,128]{2,1,0:T(8,128)S(1)}, u32[]{:S(2)}, u32[]{:S(2)}) async-start(f32[32,8,128]{2,1,0:T(8,128)} %get-tuple-element.31), calls=%async_computation | async-start | bytes 262144 | tf_op jit(solution)/shard_map/all_to_all | solution.py:323
  84.4 2.0 %leaf.1 = (f32[2,32,1024]{2,1,0:T(8,128)}, f32[2,32,32]{2,1,0:T(8,128)S(1)}) custom-call(f32[2,32,32]{2,1,0:T(8,128)S(1)} %get-tuple-element.28.gram_ref, f32[2,32,1024]{2,1,0:T(8,128)S(1)} %get-tuple-element.29.sample_ref), custom_call_target="tpu_custom_call" | custom-call | tf_op jit(solution)/shard_map/leaf/pallas_call | solution.py:324
  86.4 7.3 %all-to-all-done.every_ref = f32[32,8,128]{2,1,0:T(8,128)S(1)} async-done(((f32[32,8,128]{2,1,0:T(8,128)}), f32[32,8,128]{2,1,0:T(8,128)S(1)}, u32[]{:S(2)}, u32[]{:S(2)}) %all-to-all-start) | async-done | bytes 131104 | tf_op jit(solution)/shard_map/all_to_all | solution.py:323
  93.8 3.9 %collective-permute-start.18 = (f32[8,128]{1,0:T(8,128)S(1)}, f32[8,128]{1,0:T(8,128)S(1)}, u32[]{:S(2)}, u32[]{:S(2)}) collective-permute-start(f32[8,128]{1,0:T(8,128)S(1)} %group.1.own_ref), channel_id=1, source_target_pairs={{0,32},{32,0},{64,96},{96,64},{128,160},{160,128},{192,224},{224,1... | collective-permute-start | bytes 12296 | tf_op jit(solution)/shard_map/ppermute | solution.py:181
  100.9 2.8 %collective-permute-start.20 = (f32[8,128]{1,0:T(8,128)S(1)}, f32[8,128]{1,0:T(8,128)S(1)}, u32[]{:S(2)}, u32[]{:S(2)}) collective-permute-start(f32[8,128]{1,0:T(8,128)S(1)} %add.135.near_ref), channel_id=1, source_target_pairs={{0,192},{32,224},{64,128},{96,160},{128,64},{160,96},{192,0},{224,... | collective-permute-start | bytes 12296 | tf_op jit(solution)/shard_map/ppermute | solution.py:181
  103.7 1.6 %transfer_leaf.1 = (f32[2,32,32]{2,1,0:T(8,128)}, f32[32,32]{1,0:T(8,128)S(1)}) custom-call(f32[8,128]{1,0:T(8,128)S(1)} %group.1.own_ref, f32[2,32,32]{2,1,0:T(8,128)S(1)} %get-tuple-element.34.upper_ref), custom_call_target="tpu_custom_call" | custom-call | tf_op jit(solution)/shard_map/transfer_leaf/pallas_call | solution.py:346
  105.3 1.6 %transfer_group.1 = f32[1,32,32]{2,1,0:T(8,128)} custom-call(f32[8,128]{1,0:T(8,128)S(1)} %add.135.near_ref, f32[8,128]{1,0:T(8,128)S(1)} %collective-permute-done.20.far_ref, f32[32,32]{1,0:T(8,128)S(1)} %get-tuple-element.36.upper_ref), custom_call_target="tpu_custom_call" | custom-call | tf_op jit(solution)/shard_map/transfer_group/pallas_call | solution.py:355
  (50 shorter events, 11.4 us)
Async XLA Ops:
  6.5 23.6 %collective-permute-start = (f32[16,32,512]{2,1,0:T(8,128)S(1)}, f32[16,32,512]{2,1,0:T(8,128)S(1)}, u32[]{:S(2)}, u32[]{:S(2)}) collective-permute-start(f32[16,32,512]{2,1,0:T(8,128)S(1)} %get-tuple-element.21), channel_id=1, source_target_pairs={{0,1},{1,0},{2,3},{3,2},{4,5},{5,4},{6,7},{7,6},{8,9},{9,8},{10,11... | collective-permute-start | bytes 3145736 | tf_op jit(solution)/shard_map/ppermute | solution.py:172
  8.6 28.2 %collective-permute-start.4 = (f32[16,32,512]{2,1,0:T(8,128)S(1)}, f32[16,32,512]{2,1,0:T(8,128)S(1)}, u32[]{:S(2)}, u32[]{:S(2)}) collective-permute-start(f32[16,32,512]{2,1,0:T(8,128)S(1)} %get-tuple-element.23), channel_id=1, source_target_pairs={{0,28},{1,29},{2,30},{3,31},{4,8},{5,9},{6,10},{7,11},{8,4},{9,5},... | collective-permute-start | bytes 3145736 | tf_op jit(solution)/shard_map/ppermute | solution.py:172
  14.2 24.6 %collective-permute-start.9 = (f32[16,32,512]{2,1,0:T(8,128)S(1)}, f32[16,32,512]{2,1,0:T(8,128)S(1)}, u32[]{:S(2)}, u32[]{:S(2)}) collective-permute-start(f32[16,32,512]{2,1,0:T(8,128)S(1)} %get-tuple-element.25), channel_id=1, source_target_pairs={{0,3},{1,2},{2,1},{3,0},{4,7},{5,6},{6,5},{7,4},{8,11},{9,10},{10,... | collective-permute-start | bytes 3145736 | tf_op jit(solution)/shard_map/ppermute | solution.py:172
  15.9 23.2 %collective-permute-start.13 = (f32[16,32,512]{2,1,0:T(8,128)S(1)}, f32[16,32,512]{2,1,0:T(8,128)S(1)}, u32[]{:S(2)}, u32[]{:S(2)}) collective-permute-start(f32[16,32,512]{2,1,0:T(8,128)S(1)} %get-tuple-element.27), channel_id=1, source_target_pairs={{0,4},{1,5},{2,6},{3,7},{4,0},{5,1},{6,2},{7,3},{8,12},{9,13},{10,... | collective-permute-start | bytes 3145736 | tf_op jit(solution)/shard_map/ppermute | solution.py:172
  30.3 19.7 %collective-permute-start.1 = (f32[8,32,512]{2,1,0:T(8,128)S(1)}, f32[8,32,512]{2,1,0:T(8,128)S(1)}, u32[]{:S(2)}, u32[]{:S(2)}) collective-permute-start(f32[8,32,512]{2,1,0:T(8,128)S(1)} %get-tuple-element.44), channel_id=1, source_target_pairs={{0,3},{1,2},{2,1},{3,0},{4,7},{5,6},{6,5},{7,4},{8,11},{9,10},{10,... | collective-permute-start | bytes 1572872 | tf_op jit(solution)/shard_map/ppermute | solution.py:172
  36.9 14.1 %collective-permute-start.5 = (f32[8,32,512]{2,1,0:T(8,128)S(1)}, f32[8,32,512]{2,1,0:T(8,128)S(1)}, u32[]{:S(2)}, u32[]{:S(2)}) collective-permute-start(f32[8,32,512]{2,1,0:T(8,128)S(1)} %get-tuple-element.42), channel_id=1, source_target_pairs={{0,4},{1,5},{2,6},{3,7},{4,0},{5,1},{6,2},{7,3},{8,12},{9,13},{10,... | collective-permute-start | bytes 1572872 | tf_op jit(solution)/shard_map/ppermute | solution.py:172
  39.0 14.3 %collective-permute-start.10 = (f32[8,32,512]{2,1,0:T(8,128)S(1)}, f32[8,32,512]{2,1,0:T(8,128)S(1)}, u32[]{:S(2)}, u32[]{:S(2)}) collective-permute-start(f32[8,32,512]{2,1,0:T(8,128)S(1)} %get-tuple-element.40), channel_id=1, source_target_pairs={{0,1},{1,0},{2,3},{3,2},{4,5},{5,4},{6,7},{7,6},{8,9},{9,8},{10,11... | collective-permute-start | bytes 1572872 | tf_op jit(solution)/shard_map/ppermute | solution.py:172
  39.3 14.3 %collective-permute-start.14 = (f32[8,32,512]{2,1,0:T(8,128)S(1)}, f32[8,32,512]{2,1,0:T(8,128)S(1)}, u32[]{:S(2)}, u32[]{:S(2)}) collective-permute-start(f32[8,32,512]{2,1,0:T(8,128)S(1)} %get-tuple-element.38), channel_id=1, source_target_pairs={{0,28},{1,29},{2,30},{3,31},{4,8},{5,9},{6,10},{7,11},{8,4},{9,5},... | collective-permute-start | bytes 1572872 | tf_op jit(solution)/shard_map/ppermute | solution.py:172
  50.1 7.9 %collective-permute-start.2 = (f32[4,32,512]{2,1,0:T(8,128)S(1)}, f32[4,32,512]{2,1,0:T(8,128)S(1)}, u32[]{:S(2)}, u32[]{:S(2)}) collective-permute-start(f32[4,32,512]{2,1,0:T(8,128)S(1)} %get-tuple-element.52), channel_id=1, source_target_pairs={{0,28},{1,29},{2,30},{3,31},{4,8},{5,9},{6,10},{7,11},{8,4},{9,5},... | collective-permute-start | bytes 786440 | tf_op jit(solution)/shard_map/ppermute | solution.py:172
  51.1 7.0 %collective-permute-start.6 = (f32[4,32,512]{2,1,0:T(8,128)S(1)}, f32[4,32,512]{2,1,0:T(8,128)S(1)}, u32[]{:S(2)}, u32[]{:S(2)}) collective-permute-start(f32[4,32,512]{2,1,0:T(8,128)S(1)} %get-tuple-element.50), channel_id=1, source_target_pairs={{0,3},{1,2},{2,1},{3,0},{4,7},{5,6},{6,5},{7,4},{8,11},{9,10},{10,... | collective-permute-start | bytes 786440 | tf_op jit(solution)/shard_map/ppermute | solution.py:172
  53.4 6.5 %collective-permute-start.11 = (f32[4,32,512]{2,1,0:T(8,128)S(1)}, f32[4,32,512]{2,1,0:T(8,128)S(1)}, u32[]{:S(2)}, u32[]{:S(2)}) collective-permute-start(f32[4,32,512]{2,1,0:T(8,128)S(1)} %get-tuple-element.48), channel_id=1, source_target_pairs={{0,4},{1,5},{2,6},{3,7},{4,0},{5,1},{6,2},{7,3},{8,12},{9,13},{10,... | collective-permute-start | bytes 786440 | tf_op jit(solution)/shard_map/ppermute | solution.py:172
  53.6 22.4 %copy-start = (f32[2,32,1024]{2,1,0:T(8,128)S(1)}, f32[2,32,1024]{2,1,0:T(8,128)}, u32[]{:S(2)}) copy-start(f32[2,32,1024]{2,1,0:T(8,128)} %refs_7_.1) | copy-start | bytes 786436
  53.7 22.4 %copy-start.1 = (f32[2,1024]{1,0:T(2,128)S(1)}, f32[2,1024]{1,0:T(2,128)}, u32[]{:S(2)}) copy-start(f32[2,1024]{1,0:T(2,128)} %refs_6_.1) | copy-start | bytes 24580
  53.8 7.3 %collective-permute-start.15 = (f32[4,32,512]{2,1,0:T(8,128)S(1)}, f32[4,32,512]{2,1,0:T(8,128)S(1)}, u32[]{:S(2)}, u32[]{:S(2)}) collective-permute-start(f32[4,32,512]{2,1,0:T(8,128)S(1)} %get-tuple-element.46), channel_id=1, source_target_pairs={{0,1},{1,0},{2,3},{3,2},{4,5},{5,4},{6,7},{7,6},{8,9},{9,8},{10,11... | collective-permute-start | bytes 786440 | tf_op jit(solution)/shard_map/ppermute | solution.py:172
  58.0 5.6 %collective-permute-start.3 = (f32[2,32,512]{2,1,0:T(8,128)S(1)}, f32[2,32,512]{2,1,0:T(8,128)S(1)}, u32[]{:S(2)}, u32[]{:S(2)}) collective-permute-start(f32[2,32,512]{2,1,0:T(8,128)S(1)} %get-tuple-element.60), channel_id=1, source_target_pairs={{0,4},{1,5},{2,6},{3,7},{4,0},{5,1},{6,2},{7,3},{8,12},{9,13},{10,... | collective-permute-start | bytes 393224 | tf_op jit(solution)/shard_map/ppermute | solution.py:172
  58.2 5.8 %collective-permute-start.7 = (f32[2,32,512]{2,1,0:T(8,128)S(1)}, f32[2,32,512]{2,1,0:T(8,128)S(1)}, u32[]{:S(2)}, u32[]{:S(2)}) collective-permute-start(f32[2,32,512]{2,1,0:T(8,128)S(1)} %get-tuple-element.58), channel_id=1, source_target_pairs={{0,1},{1,0},{2,3},{3,2},{4,5},{5,4},{6,7},{7,6},{8,9},{9,8},{10,11... | collective-permute-start | bytes 393224 | tf_op jit(solution)/shard_map/ppermute | solution.py:172
  59.9 7.6 %collective-permute-start.12 = (f32[2,32,512]{2,1,0:T(8,128)S(1)}, f32[2,32,512]{2,1,0:T(8,128)S(1)}, u32[]{:S(2)}, u32[]{:S(2)}) collective-permute-start(f32[2,32,512]{2,1,0:T(8,128)S(1)} %get-tuple-element.56), channel_id=1, source_target_pairs={{0,28},{1,29},{2,30},{3,31},{4,8},{5,9},{6,10},{7,11},{8,4},{9,5},... | collective-permute-start | bytes 393224 | tf_op jit(solution)/shard_map/ppermute | solution.py:172
  61.1 6.4 %collective-permute-start.16 = (f32[2,32,512]{2,1,0:T(8,128)S(1)}, f32[2,32,512]{2,1,0:T(8,128)S(1)}, u32[]{:S(2)}, u32[]{:S(2)}) collective-permute-start(f32[2,32,512]{2,1,0:T(8,128)S(1)} %get-tuple-element.54), channel_id=1, source_target_pairs={{0,3},{1,2},{2,1},{3,0},{4,7},{5,6},{6,5},{7,4},{8,11},{9,10},{10,... | collective-permute-start | bytes 393224 | tf_op jit(solution)/shard_map/ppermute | solution.py:172
  64.0 9.6 %collective-permute-start.8 = (f32[1,32,1024]{2,1,0:T(8,128)S(1)}, f32[1,32,1024]{2,1,0:T(8,128)S(1)}, u32[]{:S(2)}, u32[]{:S(2)}) collective-permute-start(f32[1,32,1024]{2,1,0:T(8,128)S(1)} %pad_maximum_fusion), channel_id=1, source_target_pairs={{0,20},{1,21},{2,22},{3,23},{4,16},{5,17},{6,18},{7,19},{8,28},{9,... | collective-permute-start | bytes 393224 | tf_op jit(solution)/shard_map/ppermute | solution.py:172
  67.6 8.4 %collective-permute-start.17 = (f32[1,32,1024]{2,1,0:T(8,128)S(1)}, f32[1,32,1024]{2,1,0:T(8,128)S(1)}, u32[]{:S(2)}, u32[]{:S(2)}) collective-permute-start(f32[1,32,1024]{2,1,0:T(8,128)S(1)} %pad_maximum_fusion.1), channel_id=1, source_target_pairs={{0,12},{1,13},{2,14},{3,15},{4,24},{5,25},{6,26},{7,27},{8,20},{9,... | collective-permute-start | bytes 393224 | tf_op jit(solution)/shard_map/ppermute | solution.py:172
  77.1 16.6 %all-to-all-start = ((f32[32,8,128]{2,1,0:T(8,128)}), f32[32,8,128]{2,1,0:T(8,128)S(1)}, u32[]{:S(2)}, u32[]{:S(2)}) async-start(f32[32,8,128]{2,1,0:T(8,128)} %get-tuple-element.31), calls=%async_computation | async-start | bytes 262144 | tf_op jit(solution)/shard_map/all_to_all | solution.py:323
  93.8 4.7 %collective-permute-start.18 = (f32[8,128]{1,0:T(8,128)S(1)}, f32[8,128]{1,0:T(8,128)S(1)}, u32[]{:S(2)}, u32[]{:S(2)}) collective-permute-start(f32[8,128]{1,0:T(8,128)S(1)} %group.1.own_ref), channel_id=1, source_target_pairs={{0,32},{32,0},{64,96},{96,64},{128,160},{160,128},{192,224},{224,1... | collective-permute-start | bytes 12296 | tf_op jit(solution)/shard_map/ppermute | solution.py:181
  98.5 2.5 %collective-permute-start.19 = (f32[8,128]{1,0:T(8,128)S(1)}, f32[8,128]{1,0:T(8,128)S(1)}, u32[]{:S(2)}, u32[]{:S(2)}) collective-permute-start(f32[8,128]{1,0:T(8,128)S(1)} %add.134), channel_id=1, source_target_pairs={{0,64},{32,96},{64,0},{96,32},{128,192},{160,224},{192,128},{224,1... | collective-permute-start | bytes 12296 | tf_op jit(solution)/shard_map/ppermute | solution.py:181
  100.9 4.4 %collective-permute-start.20 = (f32[8,128]{1,0:T(8,128)S(1)}, f32[8,128]{1,0:T(8,128)S(1)}, u32[]{:S(2)}, u32[]{:S(2)}) collective-permute-start(f32[8,128]{1,0:T(8,128)S(1)} %add.135.near_ref), channel_id=1, source_target_pairs={{0,192},{32,224},{64,128},{96,160},{128,64},{160,96},{192,0},{224,... | collective-permute-start | bytes 12296 | tf_op jit(solution)/shard_map/ppermute | solution.py:181
